TPU v7x, 256 devices: a whole 4x4x8 slice. The times are simulated.
256 devices in a mesh: band: 32 (over z, y_lo, core), hid: 8 (over x, y_hi).
Axes of the slice: x: 4, y: 4 (y_hi: 2, y_lo: 2; y = y_hi * 2 + y_lo), z: 8, core: 2. Of those that a mesh axis runs over, the one named last changes fastest.
Arguments:
- pair: float32 [768, 768, 128], P('band', 'hid'), may hold values from -40 to 40
- residue_mask: int32 [768], replicated, may hold values 0 or 1
- hotspot: int32 [768], replicated, may hold values 0 or 1
- interface: int32 [768, 768], P('band', 'hid'), may hold values 0 or 1
- proj_weight: float32 [2, 128, 512], replicated, may hold values from -0.5 to 0.5
- gate_weight: float32 [2, 128, 128], replicated, may hold values from -0.5 to 0.5
- out_weight: float32 [2, 128, 128], replicated, may hold values from -0.5 to 0.5
Outputs:
- pair_out: float32 [768, 768, 128], P('band', 'hid')
All inputs are finite; a program needn't handle non-finite values. No bound on the sum of `interface` on one device may be relied on, other than what follows from the above.
Results may differ from a plain program's by a relative error of at most 0.0021.
Values may be sent and summed in bfloat16 or wider, within the bound.
No kernel may reach another device: no remote copies, remote signals or barrier semaphores. Data moves between devices by JAX's collectives and lax.ppermute only.
A program may use at most 128 MiB of HBM per device.

v0:
```python
import jax
import jax.numpy as jnp
from jax import lax
from jax.sharding import PartitionSpec as P

EPS = 1e-05
HIGH = lax.Precision.HIGHEST


def normalize(values):
    average = jnp.mean(values, axis=-1, keepdims=True)
    centred = values - average
    variance = jnp.mean(centred * centred, axis=-1, keepdims=True)
    return centred * lax.rsqrt(variance + EPS)


def project(state, edge, weight):
    normed = normalize(state)
    proj = jnp.einsum("rmc,cf->frm", normed, weight, precision=HIGH)
    width = weight.shape[1] // 4
    left = (edge * jax.nn.sigmoid(proj[width : 2 * width]) * proj[:width]).astype(jnp.bfloat16)
    right = (edge * jax.nn.sigmoid(proj[3 * width :]) * proj[2 * width : 3 * width]).astype(
        jnp.bfloat16
    )
    return (normed, left, right)


def outgoing(left, right):
    return lax.dot_general(
        left,
        lax.all_gather(right, "band", axis=1, tiled=True),
        (((2,), (2,)), ((0,), (0,))),
        preferred_element_type=jnp.float32,
    )


def incoming(left, right):
    columns = lax.all_to_all(left, "band", split_axis=2, concat_axis=1, tiled=True)
    return lax.dot_general(
        columns,
        lax.all_gather(right, "band", axis=1, tiled=True),
        (((1,), (1,)), ((0,), (0,))),
        preferred_element_type=jnp.float32,
    )


def finish(tri, normed, gate_w, out_w):
    gating = jax.nn.sigmoid(jnp.einsum("rmd,dc->rmc", normed, gate_w, precision=HIGH))
    gathered = lax.all_to_all(tri, "hid", split_axis=2, concat_axis=0, tiled=True)
    average = jnp.mean(gathered, axis=0)
    variance = jnp.mean(gathered * gathered, axis=0) - average * average
    scaled = (gathered - average) * lax.rsqrt(variance + EPS)
    projected = jnp.einsum("hrm,hc->rmc", scaled, out_w, precision=HIGH)
    return gating * projected


def on_device(pair, residue_mask, hotspot, interface, proj_weight, gate_weight, out_weight):
    rows = pair.shape[0]
    cols = pair.shape[1]
    row_start = lax.axis_index("band") * rows
    col_start = lax.axis_index("hid") * cols
    row_mask = lax.dynamic_slice_in_dim(residue_mask, row_start, rows, 0)
    col_mask = lax.dynamic_slice_in_dim(residue_mask, col_start, cols, 0)
    row_hot = lax.dynamic_slice_in_dim(hotspot, row_start, rows, 0)
    col_hot = lax.dynamic_slice_in_dim(hotspot, col_start, cols, 0)
    flags = jnp.maximum(interface, jnp.maximum(row_hot[:, None], col_hot[None, :]))
    edge = (row_mask[:, None] * col_mask[None, :] * flags).astype(jnp.float32)
    state = pair
    for layer in range(2):
        normed, left, right = project(state, edge, proj_weight[layer])
        left, right = (
            lax.all_to_all(left, "hid", split_axis=0, concat_axis=2, tiled=True),
            lax.all_to_all(right, "hid", split_axis=0, concat_axis=2, tiled=True),
        )
        if layer == 0:
            tri = outgoing(left, right)
        else:
            tri = incoming(left, right)
        state = state + finish(tri, normed, gate_weight[layer], out_weight[layer])
    return state


def solution(mesh):
    return jax.shard_map(
        on_device,
        mesh=mesh,
        in_specs=(P("band", "hid", None), P(), P(), P("band", "hid"), P(), P(), P()),
        out_specs=P("band", "hid", None),
        check_vma=False,
    )
```

profile of v0, /device:TPU:6, one launch (start us, length us, event | category | flops | bytes accessed | tf_op | source)
XLA Modules:
  0.0 437.6 jit_solution(17324085471123526692)
XLA Ops:
  17.6 19.2 %all_to_all.120 = bf16[128,24,96]{2,1,0:T(8,128)(2,1)S(1)} all-to-all(bf16[128,24,96]{2,1,0:T(8,128)(2,1)S(1)} %copy.28), channel_id=1, replica_groups=mesh['band'=32,'hid'=8] {'hid'}, dimensions={0} | all-to-all | bytes 1179648 | tf_op jit(solution)/shard_map/all_to_all | solution.py:73
  39.2 16.0 %all_to_all.121 = bf16[128,24,96]{2,1,0:T(8,128)(2,1)S(1)} all-to-all(bf16[128,24,96]{2,1,0:T(8,128)(2,1)S(1)} %copy.26), channel_id=1, replica_groups=mesh['band'=32,'hid'=8] {'hid'}, dimensions={0} | all-to-all | bytes 1179648 | tf_op jit(solution)/shard_map/all_to_all | solution.py:72
  56.4 93.5 %all-gather.3.cloned.1.call-done = bf16[16,768,768]{2,1,0:T(8,128)(2,1)} async-done(((bf16[16,24,768]{2,1,0:T(8,128)(2,1)}), bf16[16,768,768]{2,1,0:T(8,128)(2,1)}) %all-gather.3.cloned.1.call-update) | async-done | bytes 18874384 | tf_op jit(solution)/shard_map/all_gather | solution.py:31
  149.9 8.9 %fusion.75 = f32[16,24,768]{2,1,0:T(8,128)S(1)} fusion(bf16[16,24,768]{2,1,0:T(8,128)(2,1)S(1)} %all_to_all.90, bf16[16,768,768]{2,1,0:T(8,128)(2,1)} %all-gather.3.cloned.1.call-done), kind=kOutput, calls=%fused_computation.96 | convolution fusion | flops 452984832 | bytes 20643840 | tf_op jit(solution)/shard_map/dot_general | solution.py:29
  158.8 5.0 %copy.30 = f32[16,24,768]{1,0,2:T(8,128)} copy(f32[16,24,768]{2,1,0:T(8,128)S(1)} %fusion.75) | data formatting | bytes 2359296 | tf_op jit(solution)/shard_map/dot_general | solution.py:29
  163.8 7.4 %reshape.61 = f32[8,1,36864]{2,1,0:T(1,128)} reshape(f32[768,16,24]{2,1,0:T(8,128)} %bitcast.87) | data formatting | bytes 2359296
  171.2 7.4 %all-to-all-start.2 = ((f32[8,1,36864]{2,1,0:T(1,128)}), f32[8,1,36864]{2,1,0:T(1,128)S(1)}, u32[]{:S(2)}, u32[]{:S(2)}) async-start(f32[8,1,36864]{2,1,0:T(1,128)} %reshape.61), calls=%async_computation.2 | async-start | bytes 2359296 | tf_op jit(solution)/shard_map/all_to_all | solution.py:49
  181.1 13.8 %all-to-all-done.2 = f32[8,1,36864]{2,1,0:T(1,128)S(1)} async-done(((f32[8,1,36864]{2,1,0:T(1,128)}), f32[8,1,36864]{2,1,0:T(1,128)S(1)}, u32[]{:S(2)}, u32[]{:S(2)}) %all-to-all-start.2) | async-done | bytes 1179680 | tf_op jit(solution)/shard_map/all_to_all | solution.py:49
  198.9 7.2 %reshape.62 = f32[768,16,24]{2,1,0:T(8,128)} reshape(f32[8,36864]{1,0:T(8,128)S(1)} %reduce.4) | data formatting | bytes 2359296
  206.0 5.8 %copy.31 = f32[16,24,8,96]{3,1,0,2:T(8,128)} copy(f32[16,24,8,96]{1,0,3,2:T(8,128)} %bitcast.89) | data formatting | bytes 2359296 | tf_op jit(solution)/shard_map/all_to_all | solution.py:49
  224.2 17.1 %all_to_all.122 = bf16[128,24,96]{2,1,0:T(8,128)(2,1)S(1)} all-to-all(bf16[128,24,96]{2,1,0:T(8,128)(2,1)S(1)} %copy.38), channel_id=1, replica_groups=mesh['band'=32,'hid'=8] {'hid'}, dimensions={0} | all-to-all | bytes 1179648 | tf_op jit(solution)/shard_map/all_to_all | solution.py:73
  243.8 16.0 %all_to_all.123 = bf16[128,24,96]{2,1,0:T(8,128)(2,1)S(1)} all-to-all(bf16[128,24,96]{2,1,0:T(8,128)(2,1)S(1)} %copy.33), channel_id=1, replica_groups=mesh['band'=32,'hid'=8] {'hid'}, dimensions={0} | all-to-all | bytes 1179648 | tf_op jit(solution)/shard_map/all_to_all | solution.py:72
  263.6 5.8 %reshape.63 = bf16[32,2,4608]{2,1,0:T(2,128)(2,1)S(1)} reshape(bf16[768,16,24]{2,1,0:T(8,128)(2,1)} %bitcast.92) | data formatting | bytes 1179648
  269.4 34.5 %all_to_all.124 = bf16[32,2,4608]{2,1,0:T(2,128)(2,1)S(1)} all-to-all(bf16[32,2,4608]{2,1,0:T(2,128)(2,1)S(1)} %reshape.63), channel_id=1, replica_groups=mesh['band'=32,'hid'=8] {'band'}, dimensions={0} | all-to-all | bytes 1179648 | tf_op jit(solution)/shard_map/all_to_all | solution.py:38
  303.9 5.7 %reshape.64 = bf16[768,16,24]{2,1,0:T(8,128)(2,1)} reshape(bf16[32,2,4608]{2,1,0:T(2,128)(2,1)S(1)} %all_to_all.124) | data formatting | bytes 1179648
  309.5 5.6 %copy.37 = bf16[16,32,24,24]{2,1,3,0:T(8,128)(2,1)} copy(bf16[16,32,24,24]{2,0,3,1:T(8,128)(2,1)} %bitcast.91) | data formatting | bytes 1179648 | tf_op jit(solution)/shard_map/all_to_all | solution.py:38
  315.1 5.3 %all_to_all.105 = bf16[16,768,24]{1,2,0:T(8,128)(2,1)S(1)} reshape(bf16[16,32,24,24]{2,1,3,0:T(8,128)(2,1)} %copy.37) | data formatting | bytes 1179648 | tf_op jit(solution)/shard_map/all_to_all | solution.py:38
  320.4 45.3 %all-gather.5.cloned.1.call-done = bf16[16,768,768]{2,1,0:T(8,128)(2,1)} async-done(((bf16[16,24,768]{2,1,0:T(8,128)(2,1)}), bf16[16,768,768]{2,1,0:T(8,128)(2,1)}) %all-gather.5.cloned.1.call-update) | async-done | bytes 18874384 | tf_op jit(solution)/shard_map/all_gather | solution.py:41
  365.7 7.7 %fusion.76 = f32[16,24,768]{2,1,0:T(8,128)S(1)} fusion(bf16[16,768,24]{1,2,0:T(8,128)(2,1)S(1)} %all_to_all.105, bf16[16,768,768]{2,1,0:T(8,128)(2,1)} %all-gather.5.cloned.1.call-done), kind=kOutput, calls=%fused_computation.97 | convolution fusion | flops 452984832 | bytes 20643840 | tf_op jit(solution)/shard_map/dot_general | solution.py:39
  378.4 7.4 %reshape.65 = f32[8,1,36864]{2,1,0:T(1,128)} reshape(f32[768,16,24]{2,1,0:T(8,128)} %bitcast.88) | data formatting | bytes 2359296
  385.8 7.6 %all-to-all-start.6 = ((f32[8,1,36864]{2,1,0:T(1,128)}), f32[8,1,36864]{2,1,0:T(1,128)S(1)}, u32[]{:S(2)}, u32[]{:S(2)}) async-start(f32[8,1,36864]{2,1,0:T(1,128)} %reshape.65), calls=%async_computation.6 | async-start | bytes 2359296 | tf_op jit(solution)/shard_map/all_to_all | solution.py:49
  395.9 13.8 %all-to-all-done.6 = f32[8,1,36864]{2,1,0:T(1,128)S(1)} async-done(((f32[8,1,36864]{2,1,0:T(1,128)}), f32[8,1,36864]{2,1,0:T(1,128)S(1)}, u32[]{:S(2)}, u32[]{:S(2)}) %all-to-all-start.6) | async-done | bytes 1179680 | tf_op jit(solution)/shard_map/all_to_all | solution.py:49
  413.1 7.2 %reshape.66 = f32[768,16,24]{2,1,0:T(8,128)} reshape(f32[8,36864]{1,0:T(8,128)S(1)} %reduce.5) | data formatting | bytes 2359296
  420.3 5.0 %copy.41 = f32[16,24,8,96]{3,1,0,2:T(8,128)S(1)} copy(f32[16,24,8,96]{1,0,3,2:T(8,128)} %bitcast.90) | data formatting | bytes 2359296 | tf_op jit(solution)/shard_map/all_to_all | solution.py:49
  (79 shorter events, 55.6 us)
Async XLA Ops:
  6.5 5.0 %copy-start = (f32[24,96,128]{2,1,0:T(8,128)S(1)}, f32[24,96,128]{2,1,0:T(8,128)}, u32[]{:S(2)}) copy-start(f32[24,96,128]{2,1,0:T(8,128)} %param.7) | copy-start | bytes 3538948
  6.5 143.4 %all-gather.3.cloned.1.call-start = ((), (), s32[]{:S(2)}) async-start(), calls=%async_computation.7 | async-start | bytes 19464192 | tf_op jit(solution)/shard_map/all_gather | solution.py:31
  9.7 2.7 copy-start.4
  12.3 4.0 copy-start.12
  12.3 4.0 copy-start.14
  16.4 0.8 copy-start.8
  171.2 7.4 %copy-start.13 = (f32[24,96]{1,0:T(8,128)S(1)}, f32[24,96]{1,0:T(8,128)}, u32[]{:S(2)}) copy-start(f32[24,96]{1,0:T(8,128)} %copy-done.12) | copy-start | bytes 27652
  171.2 7.4 %copy-start.15 = (f32[2,128,128]{2,1,0:T(8,128)S(1)}, f32[2,128,128]{2,1,0:T(8,128)}, u32[]{:S(2)}) copy-start(f32[2,128,128]{2,1,0:T(8,128)} %param.12) | copy-start | bytes 393220
  171.2 23.7 %all-to-all-start.2 = ((f32[8,1,36864]{2,1,0:T(1,128)}), f32[8,1,36864]{2,1,0:T(1,128)S(1)}, u32[]{:S(2)}, u32[]{:S(2)}) async-start(f32[8,1,36864]{2,1,0:T(1,128)} %reshape.61), calls=%async_computation.2 | async-start | bytes 2359296 | tf_op jit(solution)/shard_map/all_to_all | solution.py:49
  178.5 187.2 %all-gather.5.cloned.1.call-start = ((), (), s32[]{:S(2)}) async-start(), calls=%async_computation.8 | async-start | bytes 19464192 | tf_op jit(solution)/shard_map/all_gather | solution.py:41
  211.9 1.9 copy-start.1
  213.7 1.3 copy-start.3
  213.7 1.3 copy-start.6
  218.0 1.0 copy-start.5
  219.0 3.9 copy-start.10
  219.0 3.9 copy-start.9
  385.8 7.6 %copy-start.11 = (f32[24,96]{1,0:T(8,128)S(1)}, f32[24,96]{1,0:T(8,128)}, u32[]{:S(2)}) copy-start(f32[24,96]{1,0:T(8,128)} %copy-done.10) | copy-start | bytes 27652
  385.8 7.6 %copy-start.16 = (f32[2,128,128]{2,1,0:T(8,128)S(1)}, f32[2,128,128]{2,1,0:T(8,128)}, u32[]{:S(2)}) copy-start(f32[2,128,128]{2,1,0:T(8,128)} %param.12) | copy-start | bytes 393220
  385.8 23.9 %all-to-all-start.6 = ((f32[8,1,36864]{2,1,0:T(1,128)}), f32[8,1,36864]{2,1,0:T(1,128)S(1)}, u32[]{:S(2)}, u32[]{:S(2)}) async-start(f32[8,1,36864]{2,1,0:T(1,128)} %reshape.65), calls=%async_computation.6 | async-start | bytes 2359296 | tf_op jit(solution)/shard_map/all_to_all | solution.py:49
  425.6 1.3 copy-start.2
  425.6 1.3 copy-start.7
Sparse Core Ops, SparseCore 0:
  38.9 110.9 all-gather.2
  243.5 122.1 all-gather.4
where the time goes:
time: 446 us; the launch traced here: 438 us
  waiting for transfers between devices  166 us (37%)
  blocking collectives  103 us (23%)
  local copies, waits for them, and re-layouts  88.9 us (20%)
  matrix products  36 us (8%)
  starting transfers between devices  15 us (3%)
  other arithmetic  14.4 us (3%)
  between operations  13.9 us (3%)
    all_gather x1, waiting for transfers between devices, outgoing(): lax.all_gather(right, 'band', axis=1, tiled=True)  93.5 us
    all_gather x1, waiting for transfers between devices, incoming(): lax.all_gather(right, 'band', axis=1, tiled=True)  45.3 us
    unnamed x40, local copies, waits for them, and re-layouts  43 us
    all_to_all x2, blocking collectives, on_device(): lax.all_to_all(right, 'hid', split_axis=0, concat_axis=2, tiled=True)  36.3 us
    all_to_all x1, blocking collectives, incoming(): lax.all_to_all(left, 'band', split_axis=2, concat_axis=1, tiled=True)  34.5 us
    all_to_all x2, blocking collectives, on_device(): lax.all_to_all(left, 'hid', split_axis=0, concat_axis=2, tiled=True)  32 us
    all_to_all x2, waiting for transfers between devices, finish(): lax.all_to_all(tri, 'hid', split_axis=2, concat_axis=0, tiled=True)  27.6 us
    all_to_all x2, starting transfers between devices, finish(): lax.all_to_all(tri, 'hid', split_axis=2, concat_axis=0, tiled=True)  15 us
  transfers between devices with their start and end apart: 4, of which 4 were waited for; matrix products, arithmetic and copies ran while one was open for 6% of the time, Pallas kernels for 0%

commit v1 on v0

v1 whole, which is shorter than its diff:
```python
import jax
import jax.numpy as jnp
from jax import lax
from jax.experimental import pallas as pl
from jax.experimental.pallas import tpu as pltpu
from jax.sharding import Mesh, PartitionSpec as P

EPS = 1e-05
F32 = jnp.float32
BF16 = jnp.bfloat16
ROWS = 24
COLS = 96
PIX = ROWS * COLS
CH = 128
MSG = 40
CHIPS = ("z", "yl", "x", "yh")


def split_bf16(value):
    high = value.astype(BF16)
    low = (value - high.astype(F32)).astype(BF16)
    return high, low


def lanes(shape):
    return lax.broadcasted_iota(jnp.int32, shape, len(shape) - 1)


def matmul(a, b, dims):
    return lax.dot_general(a, b, (dims, ((), ())), preferred_element_type=F32)


def edge_rows(mask_sm, hot_sm, mask_ref, hot_ref, inter_ref, edge_ref):
    band = (lax.axis_index("z") * 2 + lax.axis_index("yl")) * 2 + lax.axis_index("core")
    hid = lax.axis_index("x") * 2 + lax.axis_index("yh")
    shift = (8 - hid) * COLS
    col_mask = pltpu.roll(jnp.broadcast_to(mask_ref[...], (8, 768)), shift, 1)[0:1, 0:128]
    col_hot = pltpu.roll(jnp.broadcast_to(hot_ref[...], (8, 768)), shift, 1)[0:1, 0:128]
    col_mask = jnp.where(lanes((1, 128)) < COLS, col_mask, 0)
    for r in range(ROWS):
        flags = jnp.maximum(inter_ref[r : r + 1, :], jnp.maximum(col_hot[:, :COLS], hot_sm[band * ROWS + r]))
        value = flags * col_mask[:, :COLS] * mask_sm[band * ROWS + r]
        edge_ref[r : r + 1, :] = jnp.zeros((1, 128), F32)
        edge_ref[r : r + 1, 0:COLS] = value.astype(F32)


def project(state_ref, proj_ref, gatew_ref, edge_ref, norm_ref, mix_ref, keep_ref, send_ref, gate_ref):
    gate_hi, gate_lo = split_bf16(gatew_ref[...])
    gate_cat = jnp.concatenate([gate_hi, gate_lo, gate_hi], axis=0)

    def normalize(r, carry):
        at = pl.ds(pl.multiple_of(r * COLS, COLS), COLS)
        x = state_ref[at, :]
        centred = x - jnp.mean(x, axis=-1, keepdims=True)
        variance = jnp.mean(centred * centred, axis=-1, keepdims=True)
        high, low = split_bf16(centred * lax.rsqrt(variance + EPS))
        cat = jnp.concatenate([high, high, low], axis=1)
        norm_ref[at, :] = cat
        gate_ref[at, :] = jax.nn.sigmoid(matmul(cat, gate_cat, ((1,), (0,))))
        return carry

    lax.fori_loop(0, ROWS, normalize, 0, unroll=2)
    norm_ref[PIX : PIX + 32, :] = jnp.zeros((32, 384), BF16)
    w_hi, w_lo = split_bf16(proj_ref[...].T)
    w_cat = jnp.concatenate([w_hi, w_lo, w_hi], axis=1)

    def pair_row(r):
        at = pl.ds(pl.multiple_of(r * COLS, COLS), 128)
        values = matmul(w_cat, norm_ref[at, :], ((1,), (1,)))
        edge = edge_ref[pl.ds(r, 1), :]
        left = edge * jax.nn.sigmoid(values[CH : 2 * CH]) * values[:CH]
        right = edge * jax.nn.sigmoid(values[3 * CH :]) * values[2 * CH : 3 * CH]
        return left, right

    lane = lanes((CH, 128))

    def last(q, carry):
        left, right = pair_row(q + 16)
        keep_ref[q] = right
        mix_ref[pl.ds(q + 16, CH, stride=MSG), :] = jnp.where(lane < COLS, left, pltpu.roll(right, 32, 1))
        return carry

    def first(r, carry):
        left, right = pair_row(r)
        third = r // 8
        tail = pltpu.roll(keep_ref[r - 8 * third], 96 - 32 * third, 1)
        mix_ref[pl.ds(r, CH, stride=MSG), :] = jnp.where(lane < COLS, left, tail)
        mix_ref[pl.ds(r + 24, CH, stride=MSG), :] = right
        return carry

    lax.fori_loop(0, 8, last, 0)
    lax.fori_loop(0, 16, first, 0)

    def pack(h, carry):
        at = pl.ds(pl.multiple_of(h * MSG, MSG), MSG)
        send_ref[h] = mix_ref[at, :].astype(BF16)
        return carry

    lax.fori_loop(0, CH, pack, 0, unroll=8)


def first_kernel(mask_sm, hot_sm, mask_ref, hot_ref, inter_ref, state_ref, proj_ref, gatew_ref,
                 send_ref, gate_ref, edge_ref, norm_ref, mix_ref, keep_ref):
    edge_rows(mask_sm, hot_sm, mask_ref, hot_ref, inter_ref, edge_ref)
    project(state_ref, proj_ref, gatew_ref, edge_ref, norm_ref, mix_ref, keep_ref, send_ref, gate_ref)


def unpack(block):
    lane = lanes((8, 128))
    third = jnp.where(lane < 64, pltpu.roll(block[8:16], 64, 1), pltpu.roll(block[16:24], 96, 1))
    third = jnp.where(lane < 32, pltpu.roll(block[0:8], 32, 1), third)
    third = jnp.where(lane < COLS, third, 0.0)
    return block[0:24], jnp.concatenate([block[24:40], third], axis=0)


def outgoing_kernel(own_ref, other_ref, out_ref, left_ref, right_ref):
    core = lax.axis_index("core")

    def place(b, carry):
        z = b // 2
        base = z * 128 + (b - 2 * z) * 48
        rows = pl.ds(pl.multiple_of(b * 24, 24), 24)
        mine = pl.ds(pl.multiple_of(base + core * 24, 8), 24)
        theirs = pl.ds(pl.multiple_of(base + 24 - core * 24, 8), 24)
        for g in range(8):
            at = slice(128 * g, 128 * g + 128)
            left, right = unpack(own_ref[b * 8 + g].astype(F32))
            left_ref[rows, at] = left
            right_ref[mine, at] = right
            _, right = unpack(other_ref[b * 8 + g].astype(F32))
            right_ref[theirs, at] = right
        return carry

    lax.fori_loop(0, 16, place, 0)
    for z in range(8):
        right_ref[128 * z + 96 : 128 * z + 128, :] = jnp.zeros((32, 1024), F32)
    left = left_ref[...].astype(BF16)
    for g in range(8):
        tri = matmul(left, right_ref[128 * g : 128 * g + 128, :].astype(BF16), ((1,), (1,)))
        for b in range(16):
            out_ref[b * 8 + g] = tri[24 * b : 24 * b + 24].astype(BF16)


def incoming_kernel(own_ref, other_ref, out_ref, left_ref, right_ref, tri_ref):
    core = lax.axis_index("core")

    def place(b, carry):
        rows = pl.ds(pl.multiple_of(b * 24, 24), 24)
        rows2 = pl.ds(pl.multiple_of(384 + b * 24, 24), 24)
        for g in range(8):
            at = slice(128 * g, 128 * g + 128)
            left_ref[rows, at], right_ref[rows, at] = unpack(own_ref[b * 8 + g].astype(F32))
            left_ref[rows2, at], right_ref[rows2, at] = unpack(other_ref[b * 8 + g].astype(F32))
        return carry

    lax.fori_loop(0, 16, place, 0)
    right = right_ref[...].astype(BF16)
    for z in range(8):
        left = left_ref[:, 128 * z : 128 * z + 128].T.astype(BF16)
        tri_ref[...] = matmul(left, right, ((1,), (0,)))
        for y in range(2):
            rows = tri_ref[pl.ds(pl.multiple_of(48 * y + 24 * core, 8), 24), :].astype(BF16)
            for g in range(8):
                out_ref[(2 * z + y) * 8 + g] = rows[:, 128 * g : 128 * g + 128]


def finish(tri_ref, state_ref, gate_ref, outw_ref, scaled_ref, next_ref):
    def stats(h, carry):
        total, square = carry
        t = tri_ref[h].astype(F32)
        return total + t, square + t * t

    zero = jnp.zeros((24, 128), F32)
    total, square = lax.fori_loop(0, CH, stats, (zero, zero), unroll=8)
    average = total * (1.0 / CH)
    scale = lax.rsqrt(square * (1.0 / CH) - average * average + EPS)

    def rescale(h, carry):
        at = pl.ds(pl.multiple_of(h * 24, 24), 24)
        scaled_ref[at, :] = (tri_ref[h].astype(F32) - average) * scale
        return carry

    lax.fori_loop(0, CH, rescale, 0, unroll=8)
    w_hi, w_lo = split_bf16(outw_ref[...])
    w_cat = jnp.concatenate([w_hi, w_lo, w_hi], axis=0)

    def combine(r, carry):
        scaled = scaled_ref[pl.ds(r, CH, stride=24), :].T[:COLS]
        high, low = split_bf16(scaled)
        cat = jnp.concatenate([high, high, low], axis=1)
        at = pl.ds(pl.multiple_of(r * COLS, COLS), COLS)
        next_ref[at, :] = state_ref[at, :] + gate_ref[at, :] * matmul(cat, w_cat, ((1,), (0,)))
        return carry

    lax.fori_loop(0, ROWS, combine, 0, unroll=2)


def middle_kernel(mask_sm, hot_sm, mask_ref, hot_ref, inter_ref, tri_ref, state_ref, gate_ref, outw_ref, proj_ref,
                  gatew_ref, next_ref, send_ref, gate2_ref, edge_ref, norm_ref, mix_ref, keep_ref, scaled_ref):
    finish(tri_ref, state_ref, gate_ref, outw_ref, scaled_ref, next_ref)
    edge_rows(mask_sm, hot_sm, mask_ref, hot_ref, inter_ref, edge_ref)
    project(next_ref, proj_ref, gatew_ref, edge_ref, norm_ref, mix_ref, keep_ref, send_ref, gate2_ref)


def last_kernel(tri_ref, state_ref, gate_ref, outw_ref, next_ref, scaled_ref):
    finish(tri_ref, state_ref, gate_ref, outw_ref, scaled_ref, next_ref)


VM = pl.BlockSpec(memory_space=pltpu.VMEM)
SM = pl.BlockSpec(memory_space=pltpu.SMEM)
STATE = jax.ShapeDtypeStruct((PIX, CH), F32)
SEND = jax.ShapeDtypeStruct((CH, MSG, 128), BF16)
TRI = jax.ShapeDtypeStruct((CH, 24, 128), BF16)
PROJECT_SCRATCH = [
    pltpu.VMEM((24, 128), F32),
    pltpu.VMEM((PIX + 32, 384), BF16),
    pltpu.VMEM((CH * MSG, 128), F32),
    pltpu.VMEM((8, CH, 128), F32),
]


def exchange(message):
    return lax.all_to_all(message, CHIPS, split_axis=0, concat_axis=0, tiled=True)


def triangle(kernel, message, scratch):
    own = exchange(message)
    other = lax.ppermute(own, "core", [(0, 1), (1, 0)])
    tri = pl.pallas_call(kernel, out_shape=TRI, in_specs=[VM, VM], out_specs=VM, scratch_shapes=scratch)(own, other)
    return exchange(tri)


def on_device(pair, residue_mask, hotspot, interface, proj_weight, gate_weight, out_weight):
    state = pair.reshape(PIX, CH)
    flags = (residue_mask, hotspot, residue_mask.reshape(1, 768), hotspot.reshape(1, 768), interface)
    flag_specs = [SM, SM, VM, VM, VM]
    send, gate = pl.pallas_call(
        first_kernel, out_shape=(SEND, STATE), in_specs=flag_specs + [VM] * 3, out_specs=(VM, VM),
        scratch_shapes=PROJECT_SCRATCH,
    )(*flags, state, proj_weight[0], gate_weight[0])
    tri = triangle(outgoing_kernel, send, [pltpu.VMEM((384, 1024), F32), pltpu.VMEM((1024, 1024), F32)])
    state, send, gate = pl.pallas_call(
        middle_kernel, out_shape=(STATE, SEND, STATE), in_specs=flag_specs + [VM] * 6, out_specs=(VM, VM, VM),
        scratch_shapes=PROJECT_SCRATCH + [pltpu.VMEM((CH * 24, 128), F32)],
    )(*flags, tri, state, gate, out_weight[0], proj_weight[1], gate_weight[1])
    tri = triangle(
        incoming_kernel, send,
        [pltpu.VMEM((768, 1024), F32), pltpu.VMEM((768, 1024), F32), pltpu.VMEM((128, 1024), F32)],
    )
    state = pl.pallas_call(
        last_kernel, out_shape=STATE, in_specs=[VM] * 4, out_specs=VM, scratch_shapes=[pltpu.VMEM((CH * 24, 128), F32)],
    )(tri, state, gate, out_weight[1])
    return state.reshape(ROWS, COLS, CH)


def solution(mesh):
    grid = Mesh(mesh.devices.reshape(8, 2, 2, 4, 2), ("z", "yl", "core", "x", "yh"))
    rows = ("z", "yl", "core")
    cols = ("x", "yh")
    return jax.shard_map(
        on_device,
        mesh=grid,
        in_specs=(P(rows, cols, None), P(), P(), P(rows, cols), P(), P(), P()),
        out_specs=P(rows, cols, None),
        check_vma=False,
    )
```

time: 446 us -> 226 us (0.51); the launches traced: 438 us -> 225 us
  waiting for transfers between devices: 166 us -> 30.7 us
  local copies, waits for them, and re-layouts: 88.9 us -> 9.66 us
  Pallas kernels: 0 us -> 53 us
  matrix products: 36 us -> 0 us
  blocking collectives: 103 us -> 125 us
  other arithmetic: 14.4 us -> 0 us
  between operations: 13.9 us -> 0.03 us
  starting transfers between devices: 15 us -> 6.67 us
    all_gather x2 -> x0, waiting for transfers between devices: 139 us -> none  [the longest x1 93.5 us: outgoing(): lax.all_gather(right, 'band', axis=1, tiled=True)]
    pallas_call x0 -> x5, Pallas kernels: none -> 53 us  [the longest x1 19.5 us: on_device(): pl.pallas_call(middle_kernel, out_shape=(STATE, SEND, STATE), in_specs=fl...]
    unnamed x40 -> x12, local copies, waits for them, and re-layouts: 43 us -> 3 us
    dot_general x8 -> x0, matrix products: 36 us -> none  [the longest x1 8.91 us: outgoing(): lax.dot_general(left, lax.all_gather(right, 'band', axis=1, tiled=True),...]
    all_to_all x12 -> x0, local copies, waits for them, and re-layouts: 31.1 us -> none  [the longest x3 11.4 us: finish(): lax.all_to_all(tri, 'hid', split_axis=2, concat_axis=0, tiled=True)]
    all_to_all x5 -> x3, blocking collectives: 103 us -> 125 us  [exchange(): lax.all_to_all(message, CHIPS, split_axis=0, concat_axis=0, tiled=True)]
    dot_general x2 -> x0, local copies, waits for them, and re-layouts: 9.98 us -> none  [the longest x1 5 us: outgoing(): lax.dot_general(left, lax.all_gather(right, 'band', axis=1, tiled=True),...]
    all_to_all x2 -> x1, starting transfers between devices: 15 us -> 6.67 us  [exchange(): lax.all_to_all(message, CHIPS, split_axis=0, concat_axis=0, tiled=True)]
  transfers between devices with their start and end apart: 4 -> 3, of which waited for: 4 -> 3; matrix products, arithmetic and copies ran while one was open for 6% -> 0% of each run, Pallas kernels for 0% -> 0%
where the time goes in v1:
time: 226 us; the launch traced here: 225 us
  blocking collectives  125 us (55%)
  Pallas kernels  53 us (23%)
  waiting for transfers between devices  30.7 us (14%)
  local copies, waits for them, and re-layouts  9.66 us (4%)
  starting transfers between devices  6.67 us (3%)
    all_to_all x3, blocking collectives, exchange(): lax.all_to_all(message, CHIPS, split_axis=0, concat_axis=0, tiled=True)  125 us
    all_to_all x1, waiting for transfers between devices, exchange(): lax.all_to_all(message, CHIPS, split_axis=0, concat_axis=0, tiled=True)  24.6 us
    pallas_call x1, Pallas kernels, on_device(): pl.pallas_call(middle_kernel, out_shape=(STATE, SEND, STATE), in_specs=fl...  19.5 us
    pallas_call x1, Pallas kernels, on_device(): pl.pallas_call(first_kernel, out_shape=(SEND, STATE), in_specs=flag_specs...  14.9 us
    pallas_call x2, Pallas kernels, triangle(): pl.pallas_call(kernel, out_shape=TRI, in_specs=[VM, VM], out_specs=VM, sc...  12.2 us
    all_to_all x1, starting transfers between devices, exchange(): lax.all_to_all(message, CHIPS, split_axis=0, concat_axis=0, tiled=True)  6.67 us
    pallas_call x1, Pallas kernels, on_device(): pl.pallas_call(last_kernel, out_shape=STATE, in_specs=[VM] * 4, out_specs...  6.43 us
    ppermute x2, waiting for transfers between devices, triangle(): other = lax.ppermute(own, 'core', [(0, 1), (1, 0)])  6.06 us
  transfers between devices with their start and end apart: 3, of which 3 were waited for; matrix products, arithmetic and copies ran while one was open for 0% of the time, Pallas kernels for 0%

profile of v1, /device:TPU:6, one launch (start us, length us, event | category | flops | bytes accessed | tf_op | source)
XLA Modules:
  0.0 225.5 jit_solution(11162746578306974178)
XLA Ops:
  0.0 1.3 reshape.12.mask_ref
  1.3 1.3 reshape.13.hot_ref
  2.6 1.6 slice_bitcast_fusion.3
  4.1 1.9 slice_bitcast_fusion
  6.0 14.9 %shard_map.73 = (bf16[128,40,128]{2,1,0:T(8,128)(2,1)}, f32[2304,128]{1,0:T(8,128)}) custom-call(s32[768]{0:T(1024)} %mask_sm.3, s32[768]{0:T(1024)} %hot_sm.3, s32[1,768]{1,0:T(1,128)} %reshape.12.mask_ref, s32[1,768]{1,0:T(1,128)} %reshape.13.hot_ref, s32[24,96]{1,0:T(8,128)} %inter_ref.3, f32[2304,128]{1,0:T(8,128)} %bitcast.14, ...), custom_call_target="tpu_custom_call" | custom-call | tf_op jit(solution)/shard_map/pallas_call | solution.py:237
  20.9 51.6 %all_to_all.20.own_ref = bf16[128,40,128]{2,1,0:T(8,128)(2,1)S(1)} all-to-all(bf16[128,40,128]{2,1,0:T(8,128)(2,1)} %get-tuple-element.10), channel_id=1, replica_groups=mesh['z'=8,'yl'=2,'core'=2,'x'=4,'yh'=2] {'z','yl','x','yh'}, dimensions={0} | all-to-all | bytes 2621440 | tf_op jit(solution)/shard_map/all_to_all | solution.py:223
  72.5 0.0 collective-permute-start
  72.5 3.0 %collective-permute-done.other_ref = bf16[128,40,128]{2,1,0:T(8,128)(2,1)S(1)} collective-permute-done((bf16[128,40,128]{2,1,0:T(8,128)(2,1)S(1)}, bf16[128,40,128]{2,1,0:T(8,128)(2,1)S(1)}, u32[]{:S(2)}, u32[]{:S(2)}) %collective-permute-start) | collective-permute-done | bytes 1310752 | tf_op jit(solution)/shard_map/ppermute | solution.py:228
  75.5 0.0 copy-done
  75.5 1.1 copy-done.3
  76.6 6.0 %shard_map.74 = bf16[128,24,128]{2,1,0:T(8,128)(2,1)} custom-call(bf16[128,40,128]{2,1,0:T(8,128)(2,1)} %copy-done, bf16[128,40,128]{2,1,0:T(8,128)(2,1)} %copy-done.3), custom_call_target="tpu_custom_call" | custom-call | tf_op jit(solution)/shard_map/pallas_call | solution.py:229
  82.5 6.7 %all-to-all-start.1 = ((bf16[128,24,128]{2,1,0:T(8,128)(2,1)}), bf16[128,24,128]{2,1,0:T(8,128)(2,1)S(1)}, u32[]{:S(2)}, u32[]{:S(2)}) async-start(bf16[128,24,128]{2,1,0:T(8,128)(2,1)} %shard_map.74), calls=%async_computation.1 | async-start | bytes 1572864 | tf_op jit(solution)/shard_map/all_to_all | solution.py:223
  89.2 0.0 copy-done.5
  89.2 0.7 slice_bitcast_fusion.2
  89.9 24.6 %all-to-all-done.1.tri_ref = bf16[128,24,128]{2,1,0:T(8,128)(2,1)S(1)} async-done(((bf16[128,24,128]{2,1,0:T(8,128)(2,1)}), bf16[128,24,128]{2,1,0:T(8,128)(2,1)S(1)}, u32[]{:S(2)}, u32[]{:S(2)}) %all-to-all-start.1) | async-done | bytes 786464 | tf_op jit(solution)/shard_map/all_to_all | solution.py:223
  114.5 0.9 copy-done.2
  115.4 19.5 %shard_map.75 = (f32[2304,128]{1,0:T(8,128)}, bf16[128,40,128]{2,1,0:T(8,128)(2,1)}, f32[2304,128]{1,0:T(8,128)}) custom-call(s32[768]{0:T(1024)} %mask_sm.3, s32[768]{0:T(1024)} %hot_sm.3, s32[1,768]{1,0:T(1,128)} %reshape.12.mask_ref, s32[1,768]{1,0:T(1,128)} %reshape.13.hot_ref, s32[24,96]{1,0:T(8,128)} %inter_ref.3, bf16[128,24,128]{2,1,0:T(8,128)(2,1)} %copy-done.2, ...), custom_call_target="tpu_custom_call" | custom-call | tf_op jit(solution)/shard_map/pallas_call | solution.py:242
  134.8 42.0 %all_to_all.21.own_ref = bf16[128,40,128]{2,1,0:T(8,128)(2,1)S(1)} all-to-all(bf16[128,40,128]{2,1,0:T(8,128)(2,1)} %get-tuple-element.12), channel_id=1, replica_groups=mesh['z'=8,'yl'=2,'core'=2,'x'=4,'yh'=2] {'z','yl','x','yh'}, dimensions={0} | all-to-all | bytes 2621440 | tf_op jit(solution)/shard_map/all_to_all | solution.py:223
  176.8 0.0 collective-permute-start.1
  176.8 3.0 %collective-permute-done.1.other_ref = bf16[128,40,128]{2,1,0:T(8,128)(2,1)S(1)} collective-permute-done((bf16[128,40,128]{2,1,0:T(8,128)(2,1)S(1)}, bf16[128,40,128]{2,1,0:T(8,128)(2,1)S(1)}, u32[]{:S(2)}, u32[]{:S(2)}) %collective-permute-start.1) | collective-permute-done | bytes 1310752 | tf_op jit(solution)/shard_map/ppermute | solution.py:228
  179.9 1.1 copy-done.4
  180.9 6.2 %shard_map.76 = bf16[128,24,128]{2,1,0:T(8,128)(2,1)} custom-call(bf16[128,40,128]{2,1,0:T(8,128)(2,1)} %copy-done.1, bf16[128,40,128]{2,1,0:T(8,128)(2,1)} %copy-done.4), custom_call_target="tpu_custom_call" | custom-call | tf_op jit(solution)/shard_map/pallas_call | solution.py:229
  187.2 31.9 %all_to_all.22.tri_ref = bf16[128,24,128]{2,1,0:T(8,128)(2,1)} all-to-all(bf16[128,24,128]{2,1,0:T(8,128)(2,1)} %shard_map.76), channel_id=1, replica_groups=mesh['z'=8,'yl'=2,'core'=2,'x'=4,'yh'=2] {'z','yl','x','yh'}, dimensions={0} | all-to-all | bytes 1572864 | tf_op jit(solution)/shard_map/all_to_all | solution.py:223
  219.1 6.4 %shard_map.77 = f32[2304,128]{1,0:T(8,128)} custom-call(bf16[128,24,128]{2,1,0:T(8,128)(2,1)} %all_to_all.22.tri_ref, f32[2304,128]{1,0:T(8,128)} %get-tuple-element.13.state_ref, f32[2304,128]{1,0:T(8,128)} %get-tuple-element.14.gate_ref, f32[128,128]{1,0:T(8,128)} %get-tuple-element.17.outw_ref), custom_call_target="tpu_custom_call" | custom-call | tf_op jit(solution)/shard_map/pallas_call | solution.py:250
  (7 shorter events, 0.0 us)
Async XLA Ops:
  72.5 3.0 %copy-start = (bf16[128,40,128]{2,1,0:T(8,128)(2,1)}, bf16[128,40,128]{2,1,0:T(8,128)(2,1)S(1)}, u32[]{:S(2)}) copy-start(bf16[128,40,128]{2,1,0:T(8,128)(2,1)S(1)} %all_to_all.20.own_ref) | copy-start | bytes 3932164
  72.5 3.0 %collective-permute-start = (bf16[128,40,128]{2,1,0:T(8,128)(2,1)S(1)}, bf16[128,40,128]{2,1,0:T(8,128)(2,1)S(1)}, u32[]{:S(2)}, u32[]{:S(2)}) collective-permute-start(bf16[128,40,128]{2,1,0:T(8,128)(2,1)S(1)} %all_to_all.20.own_ref), channel_id=1, source_target_pairs={{0,8},{8,0},{1,9},{9,1},{2,10},{10,2},{3,11},{11,3},{4,12},{12,4},... | collective-permute-start | bytes 3932168 | tf_op jit(solution)/shard_map/ppermute | solution.py:228
  75.5 1.1 copy-start.3
  82.5 6.7 %copy-start.5 = (f32[2,128,128]{2,1,0:T(8,128)S(1)}, f32[2,128,128]{2,1,0:T(8,128)}, u32[]{:S(2)}) copy-start(f32[2,128,128]{2,1,0:T(8,128)} %param.13) | copy-start | bytes 393220
  82.5 32.0 %all-to-all-start.1 = ((bf16[128,24,128]{2,1,0:T(8,128)(2,1)}), bf16[128,24,128]{2,1,0:T(8,128)(2,1)S(1)}, u32[]{:S(2)}, u32[]{:S(2)}) async-start(bf16[128,24,128]{2,1,0:T(8,128)(2,1)} %shard_map.74), calls=%async_computation.1 | async-start | bytes 1572864 | tf_op jit(solution)/shard_map/all_to_all | solution.py:223
  114.5 0.9 copy-start.2
  176.8 3.0 %copy-start.1 = (bf16[128,40,128]{2,1,0:T(8,128)(2,1)}, bf16[128,40,128]{2,1,0:T(8,128)(2,1)S(1)}, u32[]{:S(2)}) copy-start(bf16[128,40,128]{2,1,0:T(8,128)(2,1)S(1)} %all_to_all.21.own_ref) | copy-start | bytes 3932164
  176.8 3.0 %collective-permute-start.1 = (bf16[128,40,128]{2,1,0:T(8,128)(2,1)S(1)}, bf16[128,40,128]{2,1,0:T(8,128)(2,1)S(1)}, u32[]{:S(2)}, u32[]{:S(2)}) collective-permute-start(bf16[128,40,128]{2,1,0:T(8,128)(2,1)S(1)} %all_to_all.21.own_ref), channel_id=1, source_target_pairs={{0,8},{8,0},{1,9},{9,1},{2,10},{10,2},{3,11},{11,3},{4,12},{12,4},... | collective-permute-start | bytes 3932168 | tf_op jit(solution)/shard_map/ppermute | solution.py:228
  179.9 1.1 copy-start.4

commit v2 on v0

v2 whole, which is shorter than its diff:
```python
import jax
import jax.numpy as jnp
from jax import lax
from jax.experimental import pallas as pl
from jax.experimental.pallas import tpu as pltpu
from jax.sharding import Mesh, PartitionSpec as P

EPS = 1e-05
F32 = jnp.float32
BF16 = jnp.bfloat16
ROWS = 24
COLS = 96
PIX = ROWS * COLS
CH = 128
PACK = 18
CHIPS = ("z", "yl", "x", "yh")


def split_bf16(value):
    high = value.astype(BF16)
    low = (value - high.astype(F32)).astype(BF16)
    return high, low


def lanes(shape):
    return lax.broadcasted_iota(jnp.int32, shape, len(shape) - 1)


def matmul(a, b, dims):
    return lax.dot_general(a, b, (dims, ((), ())), preferred_element_type=F32)


def aligned(start, size, unit):
    return pl.ds(pl.multiple_of(start, unit), size)


def packed_edge(mask_sm, hot_sm, inter_ref, edge_ref, rows_ref):
    band = (lax.axis_index("z") * 2 + lax.axis_index("yl")) * 2 + lax.axis_index("core")
    hid = lax.axis_index("x") * 2 + lax.axis_index("yh")
    lane = lanes((1, 128))
    col_mask = jnp.zeros((1, 128), jnp.int32)
    col_hot = jnp.zeros((1, 128), jnp.int32)
    for c in range(COLS):
        col_mask = jnp.where(lane == c, mask_sm[hid * COLS + c], col_mask)
        col_hot = jnp.where(lane == c, hot_sm[hid * COLS + c], col_hot)
    rows_ref[...] = jnp.zeros((ROWS, 128), jnp.int32)
    rows_ref[:, 0:COLS] = inter_ref[...]
    for r in range(ROWS):
        at = slice(r, r + 1)
        flags = jnp.maximum(rows_ref[at, :], jnp.maximum(col_hot, hot_sm[band * ROWS + r]))
        rows_ref[at, :] = flags * col_mask * mask_sm[band * ROWS + r]
    for t in range(PACK):
        tail = pltpu.roll(jnp.broadcast_to(rows_ref[18 + t % 6 : 19 + t % 6, :], (8, 128)), 96 - 32 * (t // 6), 1)
        edge_ref[t : t + 1, :] = jnp.where(lane < COLS, rows_ref[t : t + 1, :], tail[0:1, :]).astype(F32)


def tail_pixels(t):
    return aligned((18 + t % 6) * COLS + 32 * (t // 6), 32, 32)


def project(state_ref, weight, edge_ref, norm_ref, mix_ref, send_ref):
    def normalize(t, carry):
        x = jnp.concatenate([state_ref[aligned(t * COLS, COLS, COLS), :], state_ref[tail_pixels(t), :]], axis=0)
        centred = x - jnp.mean(x, axis=-1, keepdims=True)
        variance = jnp.mean(centred * centred, axis=-1, keepdims=True)
        high, low = split_bf16(centred * lax.rsqrt(variance + EPS))
        at = aligned(t * 128, 128, 128)
        norm_ref[at, 0:128] = high
        norm_ref[at, 128:256] = high
        norm_ref[at, 256:384] = low
        return carry

    lax.fori_loop(0, PACK, normalize, 0, unroll=3)
    w_hi, w_lo = split_bf16(weight.T)
    w_cat = jnp.concatenate([w_hi, w_lo, w_hi], axis=1)

    def pair(i, carry):
        values = matmul(w_cat, norm_ref[aligned(i * 256, 256, 256), :], ((1,), (1,)))
        for half in range(2):
            t = 2 * i + half
            part = values[:, 128 * half : 128 * half + 128]
            edge = edge_ref[pl.ds(t, 1), :]
            left = edge * jax.nn.sigmoid(part[CH : 2 * CH]) * part[:CH]
            right = edge * jax.nn.sigmoid(part[3 * CH :]) * part[2 * CH : 3 * CH]
            mix_ref[pl.ds(t, CH, stride=2 * PACK), :] = left
            mix_ref[pl.ds(t + PACK, CH, stride=2 * PACK), :] = right
        return carry

    lax.fori_loop(0, PACK // 2, pair, 0, unroll=3)

    def convert(i, carry):
        at = aligned(i * 256, 256, 256)
        send_ref[at, :] = mix_ref[at, :].astype(BF16)
        return carry

    lax.fori_loop(0, 18, convert, 0)


def first_kernel(mask_sm, hot_sm, inter_ref, state_ref, proj_ref, send_ref, edge_ref, rows_ref, norm_ref, mix_ref):
    packed_edge(mask_sm, hot_sm, inter_ref, edge_ref, rows_ref)
    project(state_ref, proj_ref[0], edge_ref, norm_ref, mix_ref, send_ref)


def gate_kernel(layer):
    def body(state_ref, gatew_ref, gate_ref):
        hi, lo = split_bf16(gatew_ref[layer])
        cat = jnp.concatenate([hi, lo, hi], axis=0)

        def step(i, carry):
            at = aligned(i * 128, 128, 128)
            x = state_ref[at, :]
            centred = x - jnp.mean(x, axis=-1, keepdims=True)
            variance = jnp.mean(centred * centred, axis=-1, keepdims=True)
            high, low = split_bf16(centred * lax.rsqrt(variance + EPS))
            gate_ref[at, :] = jax.nn.sigmoid(matmul(jnp.concatenate([high, high, low], axis=1), cat, ((1,), (0,))))
            return carry

        lax.fori_loop(0, PACK, step, 0, unroll=3)

    return body


PAD = 8


def widen(source_ref, wide_ref):
    def step(i, carry):
        wide_ref[aligned(PAD + i * 256, 256, 8), :] = source_ref[aligned(i * 256, 256, 256), :].astype(F32)
        return carry

    lax.fori_loop(0, 18, step, 0)


def unpack(wide_ref, base):
    lane = lanes((8, 128))
    sub = lax.broadcasted_iota(jnp.int32, (8, 128), 0)

    def rows(at):
        return wide_ref[pl.ds(base + at, 8), :]

    third = jnp.where(lane < 64, pltpu.roll(rows(4), 64, 1), pltpu.roll(rows(10), 96, 1))
    third = jnp.where(lane < 32, pltpu.roll(rows(-2), 32, 1), third)
    return rows(0), rows(8), jnp.where(sub < 2, rows(16), third)


def place(wide_ref, base, target_ref, start, column, clear):
    lane = lanes((8, 128))
    for n, part in enumerate(unpack(wide_ref, base)):
        if clear:
            part = jnp.where(lane < COLS, part, 0.0)
        target_ref[aligned(start + 8 * n, 8, 8), column] = part


def pack_tri(tri_ref, base, wide_ref, target):
    lane = lanes((8, 128))
    sub = lax.broadcasted_iota(jnp.int32, (8, 128), 0)

    def rows(at, shift=0):
        value = tri_ref[pl.ds(base + at, 8), :]
        return pltpu.roll(value, shift, 1) if shift else value

    tails = (
        jnp.where(sub < 6, rows(18, 96), rows(12, 64)),
        jnp.where(sub < 4, rows(20, 64), rows(14, 32)),
        rows(22, 32),
    )
    for n, tail in enumerate(tails):
        value = jnp.where(lane < COLS, rows(8 * n), tail)
        if n < 2:
            wide_ref[pl.ds(target + 8 * n, 8), :] = value
        else:
            wide_ref[pl.ds(target + 16, 2), :] = value[0:2]


def narrow(wide_ref, out_ref):
    def step(i, carry):
        at = aligned(i * 256, 256, 256)
        out_ref[at, :] = wide_ref[at, :].astype(BF16)
        return carry

    lax.fori_loop(0, 9, step, 0)


def outgoing_kernel(own_ref, other_ref, out_ref, own_wide, other_wide, left_ref, right_ref, tri_ref, mix_ref):
    core = lax.axis_index("core")
    widen(own_ref, own_wide)
    widen(other_ref, other_wide)

    def step(b, carry):
        z = b // 2
        base = z * 128 + (b - 2 * z) * 48
        for g in range(8):
            at = slice(128 * g, 128 * g + 128)
            message = PAD + (b * 8 + g) * 2 * PACK
            place(own_wide, message, left_ref, b * 24, at, False)
            place(own_wide, message + PACK, right_ref, base + core * 24, at, True)
            place(other_wide, message + PACK, right_ref, base + 24 - core * 24, at, True)
        return carry

    lax.fori_loop(0, 16, step, 0)
    for z in range(8):
        right_ref[128 * z + 96 : 128 * z + 128, :] = jnp.zeros((32, 1024), F32)
    left = left_ref[...].astype(BF16)
    for g in range(8):
        at = slice(128 * g, 128 * g + 128)
        tri_ref[g, 0:384, :] = matmul(left, right_ref[at, :].astype(BF16), ((1,), (1,)))

    def send(b, carry):
        for g in range(8):
            pack_tri(tri_ref.at[g], b * 24, mix_ref, (b * 8 + g) * PACK)
        return carry

    lax.fori_loop(0, 16, send, 0)
    narrow(mix_ref, out_ref)


def incoming_kernel(own_ref, other_ref, out_ref, own_wide, other_wide, left_ref, right_ref, tri_ref, mix_ref):
    core = lax.axis_index("core")
    widen(own_ref, own_wide)
    widen(other_ref, other_wide)

    def step(b, carry):
        for g in range(8):
            at = slice(128 * g, 128 * g + 128)
            message = PAD + (b * 8 + g) * 2 * PACK
            for start, wide_ref in ((0, own_wide), (384, other_wide)):
                place(wide_ref, message, left_ref, start + b * 24, at, False)
                place(wide_ref, message + PACK, right_ref, start + b * 24, at, False)
        return carry

    lax.fori_loop(0, 16, step, 0)
    right = right_ref[...].astype(BF16)
    for z in range(8):
        left = left_ref[:, 128 * z : 128 * z + 128].T.astype(BF16)
        tri = matmul(left, right, ((1,), (0,)))
        for g in range(8):
            tri_ref[z, g] = tri[:, 128 * g : 128 * g + 128]

    def send(b, carry):
        z = b // 2
        base = (b - 2 * z) * 48 + core * 24
        for g in range(8):
            pack_tri(tri_ref.at[z, g], base, mix_ref, (b * 8 + g) * PACK)
        return carry

    lax.fori_loop(0, 16, send, 0)
    narrow(mix_ref, out_ref)


def finish(tri_ref, state_ref, gate_ref, weight, scaled_ref, stat_ref, next_ref):
    def stats(i, carry):
        total, square = carry
        t = tri_ref[aligned(i * 144, 144, 144), :].astype(F32)
        first, second = t[0:72], t[72:144]
        return total + first + second, square + first * first + second * second

    zero = jnp.zeros((72, 128), F32)
    total, square = lax.fori_loop(0, 16, stats, (zero, zero))
    stat_ref[0, 0:72, :] = total
    stat_ref[1, 0:72, :] = square

    def gather(n):
        return sum(stat_ref[n, 18 * q : 18 * q + 18, :] for q in range(4)) * (1.0 / CH)

    average = gather(0)
    scale = lax.rsqrt(gather(1) - average * average + EPS)
    for q in range(4):
        stat_ref[0, 18 * q : 18 * q + 18, :] = average
        stat_ref[1, 18 * q : 18 * q + 18, :] = scale

    def rescale(i, carry):
        t = tri_ref[aligned(i * 144, 144, 144), :].astype(F32)
        for half in range(2):
            part = (t[72 * half : 72 * half + 72] - stat_ref[0, 0:72, :]) * stat_ref[1, 0:72, :]
            scaled_ref[aligned(i * 144 + 72 * half, 72, 72), :] = part
        return carry

    lax.fori_loop(0, 16, rescale, 0)
    w_hi, w_lo = split_bf16(weight.T)
    w_cat = jnp.concatenate([w_hi, w_lo, w_hi], axis=1)

    def combine(i, carry):
        pieces = [split_bf16(scaled_ref[pl.ds(2 * i + half, CH, stride=PACK), :]) for half in range(2)]
        high = jnp.concatenate([pieces[0][0], pieces[1][0]], axis=1)
        low = jnp.concatenate([pieces[0][1], pieces[1][1]], axis=1)
        values = matmul(w_cat, jnp.concatenate([high, high, low], axis=0), ((1,), (0,)))
        for half in range(2):
            t = 2 * i + half
            value = values[:, 128 * half : 128 * half + 128].T
            at = aligned(t * COLS, COLS, COLS)
            next_ref[at, :] = state_ref[at, :] + gate_ref[at, :] * value[:COLS]
            at = tail_pixels(t)
            next_ref[at, :] = state_ref[at, :] + gate_ref[at, :] * value[COLS:]
        return carry

    lax.fori_loop(0, PACK // 2, combine, 0, unroll=3)


def middle_kernel(edge_ref, tri_ref, state_ref, gate_ref, outw_ref, proj_ref, next_ref, send_ref,
                  norm_ref, mix_ref, scaled_ref, stat_ref):
    finish(tri_ref, state_ref, gate_ref, outw_ref[0], scaled_ref, stat_ref, next_ref)
    project(next_ref, proj_ref[1], edge_ref, norm_ref, mix_ref, send_ref)


def last_kernel(tri_ref, state_ref, gate_ref, outw_ref, next_ref, scaled_ref, stat_ref):
    finish(tri_ref, state_ref, gate_ref, outw_ref[1], scaled_ref, stat_ref, next_ref)


VM = pl.BlockSpec(memory_space=pltpu.VMEM)
SM = pl.BlockSpec(memory_space=pltpu.SMEM)
STATE = pltpu.VMEM((PIX, CH), F32)
SEND = pltpu.VMEM((CH * 2 * PACK, 128), BF16)
TRI = pltpu.VMEM((CH * PACK, 128), BF16)
EDGE = pltpu.VMEM((PACK, 128), F32)
PROJECT_SCRATCH = [pltpu.VMEM((PACK * 128, 384), BF16), pltpu.VMEM((CH * 2 * PACK, 128), F32)]
FINISH_SCRATCH = [pltpu.VMEM((CH * PACK, 128), F32), pltpu.VMEM((2, 72, 128), F32)]
WIDE = pltpu.VMEM((CH * 2 * PACK + 16, 128), F32)


PARAMS = pltpu.CompilerParams(vmem_limit_bytes=36 * 1024 * 1024)


def near(value):
    return pltpu.with_memory_space_constraint(value, pltpu.VMEM)


def exchange(message, rows):
    moved = lax.all_to_all(message.reshape(CH, rows // 2, 2, 128), CHIPS, split_axis=0, concat_axis=0, tiled=True)
    return moved.reshape(CH * rows, 128)


def triangle(kernel, message, scratch):
    own = exchange(message, 2 * PACK)
    other = lax.ppermute(own, "core", [(0, 1), (1, 0)])
    tri = pl.pallas_call(
        kernel, out_shape=TRI, compiler_params=PARAMS, in_specs=[VM, VM], out_specs=VM,
        scratch_shapes=[WIDE, WIDE] + scratch + [pltpu.VMEM((CH * PACK, 128), F32)],
    )(near(own), near(other))
    return exchange(tri, PACK)


def gating(layer, state, gate_weight):
    return pl.pallas_call(
        gate_kernel(layer), out_shape=STATE, compiler_params=PARAMS, in_specs=[VM, VM], out_specs=VM,
        cost_estimate=pl.CostEstimate(flops=3 * 2 * PIX * CH * CH, transcendentals=PIX * CH, bytes_accessed=8 * PIX * CH),
    )(near(state), near(gate_weight))


def on_device(pair, residue_mask, hotspot, interface, proj_weight, gate_weight, out_weight):
    state = pair.reshape(PIX, CH)
    send, edge = pl.pallas_call(
        first_kernel, out_shape=(SEND, EDGE), compiler_params=PARAMS, in_specs=[SM, SM, VM, VM, VM], out_specs=(VM, VM),
        scratch_shapes=[pltpu.VMEM((ROWS, 128), jnp.int32)] + PROJECT_SCRATCH,
    )(residue_mask, hotspot, interface, state, proj_weight)
    gate = gating(0, state, gate_weight)
    tri = triangle(
        outgoing_kernel, send,
        [pltpu.VMEM((384, 1024), F32), pltpu.VMEM((1024, 1024), F32), pltpu.VMEM((8, 392, 128), F32)],
    )
    state, send = pl.pallas_call(
        middle_kernel, out_shape=(STATE, SEND), compiler_params=PARAMS, in_specs=[VM] * 6, out_specs=(VM, VM),
        scratch_shapes=PROJECT_SCRATCH + FINISH_SCRATCH,
    )(near(edge), near(tri), near(state), near(gate), near(out_weight), near(proj_weight))
    gate = gating(1, state, gate_weight)
    tri = triangle(
        incoming_kernel, send,
        [pltpu.VMEM((768, 1024), F32), pltpu.VMEM((768, 1024), F32), pltpu.VMEM((8, 8, 128, 128), F32)],
    )
    state = pl.pallas_call(
        last_kernel, out_shape=jax.ShapeDtypeStruct((PIX, CH), F32), compiler_params=PARAMS, in_specs=[VM] * 4, out_specs=VM,
        scratch_shapes=FINISH_SCRATCH,
    )(near(tri), near(state), near(gate), near(out_weight))
    return state.reshape(ROWS, COLS, CH)


def solution(mesh):
    grid = Mesh(mesh.devices.reshape(8, 2, 2, 4, 2), ("z", "yl", "core", "x", "yh"))
    rows = ("z", "yl", "core")
    cols = ("x", "yh")
    return jax.shard_map(
        on_device,
        mesh=grid,
        in_specs=(P(rows, cols, None), P(), P(), P(rows, cols), P(), P(), P()),
        out_specs=P(rows, cols, None),
        check_vma=False,
    )
```

time: 446 us -> 185 us (0.41); the launches traced: 438 us -> 185 us
  waiting for transfers between devices: 166 us -> 43.1 us
  local copies, waits for them, and re-layouts: 88.9 us -> 8.23 us
  matrix products: 36 us -> 0 us
  Pallas kernels: 0 us -> 32.8 us
  blocking collectives: 103 us -> 87.4 us
  other arithmetic: 14.4 us -> 0 us
  between operations: 13.9 us -> 0.1 us
    all_gather x2 -> x0, waiting for transfers between devices: 139 us -> none  [the longest x1 93.5 us: outgoing(): lax.all_gather(right, 'band', axis=1, tiled=True)]
    dot_general x8 -> x0, matrix products: 36 us -> none  [the longest x1 8.91 us: outgoing(): lax.dot_general(left, lax.all_gather(right, 'band', axis=1, tiled=True),...]
    unnamed x40 -> x26, local copies, waits for them, and re-layouts: 43 us -> 8.23 us
    pallas_call x0 -> x7, Pallas kernels: none -> 32.8 us  [the longest x2 15.3 us: triangle(): pl.pallas_call(kernel, out_shape=TRI, compiler_params=PARAMS, in_specs=[V...]
    all_to_all x12 -> x0, local copies, waits for them, and re-layouts: 31.1 us -> none  [the longest x3 11.4 us: finish(): lax.all_to_all(tri, 'hid', split_axis=2, concat_axis=0, tiled=True)]
    all_to_all x5 -> x2, blocking collectives: 103 us -> 87.4 us  [exchange(): lax.all_to_all(message.reshape(CH, rows // 2, 2, 128), CHIPS, split_axis=...]
    dot_general x2 -> x0, local copies, waits for them, and re-layouts: 9.98 us -> none  [the longest x1 5 us: outgoing(): lax.dot_general(left, lax.all_gather(right, 'band', axis=1, tiled=True),...]
    all_to_all x2, waiting for transfers between devices: 27.6 us -> 37.4 us  [exchange(): lax.all_to_all(message.reshape(CH, rows // 2, 2, 128), CHIPS, split_axis=...]
  transfers between devices with their start and end apart: 4 -> 4, of which waited for: 4 -> 4; matrix products, arithmetic and copies ran while one was open for 6% -> 0% of each run, Pallas kernels for 0% -> 3%
where the time goes in v2:
time: 185 us
  blocking collectives  87.4 us (47%)
  waiting for transfers between devices  43.1 us (23%)
  Pallas kernels  32.8 us (18%)
  starting transfers between devices  13.3 us (7%)
  local copies, waits for them, and re-layouts  8.23 us (4%)
    all_to_all x2, blocking collectives, exchange(): lax.all_to_all(message.reshape(CH, rows // 2, 2, 128), CHIPS, split_axis=...  87.4 us
    all_to_all x2, waiting for transfers between devices, exchange(): lax.all_to_all(message.reshape(CH, rows // 2, 2, 128), CHIPS, split_axis=...  37.4 us
    pallas_call x2, Pallas kernels, triangle(): pl.pallas_call(kernel, out_shape=TRI, compiler_params=PARAMS, in_specs=[V...  15.3 us
    all_to_all x2, starting transfers between devices, exchange(): lax.all_to_all(message.reshape(CH, rows // 2, 2, 128), CHIPS, split_axis=...  13.3 us
    unnamed x26, local copies, waits for them, and re-layouts  8.23 us
    ppermute x2, waiting for transfers between devices, triangle(): other = lax.ppermute(own, 'core', [(0, 1), (1, 0)])  5.69 us
    pallas_call x1, Pallas kernels, on_device(): pl.pallas_call(middle_kernel, out_shape=(STATE, SEND), compiler_params=PA...  5.3 us
    pallas_call x2, Pallas kernels, gating(): pl.pallas_call(gate_kernel(layer), out_shape=STATE, compiler_params=PARAM...  4.99 us
  transfers between devices with their start and end apart: 4, of which 4 were waited for; matrix products, arithmetic and copies ran while one was open for 0% of the time, Pallas kernels for 3%

profile of v2, /device:TPU:6, one launch (start us, length us, event | category | flops | bytes accessed | tf_op | source)
XLA Modules:
  0.0 184.9 jit_solution(5285271120523014921)
XLA Ops:
  0.0 1.3 copy-done
  1.3 1.0 copy-done.4
  2.3 0.7 copy-done.10
  3.0 0.7 copy-done.11
  3.7 0.7 copy-done.12
  4.4 4.4 %shard_map.73 = (bf16[4608,128]{1,0:T(8,128)(2,1)S(1)}, f32[18,128]{1,0:T(8,128)S(1)}) custom-call(s32[768]{0:T(1024)S(1)} %copy-done.11, s32[768]{0:T(1024)S(1)} %copy-done.12, s32[24,96]{1,0:T(8,128)S(1)} %copy-done.10, f32[2304,128]{1,0:T(8,128)S(1)} %bitcast.10, f32[2,128,512]{2,1,0:T(8,128)S(1)} %copy-done.4), custom_call_target="tpu_custom_call" | custom-call | tf_op jit(solution)/shard_map/pallas_call | solution.py:351
  8.8 48.6 %all_to_all.20 = bf16[128,18,2,128]{3,2,1,0:T(2,128)(2,1)S(1)} all-to-all(bf16[128,18,2,128]{3,2,1,0:T(2,128)(2,1)S(1)} %bitcast.20), channel_id=1, replica_groups=mesh['z'=8,'yl'=2,'core'=2,'x'=4,'yh'=2] {'z','yl','x','yh'}, dimensions={0} | all-to-all | bytes 2359296 | tf_op jit(solution)/shard_map/all_to_all | solution.py:328
  57.4 2.8 %collective-permute-done.other_ref = bf16[4608,128]{1,0:T(8,128)(2,1)S(1)} collective-permute-done((bf16[4608,128]{1,0:T(8,128)(2,1)S(1)}, bf16[4608,128]{1,0:T(8,128)(2,1)S(1)}, u32[]{:S(2)}, u32[]{:S(2)}) %collective-permute-start) | collective-permute-done | bytes 1179680 | tf_op jit(solution)/shard_map/ppermute | solution.py:334
  60.3 7.4 %shard_map.74 = bf16[2304,128]{1,0:T(8,128)(2,1)} custom-call(bf16[4608,128]{1,0:T(8,128)(2,1)S(1)} %bitcast.14, bf16[4608,128]{1,0:T(8,128)(2,1)S(1)} %collective-permute-done.other_ref), custom_call_target="tpu_custom_call" | custom-call | tf_op jit(solution)/shard_map/pallas_call | solution.py:335
  67.7 6.6 %all-to-all-start.1 = ((bf16[128,9,2,128]{3,2,1,0:T(2,128)(2,1)}), bf16[128,9,2,128]{3,2,1,0:T(2,128)(2,1)S(1)}, u32[]{:S(2)}, u32[]{:S(2)}) async-start(bf16[128,9,2,128]{3,2,1,0:T(2,128)(2,1)} %bitcast.3), calls=%async_computation.1 | async-start | bytes 1179648 | tf_op jit(solution)/shard_map/all_to_all | solution.py:328
  74.3 2.5 %shard_map.75.gate_ref = f32[2304,128]{1,0:T(8,128)S(1)} custom-call(f32[2304,128]{1,0:T(8,128)S(1)} %bitcast.11, f32[2,128,128]{2,1,0:T(8,128)S(1)} %copy-done.6), custom_call_target="tpu_custom_call" | custom-call | flops 226492416 | bytes 2359296 | tf_op jit(solution)/shard_map/pallas_call | solution.py:343
  76.8 18.7 %all-to-all-done.1 = bf16[128,9,2,128]{3,2,1,0:T(2,128)(2,1)S(1)} async-done(((bf16[128,9,2,128]{3,2,1,0:T(2,128)(2,1)}), bf16[128,9,2,128]{3,2,1,0:T(2,128)(2,1)S(1)}, u32[]{:S(2)}, u32[]{:S(2)}) %all-to-all-start.1) | async-done | bytes 589856 | tf_op jit(solution)/shard_map/all_to_all | solution.py:328
  95.5 0.8 copy-done.2
  96.3 1.1 copy-done.3
  97.4 1.0 copy-done.5
  98.4 0.9 copy-done.8
  99.3 5.3 %shard_map.76 = (f32[2304,128]{1,0:T(8,128)S(1)}, bf16[4608,128]{1,0:T(8,128)(2,1)S(1)}) custom-call(f32[18,128]{1,0:T(8,128)S(1)} %get-tuple-element.9.edge_ref, bf16[2304,128]{1,0:T(8,128)(2,1)S(1)} %bitcast.17, f32[2304,128]{1,0:T(8,128)S(1)} %bitcast.12, f32[2304,128]{1,0:T(8,128)S(1)} %shard_map.75.gate_ref, f32[2,128,128]{2,1,0:T(8,128)S(1)} %copy-done.8, ...), custom_call_target="tpu_custom_call" | custom-call | tf_op jit(solution)/shard_map/pallas_call | solution.py:360
  104.6 38.9 %all_to_all.21 = bf16[128,18,2,128]{3,2,1,0:T(2,128)(2,1)S(1)} all-to-all(bf16[128,18,2,128]{3,2,1,0:T(2,128)(2,1)S(1)} %bitcast.19), channel_id=1, replica_groups=mesh['z'=8,'yl'=2,'core'=2,'x'=4,'yh'=2] {'z','yl','x','yh'}, dimensions={0} | all-to-all | bytes 2359296 | tf_op jit(solution)/shard_map/all_to_all | solution.py:328
  143.5 2.8 %collective-permute-done.1.other_ref = bf16[4608,128]{1,0:T(8,128)(2,1)S(1)} collective-permute-done((bf16[4608,128]{1,0:T(8,128)(2,1)S(1)}, bf16[4608,128]{1,0:T(8,128)(2,1)S(1)}, u32[]{:S(2)}, u32[]{:S(2)}) %collective-permute-start.1) | collective-permute-done | bytes 1179680 | tf_op jit(solution)/shard_map/ppermute | solution.py:334
  146.3 7.9 %shard_map.77 = bf16[2304,128]{1,0:T(8,128)(2,1)} custom-call(bf16[4608,128]{1,0:T(8,128)(2,1)S(1)} %bitcast.16, bf16[4608,128]{1,0:T(8,128)(2,1)S(1)} %collective-permute-done.1.other_ref), custom_call_target="tpu_custom_call" | custom-call | tf_op jit(solution)/shard_map/pallas_call | solution.py:335
  154.2 6.7 %all-to-all-start.3 = ((bf16[128,9,2,128]{3,2,1,0:T(2,128)(2,1)}), bf16[128,9,2,128]{3,2,1,0:T(2,128)(2,1)S(1)}, u32[]{:S(2)}, u32[]{:S(2)}) async-start(bf16[128,9,2,128]{3,2,1,0:T(2,128)(2,1)} %bitcast.7), calls=%async_computation.3 | async-start | bytes 1179648 | tf_op jit(solution)/shard_map/all_to_all | solution.py:328
  160.9 2.5 %shard_map.78.gate_ref = f32[2304,128]{1,0:T(8,128)S(1)} custom-call(f32[2304,128]{1,0:T(8,128)S(1)} %get-tuple-element.12.state_ref, f32[2,128,128]{2,1,0:T(8,128)S(1)} %copy-done.7), custom_call_target="tpu_custom_call" | custom-call | flops 226492416 | bytes 2359296 | tf_op jit(solution)/shard_map/pallas_call | solution.py:343
  163.4 18.7 %all-to-all-done.3 = bf16[128,9,2,128]{3,2,1,0:T(2,128)(2,1)S(1)} async-done(((bf16[128,9,2,128]{3,2,1,0:T(2,128)(2,1)}), bf16[128,9,2,128]{3,2,1,0:T(2,128)(2,1)S(1)}, u32[]{:S(2)}, u32[]{:S(2)}) %all-to-all-start.3) | async-done | bytes 589856 | tf_op jit(solution)/shard_map/all_to_all | solution.py:328
  182.1 2.7 %shard_map.79 = f32[2304,128]{1,0:T(8,128)} custom-call(bf16[2304,128]{1,0:T(8,128)(2,1)S(1)} %bitcast.18, f32[2304,128]{1,0:T(8,128)S(1)} %get-tuple-element.12.state_ref, f32[2304,128]{1,0:T(8,128)S(1)} %shard_map.78.gate_ref, f32[2,128,128]{2,1,0:T(8,128)S(1)} %copy-done.9), custom_call_target="tpu_custom_call" | custom-call | tf_op jit(solution)/shard_map/pallas_call | solution.py:369
  (19 shorter events, 0.0 us)
Async XLA Ops:
  0.0 1.3 copy-start
  1.3 1.0 copy-start.4
  2.3 0.7 copy-start.10
  3.0 0.7 copy-start.11
  3.7 0.7 copy-start.12
  57.4 2.8 %collective-permute-start = (bf16[4608,128]{1,0:T(8,128)(2,1)S(1)}, bf16[4608,128]{1,0:T(8,128)(2,1)S(1)}, u32[]{:S(2)}, u32[]{:S(2)}) collective-permute-start(bf16[4608,128]{1,0:T(8,128)(2,1)S(1)} %bitcast.13), channel_id=1, source_target_pairs={{0,8},{8,0},{1,9},{9,1},{2,10},{10,2},{3,11},{11,3},{4,12},{12,4},... | collective-permute-start | bytes 3538952 | tf_op jit(solution)/shard_map/ppermute | solution.py:334
  60.3 14.0 %copy-start.6 = (f32[2,128,128]{2,1,0:T(8,128)S(1)}, f32[2,128,128]{2,1,0:T(8,128)}, u32[]{:S(2)}) copy-start(f32[2,128,128]{2,1,0:T(8,128)} %gatew_ref.3) | copy-start | bytes 393220
  67.7 6.6 %copy-start.1 = (f32[24,96,128]{2,1,0:T(8,128)S(1)}, f32[24,96,128]{2,1,0:T(8,128)}, u32[]{:S(2)}) copy-start(f32[24,96,128]{2,1,0:T(8,128)} %param.7) | copy-start | bytes 3538948
  67.7 27.8 %all-to-all-start.1 = ((bf16[128,9,2,128]{3,2,1,0:T(2,128)(2,1)}), bf16[128,9,2,128]{3,2,1,0:T(2,128)(2,1)S(1)}, u32[]{:S(2)}, u32[]{:S(2)}) async-start(bf16[128,9,2,128]{3,2,1,0:T(2,128)(2,1)} %bitcast.3), calls=%async_computation.1 | async-start | bytes 1179648 | tf_op jit(solution)/shard_map/all_to_all | solution.py:328
  95.5 0.8 copy-start.2
  96.3 1.1 copy-start.3
  97.4 1.0 copy-start.5
  98.4 0.9 copy-start.8
  143.5 2.8 %collective-permute-start.1 = (bf16[4608,128]{1,0:T(8,128)(2,1)S(1)}, bf16[4608,128]{1,0:T(8,128)(2,1)S(1)}, u32[]{:S(2)}, u32[]{:S(2)}) collective-permute-start(bf16[4608,128]{1,0:T(8,128)(2,1)S(1)} %bitcast.15), channel_id=1, source_target_pairs={{0,8},{8,0},{1,9},{9,1},{2,10},{10,2},{3,11},{11,3},{4,12},{12,4},... | collective-permute-start | bytes 3538952 | tf_op jit(solution)/shard_map/ppermute | solution.py:334
  154.2 6.7 %copy-start.7 = (f32[2,128,128]{2,1,0:T(8,128)S(1)}, f32[2,128,128]{2,1,0:T(8,128)}, u32[]{:S(2)}) copy-start(f32[2,128,128]{2,1,0:T(8,128)} %gatew_ref.3) | copy-start | bytes 393220
  154.2 27.9 %all-to-all-start.3 = ((bf16[128,9,2,128]{3,2,1,0:T(2,128)(2,1)}), bf16[128,9,2,128]{3,2,1,0:T(2,128)(2,1)S(1)}, u32[]{:S(2)}, u32[]{:S(2)}) async-start(bf16[128,9,2,128]{3,2,1,0:T(2,128)(2,1)} %bitcast.7), calls=%async_computation.3 | async-start | bytes 1179648 | tf_op jit(solution)/shard_map/all_to_all | solution.py:328
  160.9 21.2 %copy-start.9 = (f32[2,128,128]{2,1,0:T(8,128)S(1)}, f32[2,128,128]{2,1,0:T(8,128)}, u32[]{:S(2)}) copy-start(f32[2,128,128]{2,1,0:T(8,128)} %outw_ref.3) | copy-start | bytes 393220

commit v3 on v2

--- a/solution.py
+++ b/solution.py
@@ -28,6 +28,11 @@
 
 def matmul(a, b, dims):
     return lax.dot_general(a, b, (dims, ((), ())), preferred_element_type=F32)
+
+
+def stacked(weight, axis):
+    high, low = split_bf16(weight)
+    return jnp.concatenate([high, low, high], axis=axis)
 
 
 def aligned(start, size, unit):
@@ -58,7 +63,7 @@
     return aligned((18 + t % 6) * COLS + 32 * (t // 6), 32, 32)
 
 
-def project(state_ref, weight, edge_ref, norm_ref, mix_ref, send_ref):
+def project(state_ref, w_cat, edge_ref, norm_ref, mix_ref, send_ref):
     def normalize(t, carry):
         x = jnp.concatenate([state_ref[aligned(t * COLS, COLS, COLS), :], state_ref[tail_pixels(t), :]], axis=0)
         centred = x - jnp.mean(x, axis=-1, keepdims=True)
@@ -71,9 +76,6 @@
         return carry
 
     lax.fori_loop(0, PACK, normalize, 0, unroll=3)
-    w_hi, w_lo = split_bf16(weight.T)
-    w_cat = jnp.concatenate([w_hi, w_lo, w_hi], axis=1)
-
     def pair(i, carry):
         values = matmul(w_cat, norm_ref[aligned(i * 256, 256, 256), :], ((1,), (1,)))
         for half in range(2):
@@ -96,15 +98,28 @@
     lax.fori_loop(0, 18, convert, 0)
 
 
-def first_kernel(mask_sm, hot_sm, inter_ref, state_ref, proj_ref, send_ref, edge_ref, rows_ref, norm_ref, mix_ref):
+def first_kernel(mask_sm, hot_sm, inter_ref, state_hbm, proj_hbm, send_ref, edge_ref,
+                 rows_ref, state_ref, proj_ref, sems, norm_ref, mix_ref):
+    state_copy = pltpu.make_async_copy(state_hbm, state_ref, sems.at[0])
+    proj_copy = pltpu.make_async_copy(proj_hbm.at[0], proj_ref, sems.at[1])
+    state_copy.start()
+    proj_copy.start()
     packed_edge(mask_sm, hot_sm, inter_ref, edge_ref, rows_ref)
-    project(state_ref, proj_ref[0], edge_ref, norm_ref, mix_ref, send_ref)
+    proj_copy.wait()
+    w_cat = stacked(proj_ref[...].T, 1)
+    state_copy.wait()
+    project(state_ref, w_cat, edge_ref, norm_ref, mix_ref, send_ref)
 
 
 def gate_kernel(layer):
-    def body(state_ref, gatew_ref, gate_ref):
-        hi, lo = split_bf16(gatew_ref[layer])
-        cat = jnp.concatenate([hi, lo, hi], axis=0)
+    def body(state_ref, gatew_ref, outw_ref, *refs):
+        if layer == 0:
+            proj_ref, gate_ref, outcat_ref, projcat_ref = refs
+            projcat_ref[...] = stacked(proj_ref[1].T, 1)
+        else:
+            gate_ref, outcat_ref = refs
+        outcat_ref[...] = stacked(outw_ref[layer].T, 1)
+        cat = stacked(gatew_ref[layer], 0)
 
         def step(i, carry):
             at = aligned(i * 128, 128, 128)
@@ -181,73 +196,92 @@
     lax.fori_loop(0, 9, step, 0)
 
 
-def outgoing_kernel(own_ref, other_ref, out_ref, own_wide, other_wide, left_ref, right_ref, tri_ref, mix_ref):
+def outgoing_own(own_ref, left_ref, right_ref, wide_ref, keep_ref):
     core = lax.axis_index("core")
-    widen(own_ref, own_wide)
-    widen(other_ref, other_wide)
+    widen(own_ref, wide_ref)
 
     def step(b, carry):
-        z = b // 2
-        base = z * 128 + (b - 2 * z) * 48
+        start = (b // 2) * 128 + (b % 2) * 48 + core * 24
         for g in range(8):
             at = slice(128 * g, 128 * g + 128)
             message = PAD + (b * 8 + g) * 2 * PACK
-            place(own_wide, message, left_ref, b * 24, at, False)
-            place(own_wide, message + PACK, right_ref, base + core * 24, at, True)
-            place(other_wide, message + PACK, right_ref, base + 24 - core * 24, at, True)
-        return carry
-
-    lax.fori_loop(0, 16, step, 0)
+            place(wide_ref, message, keep_ref, b * 24, at, False)
+            place(wide_ref, message + PACK, right_ref, start, at, True)
+        return carry
+
+    lax.fori_loop(0, 16, step, 0, unroll=2)
     for z in range(8):
         right_ref[128 * z + 96 : 128 * z + 128, :] = jnp.zeros((32, 1024), F32)
-    left = left_ref[...].astype(BF16)
-    for g in range(8):
-        at = slice(128 * g, 128 * g + 128)
-        tri_ref[g, 0:384, :] = matmul(left, right_ref[at, :].astype(BF16), ((1,), (1,)))
-
+    left_ref[...] = keep_ref[...].astype(BF16)
+
+
+def send_tri(tri_ref, mix_ref, out_ref):
     def send(b, carry):
         for g in range(8):
             pack_tri(tri_ref.at[g], b * 24, mix_ref, (b * 8 + g) * PACK)
         return carry
 
-    lax.fori_loop(0, 16, send, 0)
+    lax.fori_loop(0, 16, send, 0, unroll=2)
     narrow(mix_ref, out_ref)
 
 
-def incoming_kernel(own_ref, other_ref, out_ref, own_wide, other_wide, left_ref, right_ref, tri_ref, mix_ref):
+def outgoing_kernel(left_ref, _, other_ref, out_ref, right_ref, wide_ref, tri_ref, mix_ref):
     core = lax.axis_index("core")
-    widen(own_ref, own_wide)
-    widen(other_ref, other_wide)
+    widen(other_ref, wide_ref)
+
+    def step(b, carry):
+        start = (b // 2) * 128 + (b % 2) * 48 + 24 - core * 24
+        for g in range(8):
+            message = PAD + (b * 8 + g) * 2 * PACK
+            place(wide_ref, message + PACK, right_ref, start, slice(128 * g, 128 * g + 128), True)
+        return carry
+
+    lax.fori_loop(0, 16, step, 0, unroll=2)
+    left = left_ref[...]
+    for n in range(4):
+        tri = matmul(left, right_ref[256 * n : 256 * n + 256, :].astype(BF16), ((1,), (1,)))
+        tri_ref[2 * n, 0:384, :] = tri[:, 0:128]
+        tri_ref[2 * n + 1, 0:384, :] = tri[:, 128:256]
+    send_tri(tri_ref, mix_ref, out_ref)
+
+
+def incoming_half(source_ref, wide_ref, left_ref, right_ref, turn_ref, turned_ref):
+    core = lax.axis_index("core")
+    widen(source_ref, wide_ref)
 
     def step(b, carry):
         for g in range(8):
             at = slice(128 * g, 128 * g + 128)
             message = PAD + (b * 8 + g) * 2 * PACK
-            for start, wide_ref in ((0, own_wide), (384, other_wide)):
-                place(wide_ref, message, left_ref, start + b * 24, at, False)
-                place(wide_ref, message + PACK, right_ref, start + b * 24, at, False)
-        return carry
-
-    lax.fori_loop(0, 16, step, 0)
-    right = right_ref[...].astype(BF16)
+            place(wide_ref, message, left_ref, b * 24, at, False)
+            place(wide_ref, message + PACK, right_ref, b * 24, at, False)
+        return carry
+
+    lax.fori_loop(0, 16, step, 0, unroll=2)
     for z in range(8):
-        left = left_ref[:, 128 * z : 128 * z + 128].T.astype(BF16)
-        tri = matmul(left, right, ((1,), (0,)))
-        for g in range(8):
-            tri_ref[z, g] = tri[:, 128 * g : 128 * g + 128]
-
-    def send(b, carry):
-        z = b // 2
-        base = (b - 2 * z) * 48 + core * 24
-        for g in range(8):
-            pack_tri(tri_ref.at[z, g], base, mix_ref, (b * 8 + g) * PACK)
-        return carry
-
-    lax.fori_loop(0, 16, send, 0)
-    narrow(mix_ref, out_ref)
-
-
-def finish(tri_ref, state_ref, gate_ref, weight, scaled_ref, stat_ref, next_ref):
+        turn_ref[z % 2] = left_ref[:, 128 * z : 128 * z + 128].T
+        for y in range(2):
+            rows = slice(48 * z + 24 * y, 48 * z + 24 * y + 24)
+            turned_ref[rows, :] = turn_ref[z % 2, aligned(48 * y + 24 * core, 24, 8), :]
+    left = turned_ref[...].astype(BF16)
+    for n in range(4):
+        tri = matmul(left, right_ref[:, 256 * n : 256 * n + 256].astype(BF16), ((1,), (0,)))
+        yield 2 * n, tri[:, 0:128]
+        yield 2 * n + 1, tri[:, 128:256]
+
+
+def incoming_own(own_ref, part_ref, *scratch):
+    for g, tri in incoming_half(own_ref, *scratch):
+        part_ref[g] = tri
+
+
+def incoming_kernel(part_ref, other_ref, out_ref, wide_ref, left_ref, right_ref, turn_ref, turned_ref, tri_ref, mix_ref):
+    for g, tri in incoming_half(other_ref, wide_ref, left_ref, right_ref, turn_ref, turned_ref):
+        tri_ref[g, 0:384, :] = part_ref[g] + tri
+    send_tri(tri_ref, mix_ref, out_ref)
+
+
+def finish(tri_ref, state_ref, gate_ref, w_cat, scaled_ref, stat_ref, next_ref):
     def stats(i, carry):
         total, square = carry
         t = tri_ref[aligned(i * 144, 144, 144), :].astype(F32)
@@ -276,9 +310,6 @@
         return carry
 
     lax.fori_loop(0, 16, rescale, 0)
-    w_hi, w_lo = split_bf16(weight.T)
-    w_cat = jnp.concatenate([w_hi, w_lo, w_hi], axis=1)
-
     def combine(i, carry):
         pieces = [split_bf16(scaled_ref[pl.ds(2 * i + half, CH, stride=PACK), :]) for half in range(2)]
         high = jnp.concatenate([pieces[0][0], pieces[1][0]], axis=1)
@@ -296,32 +327,54 @@
     lax.fori_loop(0, PACK // 2, combine, 0, unroll=3)
 
 
-def middle_kernel(edge_ref, tri_ref, state_ref, gate_ref, outw_ref, proj_ref, next_ref, send_ref,
+def middle_kernel(edge_ref, tri_ref, state_ref, gate_ref, outcat_ref, projcat_ref, next_ref, send_ref,
                   norm_ref, mix_ref, scaled_ref, stat_ref):
-    finish(tri_ref, state_ref, gate_ref, outw_ref[0], scaled_ref, stat_ref, next_ref)
-    project(next_ref, proj_ref[1], edge_ref, norm_ref, mix_ref, send_ref)
-
-
-def last_kernel(tri_ref, state_ref, gate_ref, outw_ref, next_ref, scaled_ref, stat_ref):
-    finish(tri_ref, state_ref, gate_ref, outw_ref[1], scaled_ref, stat_ref, next_ref)
+    finish(tri_ref, state_ref, gate_ref, outcat_ref[...], scaled_ref, stat_ref, next_ref)
+    project(next_ref, projcat_ref[...], edge_ref, norm_ref, mix_ref, send_ref)
+
+
+def last_kernel(tri_ref, state_ref, gate_ref, outcat_ref, next_ref, scaled_ref, stat_ref):
+    finish(tri_ref, state_ref, gate_ref, outcat_ref[...], scaled_ref, stat_ref, next_ref)
 
 
 VM = pl.BlockSpec(memory_space=pltpu.VMEM)
 SM = pl.BlockSpec(memory_space=pltpu.SMEM)
+HB = pl.BlockSpec(memory_space=pltpu.HBM)
 STATE = pltpu.VMEM((PIX, CH), F32)
 SEND = pltpu.VMEM((CH * 2 * PACK, 128), BF16)
 TRI = pltpu.VMEM((CH * PACK, 128), BF16)
 EDGE = pltpu.VMEM((PACK, 128), F32)
+OUTCAT = pltpu.VMEM((CH, 3 * CH), BF16)
+PROJCAT = pltpu.VMEM((4 * CH, 3 * CH), BF16)
 PROJECT_SCRATCH = [pltpu.VMEM((PACK * 128, 384), BF16), pltpu.VMEM((CH * 2 * PACK, 128), F32)]
 FINISH_SCRATCH = [pltpu.VMEM((CH * PACK, 128), F32), pltpu.VMEM((2, 72, 128), F32)]
+SEND_SCRATCH = [pltpu.VMEM((8, 392, 128), F32), pltpu.VMEM((CH * PACK, 128), F32)]
 WIDE = pltpu.VMEM((CH * 2 * PACK + 16, 128), F32)
-
-
-PARAMS = pltpu.CompilerParams(vmem_limit_bytes=36 * 1024 * 1024)
+HALF = pltpu.VMEM((384, 1024), F32)
+RIGHT = pltpu.VMEM((1024, 1024), F32)
+HALF_SCRATCH = [WIDE, HALF, HALF, pltpu.VMEM((2, 128, 384), F32), pltpu.VMEM((384, 384), F32)]
+PART = pltpu.VMEM((8, 384, 128), F32)
+
+
+def call(kernel, out_shape, operands, scratch=(), specs=None, mib=16, **options):
+    outs = out_shape if isinstance(out_shape, tuple) else None
+    return pl.pallas_call(
+        kernel,
+        out_shape=out_shape,
+        in_specs=specs or [VM] * len(operands),
+        out_specs=VM if outs is None else (VM,) * len(outs),
+        scratch_shapes=list(scratch),
+        compiler_params=pltpu.CompilerParams(vmem_limit_bytes=mib * 1024 * 1024),
+        **options,
+    )(*operands)
 
 
 def near(value):
     return pltpu.with_memory_space_constraint(value, pltpu.VMEM)
+
+
+def far(value):
+    return pltpu.with_memory_space_constraint(value, pltpu.HBM)
 
 
 def exchange(message, rows):
@@ -329,47 +382,47 @@
     return moved.reshape(CH * rows, 128)
 
 
-def triangle(kernel, message, scratch):
-    own = exchange(message, 2 * PACK)
-    other = lax.ppermute(own, "core", [(0, 1), (1, 0)])
-    tri = pl.pallas_call(
-        kernel, out_shape=TRI, compiler_params=PARAMS, in_specs=[VM, VM], out_specs=VM,
-        scratch_shapes=[WIDE, WIDE] + scratch + [pltpu.VMEM((CH * PACK, 128), F32)],
-    )(near(own), near(other))
-    return exchange(tri, PACK)
-
-
-def gating(layer, state, gate_weight):
-    return pl.pallas_call(
-        gate_kernel(layer), out_shape=STATE, compiler_params=PARAMS, in_specs=[VM, VM], out_specs=VM,
-        cost_estimate=pl.CostEstimate(flops=3 * 2 * PIX * CH * CH, transcendentals=PIX * CH, bytes_accessed=8 * PIX * CH),
-    )(near(state), near(gate_weight))
+def partner(value):
+    return lax.ppermute(value, "core", [(0, 1), (1, 0)])
+
+
+def gating(layer, outs, *operands):
+    cost = pl.CostEstimate(flops=3 * 2 * PIX * CH * CH, transcendentals=PIX * CH, bytes_accessed=8 * PIX * CH)
+    return call(gate_kernel(layer), outs, operands, cost_estimate=cost)
 
 
 def on_device(pair, residue_mask, hotspot, interface, proj_weight, gate_weight, out_weight):
     state = pair.reshape(PIX, CH)
-    send, edge = pl.pallas_call(
-        first_kernel, out_shape=(SEND, EDGE), compiler_params=PARAMS, in_specs=[SM, SM, VM, VM, VM], out_specs=(VM, VM),
-        scratch_shapes=[pltpu.VMEM((ROWS, 128), jnp.int32)] + PROJECT_SCRATCH,
-    )(residue_mask, hotspot, interface, state, proj_weight)
-    gate = gating(0, state, gate_weight)
-    tri = triangle(
-        outgoing_kernel, send,
-        [pltpu.VMEM((384, 1024), F32), pltpu.VMEM((1024, 1024), F32), pltpu.VMEM((8, 392, 128), F32)],
-    )
-    state, send = pl.pallas_call(
-        middle_kernel, out_shape=(STATE, SEND), compiler_params=PARAMS, in_specs=[VM] * 6, out_specs=(VM, VM),
-        scratch_shapes=PROJECT_SCRATCH + FINISH_SCRATCH,
-    )(near(edge), near(tri), near(state), near(gate), near(out_weight), near(proj_weight))
-    gate = gating(1, state, gate_weight)
-    tri = triangle(
-        incoming_kernel, send,
-        [pltpu.VMEM((768, 1024), F32), pltpu.VMEM((768, 1024), F32), pltpu.VMEM((8, 8, 128, 128), F32)],
-    )
-    state = pl.pallas_call(
-        last_kernel, out_shape=jax.ShapeDtypeStruct((PIX, CH), F32), compiler_params=PARAMS, in_specs=[VM] * 4, out_specs=VM,
-        scratch_shapes=FINISH_SCRATCH,
-    )(near(tri), near(state), near(gate), near(out_weight))
+    send, edge = call(
+        first_kernel, (SEND, EDGE),
+        (residue_mask, hotspot, far(interface), far(state), far(proj_weight)),
+        [pltpu.VMEM((ROWS, 128), jnp.int32), pltpu.VMEM((PIX, CH), F32), pltpu.VMEM((CH, 4 * CH), F32),
+         pltpu.SemaphoreType.DMA((2,))] + PROJECT_SCRATCH,
+        [SM, SM, VM, HB, HB],
+    )
+    own = exchange(send, 2 * PACK)
+    other = partner(own)
+    left, right = call(outgoing_own, (pltpu.VMEM((384, 1024), BF16), RIGHT), (near(own),), [WIDE, HALF])
+    tri, _ = call(
+        outgoing_kernel, (TRI, RIGHT), (near(left), near(right), near(other)), [WIDE] + SEND_SCRATCH,
+        input_output_aliases={1: 1},
+    )
+    tri = exchange(tri, PACK)
+    gate, outcat, projcat = gating(0, (STATE, OUTCAT, PROJCAT), near(state), gate_weight, out_weight, proj_weight)
+    state, send = call(
+        middle_kernel, (STATE, SEND),
+        (near(edge), near(tri), near(state), near(gate), near(outcat), near(projcat)), PROJECT_SCRATCH + FINISH_SCRATCH,
+    )
+    own = exchange(send, 2 * PACK)
+    other = partner(own)
+    part = call(incoming_own, PART, (near(own),), HALF_SCRATCH)
+    tri = call(incoming_kernel, TRI, (near(part), near(other)), HALF_SCRATCH + SEND_SCRATCH)
+    tri = exchange(tri, PACK)
+    gate, outcat = gating(1, (STATE, OUTCAT), near(state), gate_weight, out_weight)
+    state = call(
+        last_kernel, jax.ShapeDtypeStruct((PIX, CH), F32), (near(tri), near(state), near(gate), near(outcat)),
+        FINISH_SCRATCH,
+    )
     return state.reshape(ROWS, COLS, CH)
 
 

time: 185 us -> 174 us (0.941)
  waiting for transfers between devices: 43.1 us -> 37.6 us
  local copies, waits for them, and re-layouts: 8.23 us -> 3.68 us
    unnamed x26 -> x20, local copies, waits for them, and re-layouts: 8.23 us -> 3.68 us
    ppermute x2, waiting for transfers between devices: 5.69 us -> 1.49 us  [partner(): return lax.ppermute(value, 'core', [(0, 1), (1, 0)])]
    pallas_call x7 -> x9, Pallas kernels: 32.8 us -> 31.9 us  [call(): pl.pallas_call(kernel, out_shape=out_shape, in_specs=specs or [VM] * len(...]
  transfers between devices with their start and end apart: 4 -> 4, of which waited for: 4 -> 4; matrix products, arithmetic and copies ran while one was open for 0% -> 0% of each run, Pallas kernels for 3% -> 5%
where the time goes in v3:
time: 174 us
  blocking collectives  87.4 us (50%)
  waiting for transfers between devices  37.6 us (22%)
  Pallas kernels  31.9 us (18%)
  starting transfers between devices  13.3 us (8%)
  local copies, waits for them, and re-layouts  3.68 us (2%)
    all_to_all x2, blocking collectives, exchange(): lax.all_to_all(message.reshape(CH, rows // 2, 2, 128), CHIPS, split_axis=...  87.4 us
    all_to_all x2, waiting for transfers between devices, exchange(): lax.all_to_all(message.reshape(CH, rows // 2, 2, 128), CHIPS, split_axis=...  36.1 us
    pallas_call x9, Pallas kernels, call(): pl.pallas_call(kernel, out_shape=out_shape, in_specs=specs or [VM] * len(...  31.9 us
    all_to_all x2, starting transfers between devices, exchange(): lax.all_to_all(message.reshape(CH, rows // 2, 2, 128), CHIPS, split_axis=...  13.3 us
    unnamed x20, local copies, waits for them, and re-layouts  3.68 us
  transfers between devices with their start and end apart: 4, of which 4 were waited for; matrix products, arithmetic and copies ran while one was open for 0% of the time, Pallas kernels for 5%

profile of v3, /device:TPU:6, one launch (start us, length us, event | category | flops | bytes accessed | tf_op | source)
XLA Modules:
  0.0 174.0 jit_solution(7357354004079858756)
XLA Ops:
  0.0 0.7 copy-done.8
  0.7 0.7 copy-done.9
  1.4 5.8 %shard_map.73 = (bf16[4608,128]{1,0:T(8,128)(2,1)S(1)}, f32[18,128]{1,0:T(8,128)S(1)}) custom-call(s32[768]{0:T(1024)S(1)} %copy-done.8, s32[768]{0:T(1024)S(1)} %copy-done.9, s32[24,96]{1,0:T(8,128)} %inter_ref.1, f32[2304,128]{1,0:T(8,128)} %bitcast.10, f32[2,128,512]{2,1,0:T(8,128)} %refs_0_.1), custom_call_target="tpu_custom_call" | custom-call | tf_op jit(solution)/shard_map/pallas_call | solution.py:361
  7.1 48.6 %all_to_all.20 = bf16[128,18,2,128]{3,2,1,0:T(2,128)(2,1)S(1)} all-to-all(bf16[128,18,2,128]{3,2,1,0:T(2,128)(2,1)S(1)} %bitcast.20), channel_id=1, replica_groups=mesh['z'=8,'yl'=2,'core'=2,'x'=4,'yh'=2] {'z','yl','x','yh'}, dimensions={0} | all-to-all | bytes 2359296 | tf_op jit(solution)/shard_map/all_to_all | solution.py:381
  55.7 0.0 collective-permute-start
  55.7 1.7 shard_map.74
  57.5 1.1 collective-permute-done.other_ref
  58.6 4.4 %shard_map.75 = (bf16[2304,128]{1,0:T(8,128)(2,1)}, f32[1024,1024]{1,0:T(8,128)S(1)}) custom-call(bf16[384,1024]{1,0:T(8,128)(2,1)S(1)} %get-tuple-element.19.left_ref, f32[1024,1024]{1,0:T(8,128)S(1)} %get-tuple-element.20._, bf16[4608,128]{1,0:T(8,128)(2,1)S(1)} %collective-permute-done.other_ref), custom_call_target="tpu_custom_call", output_to_operand_aliasing={{1}: (1, {})} | custom-call | tf_op jit(solution)/shard_map/pallas_call | solution.py:361
  62.9 6.6 %all-to-all-start.1 = ((bf16[128,9,2,128]{3,2,1,0:T(2,128)(2,1)}), bf16[128,9,2,128]{3,2,1,0:T(2,128)(2,1)S(1)}, u32[]{:S(2)}, u32[]{:S(2)}) async-start(bf16[128,9,2,128]{3,2,1,0:T(2,128)(2,1)} %bitcast.3), calls=%async_computation.1 | async-start | bytes 1179648 | tf_op jit(solution)/shard_map/all_to_all | solution.py:381
  69.6 2.6 %shard_map.76 = (f32[2304,128]{1,0:T(8,128)S(1)}, bf16[128,384]{1,0:T(8,128)(2,1)S(1)}, bf16[512,384]{1,0:T(8,128)(2,1)S(1)}) custom-call(f32[2304,128]{1,0:T(8,128)S(1)} %bitcast.11, f32[2,128,128]{2,1,0:T(8,128)S(1)} %copy-done.4, f32[2,128,128]{2,1,0:T(8,128)S(1)} %copy-done.6, f32[2,128,512]{2,1,0:T(8,128)S(1)} %copy-done.1), custom_call_target="tpu_custom_call" | custom-call | flops 226492416 | bytes 2359296 | tf_op jit(solution)/shard_map/pallas_call | solution.py:361
  72.2 0.0 copy-start.2
  72.3 1.0 copy-done.2
  73.3 17.5 %all-to-all-done.1 = bf16[128,9,2,128]{3,2,1,0:T(2,128)(2,1)S(1)} async-done(((bf16[128,9,2,128]{3,2,1,0:T(2,128)(2,1)}), bf16[128,9,2,128]{3,2,1,0:T(2,128)(2,1)S(1)}, u32[]{:S(2)}, u32[]{:S(2)}) %all-to-all-start.1) | async-done | bytes 589856 | tf_op jit(solution)/shard_map/all_to_all | solution.py:381
  90.7 1.3 copy-done.3
  92.0 5.1 %shard_map.77 = (f32[2304,128]{1,0:T(8,128)S(1)}, bf16[4608,128]{1,0:T(8,128)(2,1)S(1)}) custom-call(f32[18,128]{1,0:T(8,128)S(1)} %get-tuple-element.17.edge_ref, bf16[2304,128]{1,0:T(8,128)(2,1)S(1)} %bitcast.17, f32[2304,128]{1,0:T(8,128)S(1)} %bitcast.12, f32[2304,128]{1,0:T(8,128)S(1)} %copy-done.3, bf16[128,384]{1,0:T(8,128)(2,1)S(1)} %get-tuple-element.23.outcat_ref, ...), custom_call_target="tpu_custom_call" | custom-call | tf_op jit(solution)/shard_map/pallas_call | solution.py:361
  97.1 38.8 %all_to_all.21 = bf16[128,18,2,128]{3,2,1,0:T(2,128)(2,1)S(1)} all-to-all(bf16[128,18,2,128]{3,2,1,0:T(2,128)(2,1)S(1)} %bitcast.19), channel_id=1, replica_groups=mesh['z'=8,'yl'=2,'core'=2,'x'=4,'yh'=2] {'z','yl','x','yh'}, dimensions={0} | all-to-all | bytes 2359296 | tf_op jit(solution)/shard_map/all_to_all | solution.py:381
  136.0 0.0 collective-permute-start.1
  136.0 2.5 %shard_map.78.part_ref = f32[8,384,128]{2,1,0:T(8,128)S(1)} custom-call(bf16[4608,128]{1,0:T(8,128)(2,1)S(1)} %bitcast.16), custom_call_target="tpu_custom_call" | custom-call | tf_op jit(solution)/shard_map/pallas_call | solution.py:361
  138.4 0.4 collective-permute-done.1.other_ref
  138.8 4.6 %shard_map.79 = bf16[2304,128]{1,0:T(8,128)(2,1)} custom-call(f32[8,384,128]{2,1,0:T(8,128)S(1)} %shard_map.78.part_ref, bf16[4608,128]{1,0:T(8,128)(2,1)S(1)} %collective-permute-done.1.other_ref), custom_call_target="tpu_custom_call" | custom-call | tf_op jit(solution)/shard_map/pallas_call | solution.py:361
  143.4 6.7 %all-to-all-start.3 = ((bf16[128,9,2,128]{3,2,1,0:T(2,128)(2,1)}), bf16[128,9,2,128]{3,2,1,0:T(2,128)(2,1)S(1)}, u32[]{:S(2)}, u32[]{:S(2)}) async-start(bf16[128,9,2,128]{3,2,1,0:T(2,128)(2,1)} %bitcast.7), calls=%async_computation.3 | async-start | bytes 1179648 | tf_op jit(solution)/shard_map/all_to_all | solution.py:381
  150.1 2.6 %shard_map.80 = (f32[2304,128]{1,0:T(8,128)S(1)}, bf16[128,384]{1,0:T(8,128)(2,1)S(1)}) custom-call(f32[2304,128]{1,0:T(8,128)S(1)} %get-tuple-element.26.state_ref, f32[2,128,128]{2,1,0:T(8,128)S(1)} %copy-done.5, f32[2,128,128]{2,1,0:T(8,128)S(1)} %copy-done.7), custom_call_target="tpu_custom_call" | custom-call | flops 226492416 | bytes 2359296 | tf_op jit(solution)/shard_map/pallas_call | solution.py:361
  152.7 18.6 %all-to-all-done.3 = bf16[128,9,2,128]{3,2,1,0:T(2,128)(2,1)S(1)} async-done(((bf16[128,9,2,128]{3,2,1,0:T(2,128)(2,1)}), bf16[128,9,2,128]{3,2,1,0:T(2,128)(2,1)S(1)}, u32[]{:S(2)}, u32[]{:S(2)}) %all-to-all-start.3) | async-done | bytes 589856 | tf_op jit(solution)/shard_map/all_to_all | solution.py:381
  171.3 2.6 %shard_map.81 = f32[2304,128]{1,0:T(8,128)} custom-call(bf16[2304,128]{1,0:T(8,128)(2,1)S(1)} %bitcast.18, f32[2304,128]{1,0:T(8,128)S(1)} %get-tuple-element.26.state_ref, f32[2304,128]{1,0:T(8,128)S(1)} %get-tuple-element.27.gate_ref, bf16[128,384]{1,0:T(8,128)(2,1)S(1)} %get-tuple-element.28.outcat_ref), custom_call_target="tpu_custom_call" | custom-call | tf_op jit(solution)/shard_map/pallas_call | solution.py:361
  (15 shorter events, 0.0 us)
Async XLA Ops:
  0.0 0.7 copy-start.8
  0.7 0.7 copy-start.9
  55.7 2.8 %collective-permute-start = (bf16[4608,128]{1,0:T(8,128)(2,1)S(1)}, bf16[4608,128]{1,0:T(8,128)(2,1)S(1)}, u32[]{:S(2)}, u32[]{:S(2)}) collective-permute-start(bf16[4608,128]{1,0:T(8,128)(2,1)S(1)} %bitcast.13), channel_id=1, source_target_pairs={{0,8},{8,0},{1,9},{9,1},{2,10},{10,2},{3,11},{11,3},{4,12},{12,4},... | collective-permute-start | bytes 3538952 | tf_op jit(solution)/shard_map/ppermute | solution.py:386
  58.6 11.0 %copy-start.1 = (f32[2,128,512]{2,1,0:T(8,128)S(1)}, f32[2,128,512]{2,1,0:T(8,128)}, u32[]{:S(2)}) copy-start(f32[2,128,512]{2,1,0:T(8,128)} %refs_0_.1) | copy-start | bytes 1572868
  58.6 11.0 %copy-start.4 = (f32[2,128,128]{2,1,0:T(8,128)S(1)}, f32[2,128,128]{2,1,0:T(8,128)}, u32[]{:S(2)}) copy-start(f32[2,128,128]{2,1,0:T(8,128)} %gatew_ref.3) | copy-start | bytes 393220
  58.6 11.0 %copy-start.6 = (f32[2,128,128]{2,1,0:T(8,128)S(1)}, f32[2,128,128]{2,1,0:T(8,128)}, u32[]{:S(2)}) copy-start(f32[2,128,128]{2,1,0:T(8,128)} %outw_ref.3) | copy-start | bytes 393220
  62.9 6.6 %copy-start = (f32[24,96,128]{2,1,0:T(8,128)S(1)}, f32[24,96,128]{2,1,0:T(8,128)}, u32[]{:S(2)}) copy-start(f32[24,96,128]{2,1,0:T(8,128)} %param.7) | copy-start | bytes 3538948
  62.9 27.8 %all-to-all-start.1 = ((bf16[128,9,2,128]{3,2,1,0:T(2,128)(2,1)}), bf16[128,9,2,128]{3,2,1,0:T(2,128)(2,1)S(1)}, u32[]{:S(2)}, u32[]{:S(2)}) async-start(bf16[128,9,2,128]{3,2,1,0:T(2,128)(2,1)} %bitcast.3), calls=%async_computation.1 | async-start | bytes 1179648 | tf_op jit(solution)/shard_map/all_to_all | solution.py:381
  72.2 1.0 copy-start.2
  90.7 1.3 copy-start.3
  136.0 2.8 %collective-permute-start.1 = (bf16[4608,128]{1,0:T(8,128)(2,1)S(1)}, bf16[4608,128]{1,0:T(8,128)(2,1)S(1)}, u32[]{:S(2)}, u32[]{:S(2)}) collective-permute-start(bf16[4608,128]{1,0:T(8,128)(2,1)S(1)} %bitcast.15), channel_id=1, source_target_pairs={{0,8},{8,0},{1,9},{9,1},{2,10},{10,2},{3,11},{11,3},{4,12},{12,4},... | collective-permute-start | bytes 3538952 | tf_op jit(solution)/shard_map/ppermute | solution.py:386
  143.4 6.7 %copy-start.5 = (f32[2,128,128]{2,1,0:T(8,128)S(1)}, f32[2,128,128]{2,1,0:T(8,128)}, u32[]{:S(2)}) copy-start(f32[2,128,128]{2,1,0:T(8,128)} %gatew_ref.3) | copy-start | bytes 393220
  143.4 6.7 %copy-start.7 = (f32[2,128,128]{2,1,0:T(8,128)S(1)}, f32[2,128,128]{2,1,0:T(8,128)}, u32[]{:S(2)}) copy-start(f32[2,128,128]{2,1,0:T(8,128)} %outw_ref.3) | copy-start | bytes 393220
  143.4 27.9 %all-to-all-start.3 = ((bf16[128,9,2,128]{3,2,1,0:T(2,128)(2,1)}), bf16[128,9,2,128]{3,2,1,0:T(2,128)(2,1)S(1)}, u32[]{:S(2)}, u32[]{:S(2)}) async-start(bf16[128,9,2,128]{3,2,1,0:T(2,128)(2,1)} %bitcast.7), calls=%async_computation.3 | async-start | bytes 1179648 | tf_op jit(solution)/shard_map/all_to_all | solution.py:381

commit v4 on v3

--- a/solution.py
+++ b/solution.py
@@ -98,16 +98,23 @@
     lax.fori_loop(0, 18, convert, 0)
 
 
-def first_kernel(mask_sm, hot_sm, inter_ref, state_hbm, proj_hbm, send_ref, edge_ref,
-                 rows_ref, state_ref, proj_ref, sems, norm_ref, mix_ref):
-    state_copy = pltpu.make_async_copy(state_hbm, state_ref, sems.at[0])
-    proj_copy = pltpu.make_async_copy(proj_hbm.at[0], proj_ref, sems.at[1])
-    state_copy.start()
-    proj_copy.start()
+def first_kernel(mask_hbm, hot_hbm, inter_hbm, state_hbm, proj_hbm, send_ref, edge_ref, mask_sm, hot_sm,
+                 inter_ref, rows_ref, state_ref, proj_ref, sems, norm_ref, mix_ref):
+    copies = [
+        pltpu.make_async_copy(source, target, sems.at[n])
+        for n, (source, target) in enumerate((
+            (mask_hbm, mask_sm), (hot_hbm, hot_sm), (inter_hbm, inter_ref), (proj_hbm.at[0], proj_ref),
+            (state_hbm, state_ref),
+        ))
+    ]
+    for copy in copies:
+        copy.start()
+    for copy in copies[:3]:
+        copy.wait()
     packed_edge(mask_sm, hot_sm, inter_ref, edge_ref, rows_ref)
-    proj_copy.wait()
+    copies[3].wait()
     w_cat = stacked(proj_ref[...].T, 1)
-    state_copy.wait()
+    copies[4].wait()
     project(state_ref, w_cat, edge_ref, norm_ref, mix_ref, send_ref)
 
 
@@ -166,34 +173,43 @@
         target_ref[aligned(start + 8 * n, 8, 8), column] = part
 
 
-def pack_tri(tri_ref, base, wide_ref, target):
+def tail_slot(half, g):
+    return 8 + (half * 8 + g) * 24
+
+
+def send_tri(tri_ref, mix_ref, tail_ref, ready_ref, out_hbm, sems):
     lane = lanes((8, 128))
-    sub = lax.broadcasted_iota(jnp.int32, (8, 128), 0)
-
-    def rows(at, shift=0):
-        value = tri_ref[pl.ds(base + at, 8), :]
-        return pltpu.roll(value, shift, 1) if shift else value
-
-    tails = (
-        jnp.where(sub < 6, rows(18, 96), rows(12, 64)),
-        jnp.where(sub < 4, rows(20, 64), rows(14, 32)),
-        rows(22, 32),
-    )
-    for n, tail in enumerate(tails):
-        value = jnp.where(lane < COLS, rows(8 * n), tail)
-        if n < 2:
-            wide_ref[pl.ds(target + 8 * n, 8), :] = value
-        else:
-            wide_ref[pl.ds(target + 16, 2), :] = value[0:2]
-
-
-def narrow(wide_ref, out_ref):
-    def step(i, carry):
-        at = aligned(i * 256, 256, 256)
-        out_ref[at, :] = wide_ref[at, :].astype(BF16)
-        return carry
-
-    lax.fori_loop(0, 9, step, 0)
+
+    def send(i, carry):
+        blocks = [(half, g, (2 * i + half) * 24) for half in range(2) for g in range(8)]
+        for half, g, base in blocks:
+            slot = tail_slot(half, g)
+            value = tri_ref[g, aligned(base + 16, 8, 8), :]
+            tail_ref[slot + 10 : slot + 18, :] = pltpu.roll(value, 32, 1)
+            tail_ref[slot + 4 : slot + 12, :] = pltpu.roll(value, 64, 1)
+            tail_ref[slot - 2 : slot + 6, :] = pltpu.roll(value, 96, 1)
+        for half, g, base in blocks:
+            slot = tail_slot(half, g)
+            target = ((2 * i + half) * 8 + g) * PACK
+            for n in range(3):
+                tail = tail_ref[slot + 8 * n : slot + 8 * n + 8, :]
+                value = jnp.where(lane < COLS, tri_ref[g, aligned(base + 8 * n, 8, 8), :], tail)
+                if n < 2:
+                    mix_ref[pl.ds(target + 8 * n, 8), :] = value
+                else:
+                    mix_ref[pl.ds(target + 16, 2), :] = value[0:2]
+        at = aligned(i * 288, 288, 288)
+        ready_ref[at, :] = mix_ref[at, :].astype(BF16)
+        return carry
+
+    copies = []
+    for n in range(4):
+        lax.fori_loop(2 * n, 2 * n + 2, send, 0)
+        at = pl.ds(576 * n, 576)
+        copies.append(pltpu.make_async_copy(ready_ref.at[at], out_hbm.at[at], sems.at[n]))
+        copies[-1].start()
+    for copy in copies:
+        copy.wait()
 
 
 def outgoing_own(own_ref, left_ref, right_ref, wide_ref, keep_ref):
@@ -215,17 +231,7 @@
     left_ref[...] = keep_ref[...].astype(BF16)
 
 
-def send_tri(tri_ref, mix_ref, out_ref):
-    def send(b, carry):
-        for g in range(8):
-            pack_tri(tri_ref.at[g], b * 24, mix_ref, (b * 8 + g) * PACK)
-        return carry
-
-    lax.fori_loop(0, 16, send, 0, unroll=2)
-    narrow(mix_ref, out_ref)
-
-
-def outgoing_kernel(left_ref, _, other_ref, out_ref, right_ref, wide_ref, tri_ref, mix_ref):
+def outgoing_kernel(left_ref, _, other_ref, out_hbm, right_ref, wide_ref, tri_ref, *scratch):
     core = lax.axis_index("core")
     widen(other_ref, wide_ref)
 
@@ -242,7 +248,8 @@
         tri = matmul(left, right_ref[256 * n : 256 * n + 256, :].astype(BF16), ((1,), (1,)))
         tri_ref[2 * n, 0:384, :] = tri[:, 0:128]
         tri_ref[2 * n + 1, 0:384, :] = tri[:, 128:256]
-    send_tri(tri_ref, mix_ref, out_ref)
+    mix_ref, tail_ref, ready_ref, sems = scratch
+    send_tri(tri_ref, mix_ref, tail_ref, ready_ref, out_hbm, sems)
 
 
 def incoming_half(source_ref, wide_ref, left_ref, right_ref, turn_ref, turned_ref):
@@ -275,13 +282,22 @@
         part_ref[g] = tri
 
 
-def incoming_kernel(part_ref, other_ref, out_ref, wide_ref, left_ref, right_ref, turn_ref, turned_ref, tri_ref, mix_ref):
+def incoming_kernel(part_ref, other_ref, out_hbm, wide_ref, left_ref, right_ref, turn_ref, turned_ref, tri_ref,
+                    mix_ref, tail_ref, ready_ref, sems):
     for g, tri in incoming_half(other_ref, wide_ref, left_ref, right_ref, turn_ref, turned_ref):
         tri_ref[g, 0:384, :] = part_ref[g] + tri
-    send_tri(tri_ref, mix_ref, out_ref)
-
-
-def finish(tri_ref, state_ref, gate_ref, w_cat, scaled_ref, stat_ref, next_ref):
+    send_tri(tri_ref, mix_ref, tail_ref, ready_ref, out_hbm, sems)
+
+
+def finish(tri_ref, state_ref, gate_hbm, outcat_hbm, next_ref, scaled_ref, stat_ref, gate_ref, outcat_ref, fetch_sems,
+           done=None):
+    fetches = [
+        pltpu.make_async_copy(outcat_hbm, outcat_ref, fetch_sems.at[0]),
+        pltpu.make_async_copy(gate_hbm, gate_ref, fetch_sems.at[1]),
+    ]
+    for fetch in fetches:
+        fetch.start()
+
     def stats(i, carry):
         total, square = carry
         t = tri_ref[aligned(i * 144, 144, 144), :].astype(F32)
@@ -310,6 +326,10 @@
         return carry
 
     lax.fori_loop(0, 16, rescale, 0)
+    for fetch in fetches:
+        fetch.wait()
+    w_cat = outcat_ref[...]
+
     def combine(i, carry):
         pieces = [split_bf16(scaled_ref[pl.ds(2 * i + half, CH, stride=PACK), :]) for half in range(2)]
         high = jnp.concatenate([pieces[0][0], pieces[1][0]], axis=1)
@@ -324,17 +344,36 @@
             next_ref[at, :] = state_ref[at, :] + gate_ref[at, :] * value[COLS:]
         return carry
 
-    lax.fori_loop(0, PACK // 2, combine, 0, unroll=3)
-
-
-def middle_kernel(edge_ref, tri_ref, state_ref, gate_ref, outcat_ref, projcat_ref, next_ref, send_ref,
-                  norm_ref, mix_ref, scaled_ref, stat_ref):
-    finish(tri_ref, state_ref, gate_ref, outcat_ref[...], scaled_ref, stat_ref, next_ref)
+    if done is None:
+        lax.fori_loop(0, PACK // 2, combine, 0, unroll=3)
+    else:
+        for n in range(3):
+            for i in range(3):
+                combine(3 * n + i, 0)
+            done(n)
+        done(3)
+
+
+def middle_kernel(edge_ref, tri_ref, state_ref, gate_hbm, outcat_hbm, projcat_hbm, next_ref, send_ref,
+                  projcat_ref, sems, norm_ref, mix_ref, *scratch):
+    fetch = pltpu.make_async_copy(projcat_hbm, projcat_ref, sems.at[0])
+    fetch.start()
+    finish(tri_ref, state_ref, gate_hbm, outcat_hbm, next_ref, *scratch)
+    fetch.wait()
     project(next_ref, projcat_ref[...], edge_ref, norm_ref, mix_ref, send_ref)
 
 
-def last_kernel(tri_ref, state_ref, gate_ref, outcat_ref, next_ref, scaled_ref, stat_ref):
-    finish(tri_ref, state_ref, gate_ref, outcat_ref[...], scaled_ref, stat_ref, next_ref)
+def last_kernel(tri_ref, state_ref, gate_hbm, outcat_hbm, out_hbm, next_ref, sems, *scratch):
+    copies = []
+
+    def done(n):
+        at = pl.ds(n * PIX // 4, PIX // 4)
+        copies.append(pltpu.make_async_copy(next_ref.at[at], out_hbm.at[at], sems.at[n]))
+        copies[-1].start()
+
+    finish(tri_ref, state_ref, gate_hbm, outcat_hbm, next_ref, *scratch, done=done)
+    for copy in copies:
+        copy.wait()
 
 
 VM = pl.BlockSpec(memory_space=pltpu.VMEM)
@@ -342,13 +381,20 @@
 HB = pl.BlockSpec(memory_space=pltpu.HBM)
 STATE = pltpu.VMEM((PIX, CH), F32)
 SEND = pltpu.VMEM((CH * 2 * PACK, 128), BF16)
-TRI = pltpu.VMEM((CH * PACK, 128), BF16)
+TRI = pltpu.HBM((CH * PACK, 128), BF16)
+GATE = pltpu.HBM((PIX, CH), F32)
 EDGE = pltpu.VMEM((PACK, 128), F32)
-OUTCAT = pltpu.VMEM((CH, 3 * CH), BF16)
-PROJCAT = pltpu.VMEM((4 * CH, 3 * CH), BF16)
+OUTCAT = pltpu.HBM((CH, 3 * CH), BF16)
+PROJCAT = pltpu.HBM((4 * CH, 3 * CH), BF16)
 PROJECT_SCRATCH = [pltpu.VMEM((PACK * 128, 384), BF16), pltpu.VMEM((CH * 2 * PACK, 128), F32)]
-FINISH_SCRATCH = [pltpu.VMEM((CH * PACK, 128), F32), pltpu.VMEM((2, 72, 128), F32)]
-SEND_SCRATCH = [pltpu.VMEM((8, 392, 128), F32), pltpu.VMEM((CH * PACK, 128), F32)]
+FINISH_SCRATCH = [
+    pltpu.VMEM((CH * PACK, 128), F32), pltpu.VMEM((2, 72, 128), F32), pltpu.VMEM((PIX, CH), F32),
+    pltpu.VMEM((CH, 3 * CH), BF16), pltpu.SemaphoreType.DMA((2,)),
+]
+SEND_SCRATCH = [
+    pltpu.VMEM((8, 384, 128), F32), pltpu.VMEM((CH * PACK, 128), F32), pltpu.VMEM((400, 128), F32),
+    pltpu.VMEM((CH * PACK, 128), BF16), pltpu.SemaphoreType.DMA((4,)),
+]
 WIDE = pltpu.VMEM((CH * 2 * PACK + 16, 128), F32)
 HALF = pltpu.VMEM((384, 1024), F32)
 RIGHT = pltpu.VMEM((1024, 1024), F32)
@@ -356,13 +402,13 @@
 PART = pltpu.VMEM((8, 384, 128), F32)
 
 
-def call(kernel, out_shape, operands, scratch=(), specs=None, mib=16, **options):
+def call(kernel, out_shape, operands, scratch=(), specs=None, out_specs=None, mib=16, **options):
     outs = out_shape if isinstance(out_shape, tuple) else None
     return pl.pallas_call(
         kernel,
         out_shape=out_shape,
         in_specs=specs or [VM] * len(operands),
-        out_specs=VM if outs is None else (VM,) * len(outs),
+        out_specs=out_specs or (VM if outs is None else (VM,) * len(outs)),
         scratch_shapes=list(scratch),
         compiler_params=pltpu.CompilerParams(vmem_limit_bytes=mib * 1024 * 1024),
         **options,
@@ -395,33 +441,36 @@
     state = pair.reshape(PIX, CH)
     send, edge = call(
         first_kernel, (SEND, EDGE),
-        (residue_mask, hotspot, far(interface), far(state), far(proj_weight)),
-        [pltpu.VMEM((ROWS, 128), jnp.int32), pltpu.VMEM((PIX, CH), F32), pltpu.VMEM((CH, 4 * CH), F32),
-         pltpu.SemaphoreType.DMA((2,))] + PROJECT_SCRATCH,
-        [SM, SM, VM, HB, HB],
+        (far(residue_mask), far(hotspot), far(interface), far(state), far(proj_weight)),
+        [pltpu.SMEM((768,), jnp.int32), pltpu.SMEM((768,), jnp.int32), pltpu.VMEM((ROWS, COLS), jnp.int32),
+         pltpu.VMEM((ROWS, 128), jnp.int32), pltpu.VMEM((PIX, CH), F32), pltpu.VMEM((CH, 4 * CH), F32),
+         pltpu.SemaphoreType.DMA((5,))] + PROJECT_SCRATCH,
+        [HB] * 5,
     )
     own = exchange(send, 2 * PACK)
     other = partner(own)
     left, right = call(outgoing_own, (pltpu.VMEM((384, 1024), BF16), RIGHT), (near(own),), [WIDE, HALF])
     tri, _ = call(
         outgoing_kernel, (TRI, RIGHT), (near(left), near(right), near(other)), [WIDE] + SEND_SCRATCH,
-        input_output_aliases={1: 1},
+        out_specs=(HB, VM), input_output_aliases={1: 1},
     )
     tri = exchange(tri, PACK)
-    gate, outcat, projcat = gating(0, (STATE, OUTCAT, PROJCAT), near(state), gate_weight, out_weight, proj_weight)
+    gate, outcat, projcat = gating(0, (GATE, OUTCAT, PROJCAT), near(state), gate_weight, out_weight, proj_weight)
     state, send = call(
         middle_kernel, (STATE, SEND),
-        (near(edge), near(tri), near(state), near(gate), near(outcat), near(projcat)), PROJECT_SCRATCH + FINISH_SCRATCH,
+        (near(edge), near(tri), near(state), far(gate), far(outcat), far(projcat)),
+        [pltpu.VMEM((4 * CH, 3 * CH), BF16), pltpu.SemaphoreType.DMA((1,))] + PROJECT_SCRATCH + FINISH_SCRATCH,
+        [VM, VM, VM, HB, HB, HB],
     )
     own = exchange(send, 2 * PACK)
     other = partner(own)
     part = call(incoming_own, PART, (near(own),), HALF_SCRATCH)
-    tri = call(incoming_kernel, TRI, (near(part), near(other)), HALF_SCRATCH + SEND_SCRATCH)
+    tri = call(incoming_kernel, TRI, (near(part), near(other)), HALF_SCRATCH + SEND_SCRATCH, out_specs=HB)
     tri = exchange(tri, PACK)
-    gate, outcat = gating(1, (STATE, OUTCAT), near(state), gate_weight, out_weight)
+    gate, outcat = gating(1, (GATE, OUTCAT), near(state), gate_weight, out_weight)
     state = call(
-        last_kernel, jax.ShapeDtypeStruct((PIX, CH), F32), (near(tri), near(state), near(gate), near(outcat)),
-        FINISH_SCRATCH,
+        last_kernel, jax.ShapeDtypeStruct((PIX, CH), F32), (near(tri), near(state), far(gate), far(outcat)),
+        [pltpu.VMEM((PIX, CH), F32), pltpu.SemaphoreType.DMA((4,))] + FINISH_SCRATCH, [VM, VM, HB, HB], out_specs=HB,
     )
     return state.reshape(ROWS, COLS, CH)
 

time: 174 us -> 171 us (0.983)
  local copies, waits for them, and re-layouts: 3.68 us -> 0.02 us
    unnamed x20 -> x8, local copies, waits for them, and re-layouts: 3.68 us -> 0.02 us
  transfers between devices with their start and end apart: 4 -> 4, of which waited for: 4 -> 4; matrix products, arithmetic and copies ran while one was open for 0% -> 0% of each run, Pallas kernels for 5% -> 7%
where the time goes in v4:
time: 171 us
  blocking collectives  87.4 us (51%)
  waiting for transfers between devices  36.6 us (21%)
  Pallas kernels  33.6 us (20%)
  starting transfers between devices  13.2 us (8%)
    all_to_all x2, blocking collectives, exchange(): lax.all_to_all(message.reshape(CH, rows // 2, 2, 128), CHIPS, split_axis=...  87.4 us
    all_to_all x2, waiting for transfers between devices, exchange(): lax.all_to_all(message.reshape(CH, rows // 2, 2, 128), CHIPS, split_axis=...  35.1 us
    pallas_call x9, Pallas kernels, call(): pl.pallas_call(kernel, out_shape=out_shape, in_specs=specs or [VM] * len(...  33.6 us
    all_to_all x2, starting transfers between devices, exchange(): lax.all_to_all(message.reshape(CH, rows // 2, 2, 128), CHIPS, split_axis=...  13.2 us
  transfers between devices with their start and end apart: 4, of which 4 were waited for; matrix products, arithmetic and copies ran while one was open for 0% of the time, Pallas kernels for 7%

profile of v4, /device:TPU:6, one launch (start us, length us, event | category | flops | bytes accessed | tf_op | source)
XLA Modules:
  0.0 171.1 jit_solution(1332924449342257081)
XLA Ops:
  0.0 4.8 %shard_map.73 = (bf16[4608,128]{1,0:T(8,128)(2,1)S(1)}, f32[18,128]{1,0:T(8,128)S(1)}) custom-call(s32[768]{0:T(1024)} %mask_hbm.1, s32[768]{0:T(1024)} %hot_hbm.1, s32[24,96]{1,0:T(8,128)} %inter_hbm.1, f32[2304,128]{1,0:T(8,128)} %bitcast.10, f32[2,128,512]{2,1,0:T(8,128)} %refs_0_.1), custom_call_target="tpu_custom_call" | custom-call | tf_op jit(solution)/shard_map/pallas_call | solution.py:407
  4.8 48.6 %all_to_all.20 = bf16[128,18,2,128]{3,2,1,0:T(2,128)(2,1)S(1)} all-to-all(bf16[128,18,2,128]{3,2,1,0:T(2,128)(2,1)S(1)} %bitcast.20), channel_id=1, replica_groups=mesh['z'=8,'yl'=2,'core'=2,'x'=4,'yh'=2] {'z','yl','x','yh'}, dimensions={0} | all-to-all | bytes 2359296 | tf_op jit(solution)/shard_map/all_to_all | solution.py:427
  53.4 0.0 collective-permute-start
  53.4 1.7 %shard_map.74 = (bf16[384,1024]{1,0:T(8,128)(2,1)S(1)}, f32[1024,1024]{1,0:T(8,128)S(1)}) custom-call(bf16[4608,128]{1,0:T(8,128)(2,1)S(1)} %bitcast.14), custom_call_target="tpu_custom_call" | custom-call | tf_op jit(solution)/shard_map/pallas_call | solution.py:407
  55.2 1.1 collective-permute-done.other_ref
  56.3 4.1 %shard_map.75 = (bf16[2304,128]{1,0:T(8,128)(2,1)}, f32[1024,1024]{1,0:T(8,128)S(1)}) custom-call(bf16[384,1024]{1,0:T(8,128)(2,1)S(1)} %get-tuple-element.19.left_ref, f32[1024,1024]{1,0:T(8,128)S(1)} %get-tuple-element.20._, bf16[4608,128]{1,0:T(8,128)(2,1)S(1)} %collective-permute-done.other_ref), custom_call_target="tpu_custom_call", output_to_operand_aliasing={{1}: (1, {})} | custom-call | tf_op jit(solution)/shard_map/pallas_call | solution.py:407
  60.4 0.0 copy-start
  60.4 6.6 %all-to-all-start.1 = ((bf16[128,9,2,128]{3,2,1,0:T(2,128)(2,1)}), bf16[128,9,2,128]{3,2,1,0:T(2,128)(2,1)S(1)}, u32[]{:S(2)}, u32[]{:S(2)}) async-start(bf16[128,9,2,128]{3,2,1,0:T(2,128)(2,1)} %bitcast.22), calls=%async_computation.1 | async-start | bytes 1179648 | tf_op jit(solution)/shard_map/all_to_all | solution.py:427
  67.0 0.0 copy-done.1
  67.0 0.0 copy-done.2
  67.0 0.0 copy-done.3
  67.0 0.0 copy-done
  67.1 3.7 %shard_map.76 = (f32[2304,128]{1,0:T(8,128)}, bf16[128,384]{1,0:T(8,128)(2,1)}, bf16[512,384]{1,0:T(8,128)(2,1)}) custom-call(f32[2304,128]{1,0:T(8,128)S(1)} %bitcast.11, f32[2,128,128]{2,1,0:T(8,128)S(1)} %copy-done.2, f32[2,128,128]{2,1,0:T(8,128)S(1)} %copy-done.3, f32[2,128,512]{2,1,0:T(8,128)S(1)} %copy-done.1), custom_call_target="tpu_custom_call" | custom-call | flops 226492416 | bytes 2359296 | tf_op jit(solution)/shard_map/pallas_call | solution.py:407
  70.7 17.5 %all-to-all-done.1 = bf16[128,9,2,128]{3,2,1,0:T(2,128)(2,1)S(1)} async-done(((bf16[128,9,2,128]{3,2,1,0:T(2,128)(2,1)}), bf16[128,9,2,128]{3,2,1,0:T(2,128)(2,1)S(1)}, u32[]{:S(2)}, u32[]{:S(2)}) %all-to-all-start.1) | async-done | bytes 589856 | tf_op jit(solution)/shard_map/all_to_all | solution.py:427
  88.2 6.0 %shard_map.77 = (f32[2304,128]{1,0:T(8,128)S(1)}, bf16[4608,128]{1,0:T(8,128)(2,1)S(1)}) custom-call(f32[18,128]{1,0:T(8,128)S(1)} %get-tuple-element.17.edge_ref, bf16[2304,128]{1,0:T(8,128)(2,1)S(1)} %bitcast.17, f32[2304,128]{1,0:T(8,128)S(1)} %bitcast.12, f32[2304,128]{1,0:T(8,128)} %get-tuple-element.22.gate_hbm, ...), custom_call_target="tpu_custom_call" | custom-call | tf_op jit(solution)/shard_map/pallas_call | solution.py:407
  94.3 38.8 %all_to_all.21 = bf16[128,18,2,128]{3,2,1,0:T(2,128)(2,1)S(1)} all-to-all(bf16[128,18,2,128]{3,2,1,0:T(2,128)(2,1)S(1)} %bitcast.19), channel_id=1, replica_groups=mesh['z'=8,'yl'=2,'core'=2,'x'=4,'yh'=2] {'z','yl','x','yh'}, dimensions={0} | all-to-all | bytes 2359296 | tf_op jit(solution)/shard_map/all_to_all | solution.py:427
  133.1 0.0 collective-permute-start.1
  133.1 2.5 %shard_map.78.part_ref = f32[8,384,128]{2,1,0:T(8,128)S(1)} custom-call(bf16[4608,128]{1,0:T(8,128)(2,1)S(1)} %bitcast.16), custom_call_target="tpu_custom_call" | custom-call | tf_op jit(solution)/shard_map/pallas_call | solution.py:407
  135.6 0.4 collective-permute-done.1.other_ref
  136.0 4.3 %shard_map.79 = bf16[2304,128]{1,0:T(8,128)(2,1)} custom-call(f32[8,384,128]{2,1,0:T(8,128)S(1)} %shard_map.78.part_ref, bf16[4608,128]{1,0:T(8,128)(2,1)S(1)} %collective-permute-done.1.other_ref), custom_call_target="tpu_custom_call" | custom-call | tf_op jit(solution)/shard_map/pallas_call | solution.py:407
  140.3 6.5 %all-to-all-start.3 = ((bf16[128,9,2,128]{3,2,1,0:T(2,128)(2,1)}), bf16[128,9,2,128]{3,2,1,0:T(2,128)(2,1)S(1)}, u32[]{:S(2)}, u32[]{:S(2)}) async-start(bf16[128,9,2,128]{3,2,1,0:T(2,128)(2,1)} %bitcast.21), calls=%async_computation.3 | async-start | bytes 1179648 | tf_op jit(solution)/shard_map/all_to_all | solution.py:427
  146.9 3.6 %shard_map.80 = (f32[2304,128]{1,0:T(8,128)}, bf16[128,384]{1,0:T(8,128)(2,1)}) custom-call(f32[2304,128]{1,0:T(8,128)S(1)} %get-tuple-element.26.state_ref, f32[2,128,128]{2,1,0:T(8,128)S(1)} %copy-done.2, f32[2,128,128]{2,1,0:T(8,128)S(1)} %copy-done.3), custom_call_target="tpu_custom_call" | custom-call | flops 226492416 | bytes 2359296 | tf_op jit(solution)/shard_map/pallas_call | solution.py:407
  150.5 17.6 %all-to-all-done.3 = bf16[128,9,2,128]{3,2,1,0:T(2,128)(2,1)S(1)} async-done(((bf16[128,9,2,128]{3,2,1,0:T(2,128)(2,1)}), bf16[128,9,2,128]{3,2,1,0:T(2,128)(2,1)S(1)}, u32[]{:S(2)}, u32[]{:S(2)}) %all-to-all-start.3) | async-done | bytes 589856 | tf_op jit(solution)/shard_map/all_to_all | solution.py:427
  168.1 2.8 %shard_map.81 = f32[2304,128]{1,0:T(8,128)} custom-call(bf16[2304,128]{1,0:T(8,128)(2,1)S(1)} %bitcast.18, f32[2304,128]{1,0:T(8,128)S(1)} %get-tuple-element.26.state_ref, f32[2304,128]{1,0:T(8,128)} %get-tuple-element.27.gate_hbm, bf16[128,384]{1,0:T(8,128)(2,1)} %get-tuple-element.28.outcat_hbm), custom_call_target="tpu_custom_call" | custom-call | tf_op jit(solution)/shard_map/pallas_call | solution.py:407
  (3 shorter events, 0.0 us)
Async XLA Ops:
  53.4 2.8 %collective-permute-start = (bf16[4608,128]{1,0:T(8,128)(2,1)S(1)}, bf16[4608,128]{1,0:T(8,128)(2,1)S(1)}, u32[]{:S(2)}, u32[]{:S(2)}) collective-permute-start(bf16[4608,128]{1,0:T(8,128)(2,1)S(1)} %bitcast.13), channel_id=1, source_target_pairs={{0,8},{8,0},{1,9},{9,1},{2,10},{10,2},{3,11},{11,3},{4,12},{12,4},... | collective-permute-start | bytes 3538952 | tf_op jit(solution)/shard_map/ppermute | solution.py:432
  56.3 10.7 %copy-start.1 = (f32[2,128,512]{2,1,0:T(8,128)S(1)}, f32[2,128,512]{2,1,0:T(8,128)}, u32[]{:S(2)}) copy-start(f32[2,128,512]{2,1,0:T(8,128)} %refs_0_.1) | copy-start | bytes 1572868
  56.3 10.7 %copy-start.2 = (f32[2,128,128]{2,1,0:T(8,128)S(1)}, f32[2,128,128]{2,1,0:T(8,128)}, u32[]{:S(2)}) copy-start(f32[2,128,128]{2,1,0:T(8,128)} %gatew_ref.3) | copy-start | bytes 393220
  56.3 10.7 %copy-start.3 = (f32[2,128,128]{2,1,0:T(8,128)S(1)}, f32[2,128,128]{2,1,0:T(8,128)}, u32[]{:S(2)}) copy-start(f32[2,128,128]{2,1,0:T(8,128)} %outw_ref.3) | copy-start | bytes 393220
  60.4 6.7 %copy-start = (f32[24,96,128]{2,1,0:T(8,128)S(1)}, f32[24,96,128]{2,1,0:T(8,128)}, u32[]{:S(2)}) copy-start(f32[24,96,128]{2,1,0:T(8,128)} %param.7) | copy-start | bytes 3538948
  60.4 27.8 %all-to-all-start.1 = ((bf16[128,9,2,128]{3,2,1,0:T(2,128)(2,1)}), bf16[128,9,2,128]{3,2,1,0:T(2,128)(2,1)S(1)}, u32[]{:S(2)}, u32[]{:S(2)}) async-start(bf16[128,9,2,128]{3,2,1,0:T(2,128)(2,1)} %bitcast.22), calls=%async_computation.1 | async-start | bytes 1179648 | tf_op jit(solution)/shard_map/all_to_all | solution.py:427
  133.1 2.8 %collective-permute-start.1 = (bf16[4608,128]{1,0:T(8,128)(2,1)S(1)}, bf16[4608,128]{1,0:T(8,128)(2,1)S(1)}, u32[]{:S(2)}, u32[]{:S(2)}) collective-permute-start(bf16[4608,128]{1,0:T(8,128)(2,1)S(1)} %bitcast.15), channel_id=1, source_target_pairs={{0,8},{8,0},{1,9},{9,1},{2,10},{10,2},{3,11},{11,3},{4,12},{12,4},... | collective-permute-start | bytes 3538952 | tf_op jit(solution)/shard_map/ppermute | solution.py:432
  140.3 27.8 %all-to-all-start.3 = ((bf16[128,9,2,128]{3,2,1,0:T(2,128)(2,1)}), bf16[128,9,2,128]{3,2,1,0:T(2,128)(2,1)S(1)}, u32[]{:S(2)}, u32[]{:S(2)}) async-start(bf16[128,9,2,128]{3,2,1,0:T(2,128)(2,1)} %bitcast.21), calls=%async_computation.3 | async-start | bytes 1179648 | tf_op jit(solution)/shard_map/all_to_all | solution.py:427

commit v5 on v4

--- a/solution.py
+++ b/solution.py
@@ -63,21 +63,23 @@
     return aligned((18 + t % 6) * COLS + 32 * (t // 6), 32, 32)
 
 
-def project(state_ref, w_cat, edge_ref, norm_ref, mix_ref, send_ref):
-    def normalize(t, carry):
-        x = jnp.concatenate([state_ref[aligned(t * COLS, COLS, COLS), :], state_ref[tail_pixels(t), :]], axis=0)
-        centred = x - jnp.mean(x, axis=-1, keepdims=True)
-        variance = jnp.mean(centred * centred, axis=-1, keepdims=True)
-        high, low = split_bf16(centred * lax.rsqrt(variance + EPS))
-        at = aligned(t * 128, 128, 128)
-        norm_ref[at, 0:128] = high
-        norm_ref[at, 128:256] = high
-        norm_ref[at, 256:384] = low
-        return carry
-
-    lax.fori_loop(0, PACK, normalize, 0, unroll=3)
+def normalized(x):
+    centred = x - jnp.mean(x, axis=0, keepdims=True)
+    variance = jnp.mean(centred * centred, axis=0, keepdims=True)
+    high, low = split_bf16(centred * lax.rsqrt(variance + EPS))
+    return jnp.concatenate([high, high, low], axis=0)
+
+
+def project(state_ref, w_cat, edge_ref, norm_ref, mix_ref, send_ref, normalize=None):
+    def prepare(i, carry):
+        for half in range(2):
+            norm_ref[i, :, 128 * half : 128 * half + 128] = normalized(state_ref[2 * i + half])
+        return carry
+
+    lax.fori_loop(0, PACK // 2, normalize or prepare, 0, unroll=3)
+
     def pair(i, carry):
-        values = matmul(w_cat, norm_ref[aligned(i * 256, 256, 256), :], ((1,), (1,)))
+        values = matmul(w_cat, norm_ref[i], ((1,), (0,)))
         for half in range(2):
             t = 2 * i + half
             part = values[:, 128 * half : 128 * half + 128]
@@ -98,13 +100,13 @@
     lax.fori_loop(0, 18, convert, 0)
 
 
-def first_kernel(mask_hbm, hot_hbm, inter_hbm, state_hbm, proj_hbm, send_ref, edge_ref, mask_sm, hot_sm,
-                 inter_ref, rows_ref, state_ref, proj_ref, sems, norm_ref, mix_ref):
+def first_kernel(mask_hbm, hot_hbm, inter_hbm, pair_hbm, proj_hbm, send_ref, edge_ref, state_ref, mask_sm, hot_sm,
+                 inter_ref, rows_ref, pair_ref, proj_ref, sems, norm_ref, mix_ref):
     copies = [
         pltpu.make_async_copy(source, target, sems.at[n])
         for n, (source, target) in enumerate((
             (mask_hbm, mask_sm), (hot_hbm, hot_sm), (inter_hbm, inter_ref), (proj_hbm.at[0], proj_ref),
-            (state_hbm, state_ref),
+            (pair_hbm, pair_ref),
         ))
     ]
     for copy in copies:
@@ -115,7 +117,16 @@
     copies[3].wait()
     w_cat = stacked(proj_ref[...].T, 1)
     copies[4].wait()
-    project(state_ref, w_cat, edge_ref, norm_ref, mix_ref, send_ref)
+
+    def prepare(i, carry):
+        for half in range(2):
+            t = 2 * i + half
+            x = jnp.concatenate([pair_ref[aligned(t * COLS, COLS, COLS), :], pair_ref[tail_pixels(t), :]], axis=0).T
+            state_ref[t] = x
+            norm_ref[i, :, 128 * half : 128 * half + 128] = normalized(x)
+        return carry
+
+    project(state_ref, w_cat, edge_ref, norm_ref, mix_ref, send_ref, prepare)
 
 
 def gate_kernel(layer):
@@ -126,15 +137,10 @@
         else:
             gate_ref, outcat_ref = refs
         outcat_ref[...] = stacked(outw_ref[layer].T, 1)
-        cat = stacked(gatew_ref[layer], 0)
-
-        def step(i, carry):
-            at = aligned(i * 128, 128, 128)
-            x = state_ref[at, :]
-            centred = x - jnp.mean(x, axis=-1, keepdims=True)
-            variance = jnp.mean(centred * centred, axis=-1, keepdims=True)
-            high, low = split_bf16(centred * lax.rsqrt(variance + EPS))
-            gate_ref[at, :] = jax.nn.sigmoid(matmul(jnp.concatenate([high, high, low], axis=1), cat, ((1,), (0,))))
+        cat = stacked(gatew_ref[layer].T, 1)
+
+        def step(t, carry):
+            gate_ref[t] = jax.nn.sigmoid(matmul(cat, normalized(state_ref[t]), ((1,), (0,))))
             return carry
 
         lax.fori_loop(0, PACK, step, 0, unroll=3)
@@ -290,12 +296,12 @@
 
 
 def finish(tri_ref, state_ref, gate_hbm, outcat_hbm, next_ref, scaled_ref, stat_ref, gate_ref, outcat_ref, fetch_sems,
-           done=None):
+           done=None, after=None):
     fetches = [
         pltpu.make_async_copy(outcat_hbm, outcat_ref, fetch_sems.at[0]),
         pltpu.make_async_copy(gate_hbm, gate_ref, fetch_sems.at[1]),
     ]
-    for fetch in fetches:
+    for fetch in fetches + ([after] if after is not None else []):
         fetch.start()
 
     def stats(i, carry):
@@ -337,11 +343,13 @@
         values = matmul(w_cat, jnp.concatenate([high, high, low], axis=0), ((1,), (0,)))
         for half in range(2):
             t = 2 * i + half
-            value = values[:, 128 * half : 128 * half + 128].T
-            at = aligned(t * COLS, COLS, COLS)
-            next_ref[at, :] = state_ref[at, :] + gate_ref[at, :] * value[:COLS]
-            at = tail_pixels(t)
-            next_ref[at, :] = state_ref[at, :] + gate_ref[at, :] * value[COLS:]
+            value = state_ref[t] + gate_ref[t] * values[:, 128 * half : 128 * half + 128]
+            if done is None:
+                next_ref[t] = value
+            else:
+                value = value.T
+                next_ref[aligned(t * COLS, COLS, COLS), :] = value[:COLS]
+                next_ref[tail_pixels(t), :] = value[COLS:]
         return carry
 
     if done is None:
@@ -357,8 +365,7 @@
 def middle_kernel(edge_ref, tri_ref, state_ref, gate_hbm, outcat_hbm, projcat_hbm, next_ref, send_ref,
                   projcat_ref, sems, norm_ref, mix_ref, *scratch):
     fetch = pltpu.make_async_copy(projcat_hbm, projcat_ref, sems.at[0])
-    fetch.start()
-    finish(tri_ref, state_ref, gate_hbm, outcat_hbm, next_ref, *scratch)
+    finish(tri_ref, state_ref, gate_hbm, outcat_hbm, next_ref, *scratch, after=fetch)
     fetch.wait()
     project(next_ref, projcat_ref[...], edge_ref, norm_ref, mix_ref, send_ref)
 
@@ -379,16 +386,16 @@
 VM = pl.BlockSpec(memory_space=pltpu.VMEM)
 SM = pl.BlockSpec(memory_space=pltpu.SMEM)
 HB = pl.BlockSpec(memory_space=pltpu.HBM)
-STATE = pltpu.VMEM((PIX, CH), F32)
+STATE = pltpu.VMEM((PACK, CH, 128), F32)
 SEND = pltpu.VMEM((CH * 2 * PACK, 128), BF16)
 TRI = pltpu.HBM((CH * PACK, 128), BF16)
-GATE = pltpu.HBM((PIX, CH), F32)
+GATE = pltpu.HBM((PACK, CH, 128), F32)
 EDGE = pltpu.VMEM((PACK, 128), F32)
 OUTCAT = pltpu.HBM((CH, 3 * CH), BF16)
 PROJCAT = pltpu.HBM((4 * CH, 3 * CH), BF16)
-PROJECT_SCRATCH = [pltpu.VMEM((PACK * 128, 384), BF16), pltpu.VMEM((CH * 2 * PACK, 128), F32)]
+PROJECT_SCRATCH = [pltpu.VMEM((PACK // 2, 384, 256), BF16), pltpu.VMEM((CH * 2 * PACK, 128), F32)]
 FINISH_SCRATCH = [
-    pltpu.VMEM((CH * PACK, 128), F32), pltpu.VMEM((2, 72, 128), F32), pltpu.VMEM((PIX, CH), F32),
+    pltpu.VMEM((CH * PACK, 128), F32), pltpu.VMEM((2, 72, 128), F32), pltpu.VMEM((PACK, CH, 128), F32),
     pltpu.VMEM((CH, 3 * CH), BF16), pltpu.SemaphoreType.DMA((2,)),
 ]
 SEND_SCRATCH = [
@@ -438,10 +445,9 @@
 
 
 def on_device(pair, residue_mask, hotspot, interface, proj_weight, gate_weight, out_weight):
-    state = pair.reshape(PIX, CH)
-    send, edge = call(
-        first_kernel, (SEND, EDGE),
-        (far(residue_mask), far(hotspot), far(interface), far(state), far(proj_weight)),
+    send, edge, state = call(
+        first_kernel, (SEND, EDGE, STATE),
+        (far(residue_mask), far(hotspot), far(interface), far(pair.reshape(PIX, CH)), far(proj_weight)),
         [pltpu.SMEM((768,), jnp.int32), pltpu.SMEM((768,), jnp.int32), pltpu.VMEM((ROWS, COLS), jnp.int32),
          pltpu.VMEM((ROWS, 128), jnp.int32), pltpu.VMEM((PIX, CH), F32), pltpu.VMEM((CH, 4 * CH), F32),
          pltpu.SemaphoreType.DMA((5,))] + PROJECT_SCRATCH,

time: 171 us -> 169 us (0.988)
  Pallas kernels: 33.6 us -> 30.3 us
    pallas_call x9, Pallas kernels: 33.6 us -> 30.3 us  [call(): pl.pallas_call(kernel, out_shape=out_shape, in_specs=specs or [VM] * len(...]
  transfers between devices with their start and end apart: 4 -> 4, of which waited for: 4 -> 4; matrix products, arithmetic and copies ran while one was open for 0% -> 0% of each run, Pallas kernels for 7% -> 6%
where the time goes in v5:
time: 169 us
  blocking collectives  87.4 us (52%)
  waiting for transfers between devices  37.9 us (22%)
  Pallas kernels  30.3 us (18%)
  starting transfers between devices  13.2 us (8%)
    all_to_all x2, blocking collectives, exchange(): lax.all_to_all(message.reshape(CH, rows // 2, 2, 128), CHIPS, split_axis=...  87.4 us
    all_to_all x2, waiting for transfers between devices, exchange(): lax.all_to_all(message.reshape(CH, rows // 2, 2, 128), CHIPS, split_axis=...  36.4 us
    pallas_call x9, Pallas kernels, call(): pl.pallas_call(kernel, out_shape=out_shape, in_specs=specs or [VM] * len(...  30.3 us
    all_to_all x2, starting transfers between devices, exchange(): lax.all_to_all(message.reshape(CH, rows // 2, 2, 128), CHIPS, split_axis=...  13.2 us
  transfers between devices with their start and end apart: 4, of which 4 were waited for; matrix products, arithmetic and copies ran while one was open for 0% of the time, Pallas kernels for 6%

profile of v5, /device:TPU:6, one launch (start us, length us, event | category | flops | bytes accessed | tf_op | source)
XLA Modules:
  0.0 169.1 jit_solution(17076858877361141274)
XLA Ops:
  0.0 4.2 %shard_map.73 = (bf16[4608,128]{1,0:T(8,128)(2,1)S(1)}, f32[18,128]{1,0:T(8,128)S(1)}, f32[18,128,128]{2,1,0:T(8,128)S(1)}) custom-call(s32[768]{0:T(1024)} %mask_hbm.1, s32[768]{0:T(1024)} %hot_hbm.1, s32[24,96]{1,0:T(8,128)} %inter_hbm.1, f32[2304,128]{1,0:T(8,128)} %bitcast.19, f32[2,128,512]{2,1,0:T(8,128)} %refs_0_.1), custom_call_target="tpu_custom_call" | custom-call | tf_op jit(solution)/shard_map/pallas_call | solution.py:414
  4.3 48.6 %all_to_all.20 = bf16[128,18,2,128]{3,2,1,0:T(2,128)(2,1)S(1)} all-to-all(bf16[128,18,2,128]{3,2,1,0:T(2,128)(2,1)S(1)} %bitcast.17), channel_id=1, replica_groups=mesh['z'=8,'yl'=2,'core'=2,'x'=4,'yh'=2] {'z','yl','x','yh'}, dimensions={0} | all-to-all | bytes 2359296 | tf_op jit(solution)/shard_map/all_to_all | solution.py:434
  52.8 0.0 collective-permute-start
  52.8 1.7 %shard_map.74 = (bf16[384,1024]{1,0:T(8,128)(2,1)S(1)}, f32[1024,1024]{1,0:T(8,128)S(1)}) custom-call(bf16[4608,128]{1,0:T(8,128)(2,1)S(1)} %bitcast.11), custom_call_target="tpu_custom_call" | custom-call | tf_op jit(solution)/shard_map/pallas_call | solution.py:414
  54.6 1.1 collective-permute-done.other_ref
  55.7 4.1 %shard_map.75 = (bf16[2304,128]{1,0:T(8,128)(2,1)}, f32[1024,1024]{1,0:T(8,128)S(1)}) custom-call(bf16[384,1024]{1,0:T(8,128)(2,1)S(1)} %get-tuple-element.20.left_ref, f32[1024,1024]{1,0:T(8,128)S(1)} %get-tuple-element.21._, bf16[4608,128]{1,0:T(8,128)(2,1)S(1)} %collective-permute-done.other_ref), custom_call_target="tpu_custom_call", output_to_operand_aliasing={{1}: (1, {})} | custom-call | tf_op jit(solution)/shard_map/pallas_call | solution.py:414
  59.8 0.0 copy-start
  59.8 0.0 copy-start.1
  59.8 0.0 copy-start.2
  59.8 6.6 %all-to-all-start.1 = ((bf16[128,9,2,128]{3,2,1,0:T(2,128)(2,1)}), bf16[128,9,2,128]{3,2,1,0:T(2,128)(2,1)S(1)}, u32[]{:S(2)}, u32[]{:S(2)}) async-start(bf16[128,9,2,128]{3,2,1,0:T(2,128)(2,1)} %bitcast.20), calls=%async_computation.1 | async-start | bytes 1179648 | tf_op jit(solution)/shard_map/all_to_all | solution.py:434
  66.4 0.0 copy-done
  66.4 0.0 copy-done.1
  66.5 3.0 %shard_map.76 = (f32[18,128,128]{2,1,0:T(8,128)}, bf16[128,384]{1,0:T(8,128)(2,1)}, bf16[512,384]{1,0:T(8,128)(2,1)}) custom-call(f32[18,128,128]{2,1,0:T(8,128)S(1)} %get-tuple-element.23.state_ref, f32[2,128,128]{2,1,0:T(8,128)S(1)} %copy-done.1, f32[2,128,128]{2,1,0:T(8,128)S(1)} %copy-done.2, f32[2,128,512]{2,1,0:T(8,128)S(1)} %copy-done), custom_call_target="tpu_custom_call" | custom-call | flops 226492416 | bytes 2359296 | tf_op jit(solution)/shard_map/pallas_call | solution.py:414
  69.5 18.2 %all-to-all-done.1 = bf16[128,9,2,128]{3,2,1,0:T(2,128)(2,1)S(1)} async-done(((bf16[128,9,2,128]{3,2,1,0:T(2,128)(2,1)}), bf16[128,9,2,128]{3,2,1,0:T(2,128)(2,1)S(1)}, u32[]{:S(2)}, u32[]{:S(2)}) %all-to-all-start.1) | async-done | bytes 589856 | tf_op jit(solution)/shard_map/all_to_all | solution.py:434
  87.6 4.7 %shard_map.77 = (f32[18,128,128]{2,1,0:T(8,128)S(1)}, bf16[4608,128]{1,0:T(8,128)(2,1)S(1)}) custom-call(f32[18,128]{1,0:T(8,128)S(1)} %get-tuple-element.18.edge_ref, bf16[2304,128]{1,0:T(8,128)(2,1)S(1)} %bitcast.14, f32[18,128,128]{2,1,0:T(8,128)S(1)} %get-tuple-element.23.state_ref, f32[18,128,128]{2,1,0:T(8,128)} %get-tuple-element.24.gate_hbm, ...), custom_call_target="tpu_custom_call" | custom-call | tf_op jit(solution)/shard_map/pallas_call | solution.py:414
  92.3 38.9 %all_to_all.21 = bf16[128,18,2,128]{3,2,1,0:T(2,128)(2,1)S(1)} all-to-all(bf16[128,18,2,128]{3,2,1,0:T(2,128)(2,1)S(1)} %bitcast.16), channel_id=1, replica_groups=mesh['z'=8,'yl'=2,'core'=2,'x'=4,'yh'=2] {'z','yl','x','yh'}, dimensions={0} | all-to-all | bytes 2359296 | tf_op jit(solution)/shard_map/all_to_all | solution.py:434
  131.1 0.0 collective-permute-start.1
  131.2 2.5 %shard_map.78.part_ref = f32[8,384,128]{2,1,0:T(8,128)S(1)} custom-call(bf16[4608,128]{1,0:T(8,128)(2,1)S(1)} %bitcast.13), custom_call_target="tpu_custom_call" | custom-call | tf_op jit(solution)/shard_map/pallas_call | solution.py:414
  133.6 0.4 collective-permute-done.1.other_ref
  134.0 4.3 %shard_map.79 = bf16[2304,128]{1,0:T(8,128)(2,1)} custom-call(f32[8,384,128]{2,1,0:T(8,128)S(1)} %shard_map.78.part_ref, bf16[4608,128]{1,0:T(8,128)(2,1)S(1)} %collective-permute-done.1.other_ref), custom_call_target="tpu_custom_call" | custom-call | tf_op jit(solution)/shard_map/pallas_call | solution.py:414
  138.3 6.5 %all-to-all-start.3 = ((bf16[128,9,2,128]{3,2,1,0:T(2,128)(2,1)}), bf16[128,9,2,128]{3,2,1,0:T(2,128)(2,1)S(1)}, u32[]{:S(2)}, u32[]{:S(2)}) async-start(bf16[128,9,2,128]{3,2,1,0:T(2,128)(2,1)} %bitcast.18), calls=%async_computation.3 | async-start | bytes 1179648 | tf_op jit(solution)/shard_map/all_to_all | solution.py:434
  144.9 3.0 %shard_map.80 = (f32[18,128,128]{2,1,0:T(8,128)}, bf16[128,384]{1,0:T(8,128)(2,1)}) custom-call(f32[18,128,128]{2,1,0:T(8,128)S(1)} %get-tuple-element.28.state_ref, f32[2,128,128]{2,1,0:T(8,128)S(1)} %copy-done.1, f32[2,128,128]{2,1,0:T(8,128)S(1)} %copy-done.2), custom_call_target="tpu_custom_call" | custom-call | flops 226492416 | bytes 2359296 | tf_op jit(solution)/shard_map/pallas_call | solution.py:414
  147.9 18.3 %all-to-all-done.3 = bf16[128,9,2,128]{3,2,1,0:T(2,128)(2,1)S(1)} async-done(((bf16[128,9,2,128]{3,2,1,0:T(2,128)(2,1)}), bf16[128,9,2,128]{3,2,1,0:T(2,128)(2,1)S(1)}, u32[]{:S(2)}, u32[]{:S(2)}) %all-to-all-start.3) | async-done | bytes 589856 | tf_op jit(solution)/shard_map/all_to_all | solution.py:434
  166.1 2.8 %shard_map.81 = f32[2304,128]{1,0:T(8,128)} custom-call(bf16[2304,128]{1,0:T(8,128)(2,1)S(1)} %bitcast.15, f32[18,128,128]{2,1,0:T(8,128)S(1)} %get-tuple-element.28.state_ref, f32[18,128,128]{2,1,0:T(8,128)} %get-tuple-element.29.gate_hbm, bf16[128,384]{1,0:T(8,128)(2,1)} %get-tuple-element.30.outcat_hbm), custom_call_target="tpu_custom_call" | custom-call | tf_op jit(solution)/shard_map/pallas_call | solution.py:414
  (1 shorter events, 0.0 us)
Async XLA Ops:
  52.8 2.8 %collective-permute-start = (bf16[4608,128]{1,0:T(8,128)(2,1)S(1)}, bf16[4608,128]{1,0:T(8,128)(2,1)S(1)}, u32[]{:S(2)}, u32[]{:S(2)}) collective-permute-start(bf16[4608,128]{1,0:T(8,128)(2,1)S(1)} %bitcast.10), channel_id=1, source_target_pairs={{0,8},{8,0},{1,9},{9,1},{2,10},{10,2},{3,11},{11,3},{4,12},{12,4},... | collective-permute-start | bytes 3538952 | tf_op jit(solution)/shard_map/ppermute | solution.py:439
  59.8 6.7 %copy-start = (f32[2,128,512]{2,1,0:T(8,128)S(1)}, f32[2,128,512]{2,1,0:T(8,128)}, u32[]{:S(2)}) copy-start(f32[2,128,512]{2,1,0:T(8,128)} %refs_0_.1) | copy-start | bytes 1572868
  59.8 6.7 %copy-start.1 = (f32[2,128,128]{2,1,0:T(8,128)S(1)}, f32[2,128,128]{2,1,0:T(8,128)}, u32[]{:S(2)}) copy-start(f32[2,128,128]{2,1,0:T(8,128)} %gatew_ref.3) | copy-start | bytes 393220
  59.8 6.7 %copy-start.2 = (f32[2,128,128]{2,1,0:T(8,128)S(1)}, f32[2,128,128]{2,1,0:T(8,128)}, u32[]{:S(2)}) copy-start(f32[2,128,128]{2,1,0:T(8,128)} %outw_ref.3) | copy-start | bytes 393220
  59.8 27.8 %all-to-all-start.1 = ((bf16[128,9,2,128]{3,2,1,0:T(2,128)(2,1)}), bf16[128,9,2,128]{3,2,1,0:T(2,128)(2,1)S(1)}, u32[]{:S(2)}, u32[]{:S(2)}) async-start(bf16[128,9,2,128]{3,2,1,0:T(2,128)(2,1)} %bitcast.20), calls=%async_computation.1 | async-start | bytes 1179648 | tf_op jit(solution)/shard_map/all_to_all | solution.py:434
  131.1 2.8 %collective-permute-start.1 = (bf16[4608,128]{1,0:T(8,128)(2,1)S(1)}, bf16[4608,128]{1,0:T(8,128)(2,1)S(1)}, u32[]{:S(2)}, u32[]{:S(2)}) collective-permute-start(bf16[4608,128]{1,0:T(8,128)(2,1)S(1)} %bitcast.12), channel_id=1, source_target_pairs={{0,8},{8,0},{1,9},{9,1},{2,10},{10,2},{3,11},{11,3},{4,12},{12,4},... | collective-permute-start | bytes 3538952 | tf_op jit(solution)/shard_map/ppermute | solution.py:439
  138.3 27.8 %all-to-all-start.3 = ((bf16[128,9,2,128]{3,2,1,0:T(2,128)(2,1)}), bf16[128,9,2,128]{3,2,1,0:T(2,128)(2,1)S(1)}, u32[]{:S(2)}, u32[]{:S(2)}) async-start(bf16[128,9,2,128]{3,2,1,0:T(2,128)(2,1)} %bitcast.18), calls=%async_computation.3 | async-start | bytes 1179648 | tf_op jit(solution)/shard_map/all_to_all | solution.py:434

commit v6 on v5

--- a/solution.py
+++ b/solution.py
@@ -78,14 +78,18 @@
 
     lax.fori_loop(0, PACK // 2, normalize or prepare, 0, unroll=3)
 
+    w_value = jnp.concatenate([w_cat[:CH], w_cat[2 * CH : 3 * CH]], axis=0)
+    w_gate = jnp.concatenate([w_cat[CH : 2 * CH, : 2 * CH], w_cat[3 * CH :, : 2 * CH]], axis=0)
+
     def pair(i, carry):
-        values = matmul(w_cat, norm_ref[i], ((1,), (0,)))
+        values = matmul(w_value, norm_ref[i], ((1,), (0,)))
+        gates = matmul(w_gate, norm_ref[i, 0 : 2 * CH, :], ((1,), (0,)))
         for half in range(2):
             t = 2 * i + half
-            part = values[:, 128 * half : 128 * half + 128]
+            at = slice(128 * half, 128 * half + 128)
             edge = edge_ref[pl.ds(t, 1), :]
-            left = edge * jax.nn.sigmoid(part[CH : 2 * CH]) * part[:CH]
-            right = edge * jax.nn.sigmoid(part[3 * CH :]) * part[2 * CH : 3 * CH]
+            left = edge * jax.nn.sigmoid(gates[:CH, at]) * values[:CH, at]
+            right = edge * jax.nn.sigmoid(gates[CH:, at]) * values[CH:, at]
             mix_ref[pl.ds(t, CH, stride=2 * PACK), :] = left
             mix_ref[pl.ds(t + PACK, CH, stride=2 * PACK), :] = right
         return carry
@@ -261,24 +265,38 @@
 def incoming_half(source_ref, wide_ref, left_ref, right_ref, turn_ref, turned_ref):
     core = lax.axis_index("core")
     widen(source_ref, wide_ref)
+    lane = lanes((8, 128))
+    keep = lax.broadcasted_iota(jnp.int32, (8, 128), 0) < 6
 
     def step(b, carry):
+        at = aligned(8 * b, 8, 8)
         for g in range(8):
-            at = slice(128 * g, 128 * g + 128)
+            column = slice(128 * g, 128 * g + 128)
             message = PAD + (b * 8 + g) * 2 * PACK
-            place(wide_ref, message, left_ref, b * 24, at, False)
-            place(wide_ref, message + PACK, right_ref, b * 24, at, False)
+            for p in range(3):
+                left_ref[g, p, at, :] = wide_ref[pl.ds(message + 6 * p, 8), :]
+            right = [wide_ref[pl.ds(message + PACK + 6 * p, 8), :] for p in range(3)]
+            tail = jnp.where(lane < 64, pltpu.roll(right[1], 64, 1), pltpu.roll(right[2], 96, 1))
+            right.append(jnp.where(lane < 32, pltpu.roll(right[0], 32, 1), tail))
+            for p in range(4):
+                right_ref[p, at, column] = jnp.where(keep, right[p], 0.0)
         return carry
 
     lax.fori_loop(0, 16, step, 0, unroll=2)
     for z in range(8):
-        turn_ref[z % 2] = left_ref[:, 128 * z : 128 * z + 128].T
+        slot = z % 2
+        for p in range(3):
+            turned = left_ref[z, p].T
+            turn_ref[slot, p] = turned
+            turn_ref[slot, 3, 32 * p : 32 * p + 32, :] = turned[COLS:]
         for y in range(2):
             rows = slice(48 * z + 24 * y, 48 * z + 24 * y + 24)
-            turned_ref[rows, :] = turn_ref[z % 2, aligned(48 * y + 24 * core, 24, 8), :]
+            for p in range(4):
+                turned_ref[rows, 128 * p : 128 * p + 128] = turn_ref[slot, p, aligned(48 * y + 24 * core, 24, 8), :]
     left = turned_ref[...].astype(BF16)
     for n in range(4):
-        tri = matmul(left, right_ref[:, 256 * n : 256 * n + 256].astype(BF16), ((1,), (0,)))
+        right = right_ref[:, :, 256 * n : 256 * n + 256].reshape(512, 256).astype(BF16)
+        tri = matmul(left, right, ((1,), (0,)))
         yield 2 * n, tri[:, 0:128]
         yield 2 * n + 1, tri[:, 128:256]
 
@@ -306,7 +324,9 @@
 
     def stats(i, carry):
         total, square = carry
-        t = tri_ref[aligned(i * 144, 144, 144), :].astype(F32)
+        at = aligned(i * 144, 144, 144)
+        t = tri_ref[at, :].astype(F32)
+        scaled_ref[at, :] = t
         first, second = t[0:72], t[72:144]
         return total + first + second, square + first * first + second * second
 
@@ -320,24 +340,18 @@
 
     average = gather(0)
     scale = lax.rsqrt(gather(1) - average * average + EPS)
-    for q in range(4):
-        stat_ref[0, 18 * q : 18 * q + 18, :] = average
-        stat_ref[1, 18 * q : 18 * q + 18, :] = scale
-
-    def rescale(i, carry):
-        t = tri_ref[aligned(i * 144, 144, 144), :].astype(F32)
-        for half in range(2):
-            part = (t[72 * half : 72 * half + 72] - stat_ref[0, 0:72, :]) * stat_ref[1, 0:72, :]
-            scaled_ref[aligned(i * 144 + 72 * half, 72, 72), :] = part
-        return carry
-
-    lax.fori_loop(0, 16, rescale, 0)
+    stat_ref[0, 0:18, :] = average
+    stat_ref[1, 0:18, :] = scale
     for fetch in fetches:
         fetch.wait()
     w_cat = outcat_ref[...]
 
     def combine(i, carry):
-        pieces = [split_bf16(scaled_ref[pl.ds(2 * i + half, CH, stride=PACK), :]) for half in range(2)]
+        pieces = []
+        for half in range(2):
+            t = 2 * i + half
+            centred = scaled_ref[pl.ds(t, CH, stride=PACK), :] - stat_ref[0, pl.ds(t, 1), :]
+            pieces.append(split_bf16(centred * stat_ref[1, pl.ds(t, 1), :]))
         high = jnp.concatenate([pieces[0][0], pieces[1][0]], axis=1)
         low = jnp.concatenate([pieces[0][1], pieces[1][1]], axis=1)
         values = matmul(w_cat, jnp.concatenate([high, high, low], axis=0), ((1,), (0,)))
@@ -405,7 +419,10 @@
 WIDE = pltpu.VMEM((CH * 2 * PACK + 16, 128), F32)
 HALF = pltpu.VMEM((384, 1024), F32)
 RIGHT = pltpu.VMEM((1024, 1024), F32)
-HALF_SCRATCH = [WIDE, HALF, HALF, pltpu.VMEM((2, 128, 384), F32), pltpu.VMEM((384, 384), F32)]
+HALF_SCRATCH = [
+    WIDE, pltpu.VMEM((8, 3, 128, 128), F32), pltpu.VMEM((4, 128, 1024), F32), pltpu.VMEM((2, 4, 128, 128), F32),
+    pltpu.VMEM((384, 512), F32),
+]
 PART = pltpu.VMEM((8, 384, 128), F32)
 
 

time: 169 us -> 169 us (level)
  no operation moved by 1% of the time
where the time goes in v6:
time: 169 us
  blocking collectives  87.4 us (52%)
  waiting for transfers between devices  38 us (22%)
  Pallas kernels  29.7 us (18%)
  starting transfers between devices  13.2 us (8%)
    all_to_all x2, blocking collectives, exchange(): lax.all_to_all(message.reshape(CH, rows // 2, 2, 128), CHIPS, split_axis=...  87.4 us
    all_to_all x2, waiting for transfers between devices, exchange(): lax.all_to_all(message.reshape(CH, rows // 2, 2, 128), CHIPS, split_axis=...  36.4 us
    pallas_call x9, Pallas kernels, call(): pl.pallas_call(kernel, out_shape=out_shape, in_specs=specs or [VM] * len(...  29.7 us
    all_to_all x2, starting transfers between devices, exchange(): lax.all_to_all(message.reshape(CH, rows // 2, 2, 128), CHIPS, split_axis=...  13.2 us
  transfers between devices with their start and end apart: 4, of which 4 were waited for; matrix products, arithmetic and copies ran while one was open for 0% of the time, Pallas kernels for 6%

profile of v6, /device:TPU:6, one launch (start us, length us, event | category | flops | bytes accessed | tf_op | source)
XLA Modules:
  0.0 168.6 jit_solution(15619674640420930361)
XLA Ops:
  0.0 4.0 %shard_map.73 = (bf16[4608,128]{1,0:T(8,128)(2,1)S(1)}, f32[18,128]{1,0:T(8,128)S(1)}, f32[18,128,128]{2,1,0:T(8,128)S(1)}) custom-call(s32[768]{0:T(1024)} %mask_hbm.1, s32[768]{0:T(1024)} %hot_hbm.1, s32[24,96]{1,0:T(8,128)} %inter_hbm.1, f32[2304,128]{1,0:T(8,128)} %bitcast.19, f32[2,128,512]{2,1,0:T(8,128)} %refs_0_.1), custom_call_target="tpu_custom_call" | custom-call | tf_op jit(solution)/shard_map/pallas_call | solution.py:431
  4.0 48.6 %all_to_all.20 = bf16[128,18,2,128]{3,2,1,0:T(2,128)(2,1)S(1)} all-to-all(bf16[128,18,2,128]{3,2,1,0:T(2,128)(2,1)S(1)} %bitcast.17), channel_id=1, replica_groups=mesh['z'=8,'yl'=2,'core'=2,'x'=4,'yh'=2] {'z','yl','x','yh'}, dimensions={0} | all-to-all | bytes 2359296 | tf_op jit(solution)/shard_map/all_to_all | solution.py:451
  52.6 0.0 collective-permute-start
  52.6 1.7 %shard_map.74 = (bf16[384,1024]{1,0:T(8,128)(2,1)S(1)}, f32[1024,1024]{1,0:T(8,128)S(1)}) custom-call(bf16[4608,128]{1,0:T(8,128)(2,1)S(1)} %bitcast.11), custom_call_target="tpu_custom_call" | custom-call | tf_op jit(solution)/shard_map/pallas_call | solution.py:431
  54.3 1.1 collective-permute-done.other_ref
  55.4 4.1 %shard_map.75 = (bf16[2304,128]{1,0:T(8,128)(2,1)}, f32[1024,1024]{1,0:T(8,128)S(1)}) custom-call(bf16[384,1024]{1,0:T(8,128)(2,1)S(1)} %get-tuple-element.20.left_ref, f32[1024,1024]{1,0:T(8,128)S(1)} %get-tuple-element.21._, bf16[4608,128]{1,0:T(8,128)(2,1)S(1)} %collective-permute-done.other_ref), custom_call_target="tpu_custom_call", output_to_operand_aliasing={{1}: (1, {})} | custom-call | tf_op jit(solution)/shard_map/pallas_call | solution.py:431
  59.5 0.0 copy-start
  59.5 0.0 copy-start.1
  59.5 0.0 copy-start.2
  59.5 6.6 %all-to-all-start.1 = ((bf16[128,9,2,128]{3,2,1,0:T(2,128)(2,1)}), bf16[128,9,2,128]{3,2,1,0:T(2,128)(2,1)S(1)}, u32[]{:S(2)}, u32[]{:S(2)}) async-start(bf16[128,9,2,128]{3,2,1,0:T(2,128)(2,1)} %bitcast.20), calls=%async_computation.1 | async-start | bytes 1179648 | tf_op jit(solution)/shard_map/all_to_all | solution.py:451
  66.2 0.0 copy-done
  66.2 0.0 copy-done.1
  66.2 3.0 %shard_map.76 = (f32[18,128,128]{2,1,0:T(8,128)}, bf16[128,384]{1,0:T(8,128)(2,1)}, bf16[512,384]{1,0:T(8,128)(2,1)}) custom-call(f32[18,128,128]{2,1,0:T(8,128)S(1)} %get-tuple-element.23.state_ref, f32[2,128,128]{2,1,0:T(8,128)S(1)} %copy-done.1, f32[2,128,128]{2,1,0:T(8,128)S(1)} %copy-done.2, f32[2,128,512]{2,1,0:T(8,128)S(1)} %copy-done), custom_call_target="tpu_custom_call" | custom-call | flops 226492416 | bytes 2359296 | tf_op jit(solution)/shard_map/pallas_call | solution.py:431
  69.2 18.2 %all-to-all-done.1 = bf16[128,9,2,128]{3,2,1,0:T(2,128)(2,1)S(1)} async-done(((bf16[128,9,2,128]{3,2,1,0:T(2,128)(2,1)}), bf16[128,9,2,128]{3,2,1,0:T(2,128)(2,1)S(1)}, u32[]{:S(2)}, u32[]{:S(2)}) %all-to-all-start.1) | async-done | bytes 589856 | tf_op jit(solution)/shard_map/all_to_all | solution.py:451
  87.4 4.4 %shard_map.77 = (f32[18,128,128]{2,1,0:T(8,128)S(1)}, bf16[4608,128]{1,0:T(8,128)(2,1)S(1)}) custom-call(f32[18,128]{1,0:T(8,128)S(1)} %get-tuple-element.18.edge_ref, bf16[2304,128]{1,0:T(8,128)(2,1)S(1)} %bitcast.14, f32[18,128,128]{2,1,0:T(8,128)S(1)} %get-tuple-element.23.state_ref, f32[18,128,128]{2,1,0:T(8,128)} %get-tuple-element.24.gate_hbm, ...), custom_call_target="tpu_custom_call" | custom-call | tf_op jit(solution)/shard_map/pallas_call | solution.py:431
  91.8 38.8 %all_to_all.21 = bf16[128,18,2,128]{3,2,1,0:T(2,128)(2,1)S(1)} all-to-all(bf16[128,18,2,128]{3,2,1,0:T(2,128)(2,1)S(1)} %bitcast.16), channel_id=1, replica_groups=mesh['z'=8,'yl'=2,'core'=2,'x'=4,'yh'=2] {'z','yl','x','yh'}, dimensions={0} | all-to-all | bytes 2359296 | tf_op jit(solution)/shard_map/all_to_all | solution.py:451
  130.7 0.0 collective-permute-start.1
  130.7 2.4 %shard_map.78.part_ref = f32[8,384,128]{2,1,0:T(8,128)S(1)} custom-call(bf16[4608,128]{1,0:T(8,128)(2,1)S(1)} %bitcast.13), custom_call_target="tpu_custom_call" | custom-call | tf_op jit(solution)/shard_map/pallas_call | solution.py:431
  133.0 0.5 collective-permute-done.1.other_ref
  133.5 4.3 %shard_map.79 = bf16[2304,128]{1,0:T(8,128)(2,1)} custom-call(f32[8,384,128]{2,1,0:T(8,128)S(1)} %shard_map.78.part_ref, bf16[4608,128]{1,0:T(8,128)(2,1)S(1)} %collective-permute-done.1.other_ref), custom_call_target="tpu_custom_call" | custom-call | tf_op jit(solution)/shard_map/pallas_call | solution.py:431
  137.8 6.5 %all-to-all-start.3 = ((bf16[128,9,2,128]{3,2,1,0:T(2,128)(2,1)}), bf16[128,9,2,128]{3,2,1,0:T(2,128)(2,1)S(1)}, u32[]{:S(2)}, u32[]{:S(2)}) async-start(bf16[128,9,2,128]{3,2,1,0:T(2,128)(2,1)} %bitcast.18), calls=%async_computation.3 | async-start | bytes 1179648 | tf_op jit(solution)/shard_map/all_to_all | solution.py:451
  144.3 3.0 %shard_map.80 = (f32[18,128,128]{2,1,0:T(8,128)}, bf16[128,384]{1,0:T(8,128)(2,1)}) custom-call(f32[18,128,128]{2,1,0:T(8,128)S(1)} %get-tuple-element.28.state_ref, f32[2,128,128]{2,1,0:T(8,128)S(1)} %copy-done.1, f32[2,128,128]{2,1,0:T(8,128)S(1)} %copy-done.2), custom_call_target="tpu_custom_call" | custom-call | flops 226492416 | bytes 2359296 | tf_op jit(solution)/shard_map/pallas_call | solution.py:431
  147.3 18.2 %all-to-all-done.3 = bf16[128,9,2,128]{3,2,1,0:T(2,128)(2,1)S(1)} async-done(((bf16[128,9,2,128]{3,2,1,0:T(2,128)(2,1)}), bf16[128,9,2,128]{3,2,1,0:T(2,128)(2,1)S(1)}, u32[]{:S(2)}, u32[]{:S(2)}) %all-to-all-start.3) | async-done | bytes 589856 | tf_op jit(solution)/shard_map/all_to_all | solution.py:451
  165.5 2.9 %shard_map.81 = f32[2304,128]{1,0:T(8,128)} custom-call(bf16[2304,128]{1,0:T(8,128)(2,1)S(1)} %bitcast.15, f32[18,128,128]{2,1,0:T(8,128)S(1)} %get-tuple-element.28.state_ref, f32[18,128,128]{2,1,0:T(8,128)} %get-tuple-element.29.gate_hbm, bf16[128,384]{1,0:T(8,128)(2,1)} %get-tuple-element.30.outcat_hbm), custom_call_target="tpu_custom_call" | custom-call | tf_op jit(solution)/shard_map/pallas_call | solution.py:431
  (1 shorter events, 0.0 us)
Async XLA Ops:
  52.6 2.8 %collective-permute-start = (bf16[4608,128]{1,0:T(8,128)(2,1)S(1)}, bf16[4608,128]{1,0:T(8,128)(2,1)S(1)}, u32[]{:S(2)}, u32[]{:S(2)}) collective-permute-start(bf16[4608,128]{1,0:T(8,128)(2,1)S(1)} %bitcast.10), channel_id=1, source_target_pairs={{0,8},{8,0},{1,9},{9,1},{2,10},{10,2},{3,11},{11,3},{4,12},{12,4},... | collective-permute-start | bytes 3538952 | tf_op jit(solution)/shard_map/ppermute | solution.py:456
  59.5 6.7 %copy-start = (f32[2,128,512]{2,1,0:T(8,128)S(1)}, f32[2,128,512]{2,1,0:T(8,128)}, u32[]{:S(2)}) copy-start(f32[2,128,512]{2,1,0:T(8,128)} %refs_0_.1) | copy-start | bytes 1572868
  59.5 6.7 %copy-start.1 = (f32[2,128,128]{2,1,0:T(8,128)S(1)}, f32[2,128,128]{2,1,0:T(8,128)}, u32[]{:S(2)}) copy-start(f32[2,128,128]{2,1,0:T(8,128)} %gatew_ref.3) | copy-start | bytes 393220
  59.5 6.7 %copy-start.2 = (f32[2,128,128]{2,1,0:T(8,128)S(1)}, f32[2,128,128]{2,1,0:T(8,128)}, u32[]{:S(2)}) copy-start(f32[2,128,128]{2,1,0:T(8,128)} %outw_ref.3) | copy-start | bytes 393220
  59.5 27.8 %all-to-all-start.1 = ((bf16[128,9,2,128]{3,2,1,0:T(2,128)(2,1)}), bf16[128,9,2,128]{3,2,1,0:T(2,128)(2,1)S(1)}, u32[]{:S(2)}, u32[]{:S(2)}) async-start(bf16[128,9,2,128]{3,2,1,0:T(2,128)(2,1)} %bitcast.20), calls=%async_computation.1 | async-start | bytes 1179648 | tf_op jit(solution)/shard_map/all_to_all | solution.py:451
  130.7 2.8 %collective-permute-start.1 = (bf16[4608,128]{1,0:T(8,128)(2,1)S(1)}, bf16[4608,128]{1,0:T(8,128)(2,1)S(1)}, u32[]{:S(2)}, u32[]{:S(2)}) collective-permute-start(bf16[4608,128]{1,0:T(8,128)(2,1)S(1)} %bitcast.12), channel_id=1, source_target_pairs={{0,8},{8,0},{1,9},{9,1},{2,10},{10,2},{3,11},{11,3},{4,12},{12,4},... | collective-permute-start | bytes 3538952 | tf_op jit(solution)/shard_map/ppermute | solution.py:456
  137.8 27.8 %all-to-all-start.3 = ((bf16[128,9,2,128]{3,2,1,0:T(2,128)(2,1)}), bf16[128,9,2,128]{3,2,1,0:T(2,128)(2,1)S(1)}, u32[]{:S(2)}, u32[]{:S(2)}) async-start(bf16[128,9,2,128]{3,2,1,0:T(2,128)(2,1)} %bitcast.18), calls=%async_computation.3 | async-start | bytes 1179648 | tf_op jit(solution)/shard_map/all_to_all | solution.py:451

commit v7 on v6

--- a/solution.py
+++ b/solution.py
@@ -70,42 +70,31 @@
     return jnp.concatenate([high, high, low], axis=0)
 
 
-def project(state_ref, w_cat, edge_ref, norm_ref, mix_ref, send_ref, normalize=None):
-    def prepare(i, carry):
-        for half in range(2):
-            norm_ref[i, :, 128 * half : 128 * half + 128] = normalized(state_ref[2 * i + half])
-        return carry
-
-    lax.fori_loop(0, PACK // 2, normalize or prepare, 0, unroll=3)
-
-    w_value = jnp.concatenate([w_cat[:CH], w_cat[2 * CH : 3 * CH]], axis=0)
-    w_gate = jnp.concatenate([w_cat[CH : 2 * CH, : 2 * CH], w_cat[3 * CH :, : 2 * CH]], axis=0)
-
-    def pair(i, carry):
-        values = matmul(w_value, norm_ref[i], ((1,), (0,)))
-        gates = matmul(w_gate, norm_ref[i, 0 : 2 * CH, :], ((1,), (0,)))
+def project(source, w_cat, edge_ref, mix_ref, send_ref):
+    def group(i, carry):
+        values = matmul(w_cat, jnp.concatenate([normalized(x) for x in source(i)], axis=1), ((1,), (0,)))
         for half in range(2):
             t = 2 * i + half
-            at = slice(128 * half, 128 * half + 128)
+            part = values[:, 128 * half : 128 * half + 128]
             edge = edge_ref[pl.ds(t, 1), :]
-            left = edge * jax.nn.sigmoid(gates[:CH, at]) * values[:CH, at]
-            right = edge * jax.nn.sigmoid(gates[CH:, at]) * values[CH:, at]
+            left = edge * jax.nn.sigmoid(part[CH : 2 * CH]) * part[:CH]
+            right = edge * jax.nn.sigmoid(part[3 * CH :]) * part[2 * CH : 3 * CH]
             mix_ref[pl.ds(t, CH, stride=2 * PACK), :] = left
             mix_ref[pl.ds(t + PACK, CH, stride=2 * PACK), :] = right
         return carry
 
-    lax.fori_loop(0, PACK // 2, pair, 0, unroll=3)
+    lax.fori_loop(0, PACK // 2, group, 0, unroll=True)
 
     def convert(i, carry):
         at = aligned(i * 256, 256, 256)
         send_ref[at, :] = mix_ref[at, :].astype(BF16)
         return carry
 
-    lax.fori_loop(0, 18, convert, 0)
+    lax.fori_loop(0, 18, convert, 0, unroll=2)
 
 
 def first_kernel(mask_hbm, hot_hbm, inter_hbm, pair_hbm, proj_hbm, send_ref, edge_ref, state_ref, mask_sm, hot_sm,
-                 inter_ref, rows_ref, pair_ref, proj_ref, sems, norm_ref, mix_ref):
+                 inter_ref, rows_ref, pair_ref, proj_ref, sems, mix_ref):
     copies = [
         pltpu.make_async_copy(source, target, sems.at[n])
         for n, (source, target) in enumerate((
@@ -122,15 +111,15 @@
     w_cat = stacked(proj_ref[...].T, 1)
     copies[4].wait()
 
-    def prepare(i, carry):
+    def source(i):
         for half in range(2):
             t = 2 * i + half
-            x = jnp.concatenate([pair_ref[aligned(t * COLS, COLS, COLS), :], pair_ref[tail_pixels(t), :]], axis=0).T
+            rows = (pair_ref[aligned(t * COLS, COLS, COLS), :], pair_ref[tail_pixels(t), :])
+            x = jnp.concatenate(rows, axis=0).T
             state_ref[t] = x
-            norm_ref[i, :, 128 * half : 128 * half + 128] = normalized(x)
-        return carry
-
-    project(state_ref, w_cat, edge_ref, norm_ref, mix_ref, send_ref, prepare)
+            yield x
+
+    project(source, w_cat, edge_ref, mix_ref, send_ref)
 
 
 def gate_kernel(layer):
@@ -160,7 +149,7 @@
         wide_ref[aligned(PAD + i * 256, 256, 8), :] = source_ref[aligned(i * 256, 256, 256), :].astype(F32)
         return carry
 
-    lax.fori_loop(0, 18, step, 0)
+    lax.fori_loop(0, 18, step, 0, unroll=2)
 
 
 def unpack(wide_ref, base):
@@ -222,42 +211,48 @@
         copy.wait()
 
 
-def outgoing_own(own_ref, left_ref, right_ref, wide_ref, keep_ref):
+def outgoing_own(own_ref, left_ref, *refs):
+    right_refs, (wide_ref, keep_ref) = refs[:4], refs[4:]
     core = lax.axis_index("core")
     widen(own_ref, wide_ref)
-
-    def step(b, carry):
-        start = (b // 2) * 128 + (b % 2) * 48 + core * 24
-        for g in range(8):
-            at = slice(128 * g, 128 * g + 128)
-            message = PAD + (b * 8 + g) * 2 * PACK
-            place(wide_ref, message, keep_ref, b * 24, at, False)
-            place(wide_ref, message + PACK, right_ref, start, at, True)
-        return carry
-
-    lax.fori_loop(0, 16, step, 0, unroll=2)
-    for z in range(8):
-        right_ref[128 * z + 96 : 128 * z + 128, :] = jnp.zeros((32, 1024), F32)
+    for n, right_ref in enumerate(right_refs):
+        for z in range(2):
+            right_ref[128 * z + 96 : 128 * z + 128, :] = jnp.zeros((32, 1024), F32)
+
+        def step(c, carry):
+            b = 4 * n + c
+            start = (c // 2) * 128 + (c % 2) * 48 + core * 24
+            for g in range(8):
+                at = slice(128 * g, 128 * g + 128)
+                message = PAD + (b * 8 + g) * 2 * PACK
+                place(wide_ref, message, keep_ref, b * 24, at, False)
+                place(wide_ref, message + PACK, right_ref, start, at, True)
+            return carry
+
+        lax.fori_loop(0, 4, step, 0, unroll=2)
     left_ref[...] = keep_ref[...].astype(BF16)
 
 
-def outgoing_kernel(left_ref, _, other_ref, out_hbm, right_ref, wide_ref, tri_ref, *scratch):
+def outgoing_kernel(left_ref, _0, _1, _2, _3, other_ref, out_hbm, *refs):
+    right_refs, (wide_ref, tri_ref, *scratch) = refs[:4], refs[4:]
     core = lax.axis_index("core")
     widen(other_ref, wide_ref)
-
-    def step(b, carry):
-        start = (b // 2) * 128 + (b % 2) * 48 + 24 - core * 24
-        for g in range(8):
-            message = PAD + (b * 8 + g) * 2 * PACK
-            place(wide_ref, message + PACK, right_ref, start, slice(128 * g, 128 * g + 128), True)
-        return carry
-
-    lax.fori_loop(0, 16, step, 0, unroll=2)
     left = left_ref[...]
+
+    def fill(n):
+        for c in range(4):
+            for g in range(8):
+                message = PAD + ((4 * n + c) * 8 + g) * 2 * PACK
+                start = (c // 2) * 128 + (c % 2) * 48 + 24 - core * 24
+                place(wide_ref, message + PACK, right_refs[n], start, slice(128 * g, 128 * g + 128), True)
+
+    fill(0)
     for n in range(4):
-        tri = matmul(left, right_ref[256 * n : 256 * n + 256, :].astype(BF16), ((1,), (1,)))
-        tri_ref[2 * n, 0:384, :] = tri[:, 0:128]
-        tri_ref[2 * n + 1, 0:384, :] = tri[:, 128:256]
+        tri = matmul(left, right_refs[n][...].astype(BF16), ((1,), (1,)))
+        if n < 3:
+            fill(n + 1)
+        tri_ref[2 * n] = tri[:, 0:128]
+        tri_ref[2 * n + 1] = tri[:, 128:256]
     mix_ref, tail_ref, ready_ref, sems = scratch
     send_tri(tri_ref, mix_ref, tail_ref, ready_ref, out_hbm, sems)
 
@@ -309,17 +304,16 @@
 def incoming_kernel(part_ref, other_ref, out_hbm, wide_ref, left_ref, right_ref, turn_ref, turned_ref, tri_ref,
                     mix_ref, tail_ref, ready_ref, sems):
     for g, tri in incoming_half(other_ref, wide_ref, left_ref, right_ref, turn_ref, turned_ref):
-        tri_ref[g, 0:384, :] = part_ref[g] + tri
+        tri_ref[g] = part_ref[g] + tri
     send_tri(tri_ref, mix_ref, tail_ref, ready_ref, out_hbm, sems)
 
 
-def finish(tri_ref, state_ref, gate_hbm, outcat_hbm, next_ref, scaled_ref, stat_ref, gate_ref, outcat_ref, fetch_sems,
-           done=None, after=None):
+def finish(tri_ref, state_ref, gate_hbm, outcat_hbm, scaled_ref, stat_ref, gate_ref, outcat_ref, fetch_sems, after=()):
     fetches = [
         pltpu.make_async_copy(outcat_hbm, outcat_ref, fetch_sems.at[0]),
         pltpu.make_async_copy(gate_hbm, gate_ref, fetch_sems.at[1]),
     ]
-    for fetch in fetches + ([after] if after is not None else []):
+    for fetch in fetches + list(after):
         fetch.start()
 
     def stats(i, carry):
@@ -331,7 +325,7 @@
         return total + first + second, square + first * first + second * second
 
     zero = jnp.zeros((72, 128), F32)
-    total, square = lax.fori_loop(0, 16, stats, (zero, zero))
+    total, square = lax.fori_loop(0, 16, stats, (zero, zero), unroll=2)
     stat_ref[0, 0:72, :] = total
     stat_ref[1, 0:72, :] = square
 
@@ -346,7 +340,7 @@
         fetch.wait()
     w_cat = outcat_ref[...]
 
-    def combine(i, carry):
+    def updated(i):
         pieces = []
         for half in range(2):
             t = 2 * i + half
@@ -357,34 +351,27 @@
         values = matmul(w_cat, jnp.concatenate([high, high, low], axis=0), ((1,), (0,)))
         for half in range(2):
             t = 2 * i + half
-            value = state_ref[t] + gate_ref[t] * values[:, 128 * half : 128 * half + 128]
-            if done is None:
-                next_ref[t] = value
-            else:
-                value = value.T
-                next_ref[aligned(t * COLS, COLS, COLS), :] = value[:COLS]
-                next_ref[tail_pixels(t), :] = value[COLS:]
-        return carry
-
-    if done is None:
-        lax.fori_loop(0, PACK // 2, combine, 0, unroll=3)
-    else:
-        for n in range(3):
-            for i in range(3):
-                combine(3 * n + i, 0)
-            done(n)
-        done(3)
+            yield state_ref[t] + gate_ref[t] * values[:, 128 * half : 128 * half + 128]
+
+    return updated
 
 
 def middle_kernel(edge_ref, tri_ref, state_ref, gate_hbm, outcat_hbm, projcat_hbm, next_ref, send_ref,
-                  projcat_ref, sems, norm_ref, mix_ref, *scratch):
+                  projcat_ref, sems, mix_ref, *scratch):
     fetch = pltpu.make_async_copy(projcat_hbm, projcat_ref, sems.at[0])
-    finish(tri_ref, state_ref, gate_hbm, outcat_hbm, next_ref, *scratch, after=fetch)
+    updated = finish(tri_ref, state_ref, gate_hbm, outcat_hbm, *scratch, after=(fetch,))
     fetch.wait()
-    project(next_ref, projcat_ref[...], edge_ref, norm_ref, mix_ref, send_ref)
+
+    def source(i):
+        for half, value in enumerate(updated(i)):
+            next_ref[2 * i + half] = value
+            yield value
+
+    project(source, projcat_ref[...], edge_ref, mix_ref, send_ref)
 
 
 def last_kernel(tri_ref, state_ref, gate_hbm, outcat_hbm, out_hbm, next_ref, sems, *scratch):
+    updated = finish(tri_ref, state_ref, gate_hbm, outcat_hbm, *scratch)
     copies = []
 
     def done(n):
@@ -392,7 +379,15 @@
         copies.append(pltpu.make_async_copy(next_ref.at[at], out_hbm.at[at], sems.at[n]))
         copies[-1].start()
 
-    finish(tri_ref, state_ref, gate_hbm, outcat_hbm, next_ref, *scratch, done=done)
+    for i in range(PACK // 2):
+        for half, value in enumerate(updated(i)):
+            t = 2 * i + half
+            value = value.T
+            next_ref[t * COLS : t * COLS + COLS, :] = value[:COLS]
+            next_ref[tail_pixels(t), :] = value[COLS:]
+        if i % 3 == 2:
+            done(i // 3)
+    done(3)
     for copy in copies:
         copy.wait()
 
@@ -407,7 +402,7 @@
 EDGE = pltpu.VMEM((PACK, 128), F32)
 OUTCAT = pltpu.HBM((CH, 3 * CH), BF16)
 PROJCAT = pltpu.HBM((4 * CH, 3 * CH), BF16)
-PROJECT_SCRATCH = [pltpu.VMEM((PACK // 2, 384, 256), BF16), pltpu.VMEM((CH * 2 * PACK, 128), F32)]
+PROJECT_SCRATCH = [pltpu.VMEM((CH * 2 * PACK, 128), F32)]
 FINISH_SCRATCH = [
     pltpu.VMEM((CH * PACK, 128), F32), pltpu.VMEM((2, 72, 128), F32), pltpu.VMEM((PACK, CH, 128), F32),
     pltpu.VMEM((CH, 3 * CH), BF16), pltpu.SemaphoreType.DMA((2,)),
@@ -418,7 +413,7 @@
 ]
 WIDE = pltpu.VMEM((CH * 2 * PACK + 16, 128), F32)
 HALF = pltpu.VMEM((384, 1024), F32)
-RIGHT = pltpu.VMEM((1024, 1024), F32)
+RIGHT = (pltpu.VMEM((256, 1024), F32),) * 4
 HALF_SCRATCH = [
     WIDE, pltpu.VMEM((8, 3, 128, 128), F32), pltpu.VMEM((4, 128, 1024), F32), pltpu.VMEM((2, 4, 128, 128), F32),
     pltpu.VMEM((384, 512), F32),
@@ -472,10 +467,10 @@
     )
     own = exchange(send, 2 * PACK)
     other = partner(own)
-    left, right = call(outgoing_own, (pltpu.VMEM((384, 1024), BF16), RIGHT), (near(own),), [WIDE, HALF])
-    tri, _ = call(
-        outgoing_kernel, (TRI, RIGHT), (near(left), near(right), near(other)), [WIDE] + SEND_SCRATCH,
-        out_specs=(HB, VM), input_output_aliases={1: 1},
+    left, *right = call(outgoing_own, (pltpu.VMEM((384, 1024), BF16),) + RIGHT, (near(own),), [WIDE, HALF])
+    tri, *_ = call(
+        outgoing_kernel, (TRI,) + RIGHT, (near(left), *map(near, right), near(other)), [WIDE] + SEND_SCRATCH,
+        out_specs=(HB, VM, VM, VM, VM), input_output_aliases={1: 1, 2: 2, 3: 3, 4: 4},
     )
     tri = exchange(tri, PACK)
     gate, outcat, projcat = gating(0, (GATE, OUTCAT, PROJCAT), near(state), gate_weight, out_weight, proj_weight)

time: 169 us -> 167 us (0.988)
  Pallas kernels: 29.7 us -> 27.8 us
    pallas_call x9, Pallas kernels: 29.7 us -> 27.8 us  [call(): pl.pallas_call(kernel, out_shape=out_shape, in_specs=specs or [VM] * len(...]
where the time goes in v7:
time: 167 us
  blocking collectives  87.4 us (52%)
  waiting for transfers between devices  38.1 us (23%)
  Pallas kernels  27.8 us (17%)
  starting transfers between devices  13.2 us (8%)
    all_to_all x2, blocking collectives, exchange(): lax.all_to_all(message.reshape(CH, rows // 2, 2, 128), CHIPS, split_axis=...  87.4 us
    all_to_all x2, waiting for transfers between devices, exchange(): lax.all_to_all(message.reshape(CH, rows // 2, 2, 128), CHIPS, split_axis=...  36.4 us
    pallas_call x9, Pallas kernels, call(): pl.pallas_call(kernel, out_shape=out_shape, in_specs=specs or [VM] * len(...  27.8 us
    all_to_all x2, starting transfers between devices, exchange(): lax.all_to_all(message.reshape(CH, rows // 2, 2, 128), CHIPS, split_axis=...  13.2 us
  transfers between devices with their start and end apart: 4, of which 4 were waited for; matrix products, arithmetic and copies ran while one was open for 0% of the time, Pallas kernels for 6%

profile of v7, /device:TPU:6, one launch (start us, length us, event | category | flops | bytes accessed | tf_op | source)
XLA Modules:
  0.0 166.8 jit_solution(11080302423981238226)
XLA Ops:
  0.0 3.1 %shard_map.73 = (bf16[4608,128]{1,0:T(8,128)(2,1)S(1)}, f32[18,128]{1,0:T(8,128)S(1)}, f32[18,128,128]{2,1,0:T(8,128)S(1)}) custom-call(s32[768]{0:T(1024)} %mask_hbm.1, s32[768]{0:T(1024)} %hot_hbm.1, s32[24,96]{1,0:T(8,128)} %inter_hbm.1, f32[2304,128]{1,0:T(8,128)} %bitcast.19, f32[2,128,512]{2,1,0:T(8,128)} %refs_0_.1), custom_call_target="tpu_custom_call" | custom-call | tf_op jit(solution)/shard_map/pallas_call | solution.py:426
  3.1 48.6 %all_to_all.20 = bf16[128,18,2,128]{3,2,1,0:T(2,128)(2,1)S(1)} all-to-all(bf16[128,18,2,128]{3,2,1,0:T(2,128)(2,1)S(1)} %bitcast.17), channel_id=1, replica_groups=mesh['z'=8,'yl'=2,'core'=2,'x'=4,'yh'=2] {'z','yl','x','yh'}, dimensions={0} | all-to-all | bytes 2359296 | tf_op jit(solution)/shard_map/all_to_all | solution.py:446
  51.7 0.0 collective-permute-start
  51.7 1.6 shard_map.74
  53.4 1.2 collective-permute-done.other_ref
  54.6 3.3 %shard_map.75 = (bf16[2304,128]{1,0:T(8,128)(2,1)}, f32[256,1024]{1,0:T(8,128)S(1)}, f32[256,1024]{1,0:T(8,128)S(1)}, f32[256,1024]{1,0:T(8,128)S(1)}, f32[256,1024]{1,0:T(8,128)S(1)}) custom-call(bf16[384,1024]{1,0:T(8,128)(2,1)S(1)} %get-tuple-element.23.left_ref, ...), custom_call_target="tpu_custom_call", output_to_operand_aliasing={{1}: (1, {}), {2}: (2, {}), {3}: (3, {}), {4}: (4, {})} | custom-call | tf_op jit(solution)/shard_map/pallas_call | solution.py:426
  57.9 0.0 copy-start
  57.9 0.0 copy-start.1
  57.9 0.0 copy-start.2
  57.9 6.6 %all-to-all-start.1 = ((bf16[128,9,2,128]{3,2,1,0:T(2,128)(2,1)}), bf16[128,9,2,128]{3,2,1,0:T(2,128)(2,1)S(1)}, u32[]{:S(2)}, u32[]{:S(2)}) async-start(bf16[128,9,2,128]{3,2,1,0:T(2,128)(2,1)} %bitcast.20), calls=%async_computation.1 | async-start | bytes 1179648 | tf_op jit(solution)/shard_map/all_to_all | solution.py:446
  64.5 0.0 copy-done
  64.5 0.0 copy-done.1
  64.6 3.0 %shard_map.76 = (f32[18,128,128]{2,1,0:T(8,128)}, bf16[128,384]{1,0:T(8,128)(2,1)}, bf16[512,384]{1,0:T(8,128)(2,1)}) custom-call(f32[18,128,128]{2,1,0:T(8,128)S(1)} %get-tuple-element.29.state_ref, f32[2,128,128]{2,1,0:T(8,128)S(1)} %copy-done.1, f32[2,128,128]{2,1,0:T(8,128)S(1)} %copy-done.2, f32[2,128,512]{2,1,0:T(8,128)S(1)} %copy-done), custom_call_target="tpu_custom_call" | custom-call | flops 226492416 | bytes 2359296 | tf_op jit(solution)/shard_map/pallas_call | solution.py:426
  67.6 18.2 %all-to-all-done.1 = bf16[128,9,2,128]{3,2,1,0:T(2,128)(2,1)S(1)} async-done(((bf16[128,9,2,128]{3,2,1,0:T(2,128)(2,1)}), bf16[128,9,2,128]{3,2,1,0:T(2,128)(2,1)S(1)}, u32[]{:S(2)}, u32[]{:S(2)}) %all-to-all-start.1) | async-done | bytes 589856 | tf_op jit(solution)/shard_map/all_to_all | solution.py:446
  85.7 4.4 %shard_map.77 = (f32[18,128,128]{2,1,0:T(8,128)S(1)}, bf16[4608,128]{1,0:T(8,128)(2,1)S(1)}) custom-call(f32[18,128]{1,0:T(8,128)S(1)} %get-tuple-element.21.edge_ref, bf16[2304,128]{1,0:T(8,128)(2,1)S(1)} %bitcast.14, f32[18,128,128]{2,1,0:T(8,128)S(1)} %get-tuple-element.29.state_ref, f32[18,128,128]{2,1,0:T(8,128)} %get-tuple-element.30.gate_hbm, ...), custom_call_target="tpu_custom_call" | custom-call | tf_op jit(solution)/shard_map/pallas_call | solution.py:426
  90.1 38.9 %all_to_all.21 = bf16[128,18,2,128]{3,2,1,0:T(2,128)(2,1)S(1)} all-to-all(bf16[128,18,2,128]{3,2,1,0:T(2,128)(2,1)S(1)} %bitcast.16), channel_id=1, replica_groups=mesh['z'=8,'yl'=2,'core'=2,'x'=4,'yh'=2] {'z','yl','x','yh'}, dimensions={0} | all-to-all | bytes 2359296 | tf_op jit(solution)/shard_map/all_to_all | solution.py:446
  129.0 0.0 collective-permute-start.1
  129.0 2.3 %shard_map.78.part_ref = f32[8,384,128]{2,1,0:T(8,128)S(1)} custom-call(bf16[4608,128]{1,0:T(8,128)(2,1)S(1)} %bitcast.13), custom_call_target="tpu_custom_call" | custom-call | tf_op jit(solution)/shard_map/pallas_call | solution.py:426
  131.3 0.5 collective-permute-done.1.other_ref
  131.8 4.2 %shard_map.79 = bf16[2304,128]{1,0:T(8,128)(2,1)} custom-call(f32[8,384,128]{2,1,0:T(8,128)S(1)} %shard_map.78.part_ref, bf16[4608,128]{1,0:T(8,128)(2,1)S(1)} %collective-permute-done.1.other_ref), custom_call_target="tpu_custom_call" | custom-call | tf_op jit(solution)/shard_map/pallas_call | solution.py:426
  136.1 6.5 %all-to-all-start.3 = ((bf16[128,9,2,128]{3,2,1,0:T(2,128)(2,1)}), bf16[128,9,2,128]{3,2,1,0:T(2,128)(2,1)S(1)}, u32[]{:S(2)}, u32[]{:S(2)}) async-start(bf16[128,9,2,128]{3,2,1,0:T(2,128)(2,1)} %bitcast.18), calls=%async_computation.3 | async-start | bytes 1179648 | tf_op jit(solution)/shard_map/all_to_all | solution.py:446
  142.6 3.0 %shard_map.80 = (f32[18,128,128]{2,1,0:T(8,128)}, bf16[128,384]{1,0:T(8,128)(2,1)}) custom-call(f32[18,128,128]{2,1,0:T(8,128)S(1)} %get-tuple-element.34.state_ref, f32[2,128,128]{2,1,0:T(8,128)S(1)} %copy-done.1, f32[2,128,128]{2,1,0:T(8,128)S(1)} %copy-done.2), custom_call_target="tpu_custom_call" | custom-call | flops 226492416 | bytes 2359296 | tf_op jit(solution)/shard_map/pallas_call | solution.py:426
  145.6 18.2 %all-to-all-done.3 = bf16[128,9,2,128]{3,2,1,0:T(2,128)(2,1)S(1)} async-done(((bf16[128,9,2,128]{3,2,1,0:T(2,128)(2,1)}), bf16[128,9,2,128]{3,2,1,0:T(2,128)(2,1)S(1)}, u32[]{:S(2)}, u32[]{:S(2)}) %all-to-all-start.3) | async-done | bytes 589856 | tf_op jit(solution)/shard_map/all_to_all | solution.py:446
  163.8 2.8 %shard_map.81 = f32[2304,128]{1,0:T(8,128)} custom-call(bf16[2304,128]{1,0:T(8,128)(2,1)S(1)} %bitcast.15, f32[18,128,128]{2,1,0:T(8,128)S(1)} %get-tuple-element.34.state_ref, f32[18,128,128]{2,1,0:T(8,128)} %get-tuple-element.35.gate_hbm, bf16[128,384]{1,0:T(8,128)(2,1)} %get-tuple-element.36.outcat_hbm), custom_call_target="tpu_custom_call" | custom-call | tf_op jit(solution)/shard_map/pallas_call | solution.py:426
  (1 shorter events, 0.0 us)
Async XLA Ops:
  51.7 2.8 %collective-permute-start = (bf16[4608,128]{1,0:T(8,128)(2,1)S(1)}, bf16[4608,128]{1,0:T(8,128)(2,1)S(1)}, u32[]{:S(2)}, u32[]{:S(2)}) collective-permute-start(bf16[4608,128]{1,0:T(8,128)(2,1)S(1)} %bitcast.10), channel_id=1, source_target_pairs={{0,8},{8,0},{1,9},{9,1},{2,10},{10,2},{3,11},{11,3},{4,12},{12,4},... | collective-permute-start | bytes 3538952 | tf_op jit(solution)/shard_map/ppermute | solution.py:451
  57.9 6.7 %copy-start = (f32[2,128,512]{2,1,0:T(8,128)S(1)}, f32[2,128,512]{2,1,0:T(8,128)}, u32[]{:S(2)}) copy-start(f32[2,128,512]{2,1,0:T(8,128)} %refs_0_.1) | copy-start | bytes 1572868
  57.9 6.7 %copy-start.1 = (f32[2,128,128]{2,1,0:T(8,128)S(1)}, f32[2,128,128]{2,1,0:T(8,128)}, u32[]{:S(2)}) copy-start(f32[2,128,128]{2,1,0:T(8,128)} %gatew_ref.3) | copy-start | bytes 393220
  57.9 6.7 %copy-start.2 = (f32[2,128,128]{2,1,0:T(8,128)S(1)}, f32[2,128,128]{2,1,0:T(8,128)}, u32[]{:S(2)}) copy-start(f32[2,128,128]{2,1,0:T(8,128)} %outw_ref.3) | copy-start | bytes 393220
  57.9 27.8 %all-to-all-start.1 = ((bf16[128,9,2,128]{3,2,1,0:T(2,128)(2,1)}), bf16[128,9,2,128]{3,2,1,0:T(2,128)(2,1)S(1)}, u32[]{:S(2)}, u32[]{:S(2)}) async-start(bf16[128,9,2,128]{3,2,1,0:T(2,128)(2,1)} %bitcast.20), calls=%async_computation.1 | async-start | bytes 1179648 | tf_op jit(solution)/shard_map/all_to_all | solution.py:446
  129.0 2.8 %collective-permute-start.1 = (bf16[4608,128]{1,0:T(8,128)(2,1)S(1)}, bf16[4608,128]{1,0:T(8,128)(2,1)S(1)}, u32[]{:S(2)}, u32[]{:S(2)}) collective-permute-start(bf16[4608,128]{1,0:T(8,128)(2,1)S(1)} %bitcast.12), channel_id=1, source_target_pairs={{0,8},{8,0},{1,9},{9,1},{2,10},{10,2},{3,11},{11,3},{4,12},{12,4},... | collective-permute-start | bytes 3538952 | tf_op jit(solution)/shard_map/ppermute | solution.py:451
  136.1 27.8 %all-to-all-start.3 = ((bf16[128,9,2,128]{3,2,1,0:T(2,128)(2,1)}), bf16[128,9,2,128]{3,2,1,0:T(2,128)(2,1)S(1)}, u32[]{:S(2)}, u32[]{:S(2)}) async-start(bf16[128,9,2,128]{3,2,1,0:T(2,128)(2,1)} %bitcast.18), calls=%async_computation.3 | async-start | bytes 1179648 | tf_op jit(solution)/shard_map/all_to_all | solution.py:446

commit v8 on v7

--- a/solution.py
+++ b/solution.py
@@ -308,11 +308,11 @@
     send_tri(tri_ref, mix_ref, tail_ref, ready_ref, out_hbm, sems)
 
 
-def finish(tri_ref, state_ref, gate_hbm, outcat_hbm, scaled_ref, stat_ref, gate_ref, outcat_ref, fetch_sems, after=()):
-    fetches = [
-        pltpu.make_async_copy(outcat_hbm, outcat_ref, fetch_sems.at[0]),
-        pltpu.make_async_copy(gate_hbm, gate_ref, fetch_sems.at[1]),
-    ]
+def finish(tri_ref, state_ref, gate_ref, outcat_hbm, scaled_ref, stat_ref, outcat_ref, fetch_sems, gate_hbm=None, after=()):
+    fetches = [pltpu.make_async_copy(outcat_hbm, outcat_ref, fetch_sems.at[3])]
+    for n in range(0 if gate_hbm is None else 3):
+        at = pl.ds(6 * n, 6)
+        fetches.append(pltpu.make_async_copy(gate_hbm.at[at], gate_ref.at[at], fetch_sems.at[n]))
     for fetch in fetches + list(after):
         fetch.start()
 
@@ -336,8 +336,7 @@
     scale = lax.rsqrt(gather(1) - average * average + EPS)
     stat_ref[0, 0:18, :] = average
     stat_ref[1, 0:18, :] = scale
-    for fetch in fetches:
-        fetch.wait()
+    fetches[0].wait()
     w_cat = outcat_ref[...]
 
     def updated(i):
@@ -353,25 +352,28 @@
             t = 2 * i + half
             yield state_ref[t] + gate_ref[t] * values[:, 128 * half : 128 * half + 128]
 
-    return updated
+    return updated, fetches[1:]
 
 
 def middle_kernel(edge_ref, tri_ref, state_ref, gate_hbm, outcat_hbm, projcat_hbm, next_ref, send_ref,
-                  projcat_ref, sems, mix_ref, *scratch):
+                  projcat_ref, sems, mix_ref, gate_ref, *scratch):
     fetch = pltpu.make_async_copy(projcat_hbm, projcat_ref, sems.at[0])
-    updated = finish(tri_ref, state_ref, gate_hbm, outcat_hbm, *scratch, after=(fetch,))
-    fetch.wait()
-
-    def source(i):
+    updated, parts = finish(tri_ref, state_ref, gate_ref, outcat_hbm, *scratch, gate_hbm=gate_hbm, after=(fetch,))
+
+    def combine(i, carry):
         for half, value in enumerate(updated(i)):
             next_ref[2 * i + half] = value
-            yield value
-
-    project(source, projcat_ref[...], edge_ref, mix_ref, send_ref)
-
-
-def last_kernel(tri_ref, state_ref, gate_hbm, outcat_hbm, out_hbm, next_ref, sems, *scratch):
-    updated = finish(tri_ref, state_ref, gate_hbm, outcat_hbm, *scratch)
+        return carry
+
+    for n, part in enumerate(parts):
+        part.wait()
+        lax.fori_loop(3 * n, 3 * n + 3, combine, 0, unroll=True)
+    fetch.wait()
+    project(lambda i: (next_ref[2 * i], next_ref[2 * i + 1]), projcat_ref[...], edge_ref, mix_ref, send_ref)
+
+
+def last_kernel(tri_ref, state_ref, gate_ref, outcat_hbm, out_hbm, next_ref, sems, *scratch):
+    updated, _ = finish(tri_ref, state_ref, gate_ref, outcat_hbm, *scratch)
     copies = []
 
     def done(n):
@@ -404,8 +406,8 @@
 PROJCAT = pltpu.HBM((4 * CH, 3 * CH), BF16)
 PROJECT_SCRATCH = [pltpu.VMEM((CH * 2 * PACK, 128), F32)]
 FINISH_SCRATCH = [
-    pltpu.VMEM((CH * PACK, 128), F32), pltpu.VMEM((2, 72, 128), F32), pltpu.VMEM((PACK, CH, 128), F32),
-    pltpu.VMEM((CH, 3 * CH), BF16), pltpu.SemaphoreType.DMA((2,)),
+    pltpu.VMEM((CH * PACK, 128), F32), pltpu.VMEM((2, 72, 128), F32), pltpu.VMEM((CH, 3 * CH), BF16),
+    pltpu.SemaphoreType.DMA((4,)),
 ]
 SEND_SCRATCH = [
     pltpu.VMEM((8, 384, 128), F32), pltpu.VMEM((CH * PACK, 128), F32), pltpu.VMEM((400, 128), F32),
@@ -477,7 +479,8 @@
     state, send = call(
         middle_kernel, (STATE, SEND),
         (near(edge), near(tri), near(state), far(gate), far(outcat), far(projcat)),
-        [pltpu.VMEM((4 * CH, 3 * CH), BF16), pltpu.SemaphoreType.DMA((1,))] + PROJECT_SCRATCH + FINISH_SCRATCH,
+        [pltpu.VMEM((4 * CH, 3 * CH), BF16), pltpu.SemaphoreType.DMA((1,))] + PROJECT_SCRATCH
+        + [pltpu.VMEM((PACK, CH, 128), F32)] + FINISH_SCRATCH,
         [VM, VM, VM, HB, HB, HB],
     )
     own = exchange(send, 2 * PACK)
@@ -485,10 +488,10 @@
     part = call(incoming_own, PART, (near(own),), HALF_SCRATCH)
     tri = call(incoming_kernel, TRI, (near(part), near(other)), HALF_SCRATCH + SEND_SCRATCH, out_specs=HB)
     tri = exchange(tri, PACK)
-    gate, outcat = gating(1, (GATE, OUTCAT), near(state), gate_weight, out_weight)
+    gate, outcat = gating(1, (STATE, OUTCAT), near(state), gate_weight, out_weight)
     state = call(
-        last_kernel, jax.ShapeDtypeStruct((PIX, CH), F32), (near(tri), near(state), far(gate), far(outcat)),
-        [pltpu.VMEM((PIX, CH), F32), pltpu.SemaphoreType.DMA((4,))] + FINISH_SCRATCH, [VM, VM, HB, HB], out_specs=HB,
+        last_kernel, jax.ShapeDtypeStruct((PIX, CH), F32), (near(tri), near(state), near(gate), far(outcat)),
+        [pltpu.VMEM((PIX, CH), F32), pltpu.SemaphoreType.DMA((4,))] + FINISH_SCRATCH, [VM, VM, VM, HB], out_specs=HB,
     )
     return state.reshape(ROWS, COLS, CH)
 

time: 167 us -> 166 us (level)
  Pallas kernels: 27.8 us -> 25.9 us
    pallas_call x9, Pallas kernels: 27.8 us -> 25.9 us  [call(): pl.pallas_call(kernel, out_shape=out_shape, in_specs=specs or [VM] * len(...]
where the time goes in v8:
time: 166 us
  blocking collectives  87.4 us (53%)
  waiting for transfers between devices  38.8 us (23%)
  Pallas kernels  25.9 us (16%)
  starting transfers between devices  13.2 us (8%)
    all_to_all x2, blocking collectives, exchange(): lax.all_to_all(message.reshape(CH, rows // 2, 2, 128), CHIPS, split_axis=...  87.4 us
    all_to_all x2, waiting for transfers between devices, exchange(): lax.all_to_all(message.reshape(CH, rows // 2, 2, 128), CHIPS, split_axis=...  37.1 us
    pallas_call x9, Pallas kernels, call(): pl.pallas_call(kernel, out_shape=out_shape, in_specs=specs or [VM] * len(...  25.9 us
    all_to_all x2, starting transfers between devices, exchange(): lax.all_to_all(message.reshape(CH, rows // 2, 2, 128), CHIPS, split_axis=...  13.2 us
  transfers between devices with their start and end apart: 4, of which 4 were waited for; matrix products, arithmetic and copies ran while one was open for 0% of the time, Pallas kernels for 6%

profile of v8, /device:TPU:6, one launch (start us, length us, event | category | flops | bytes accessed | tf_op | source)
XLA Modules:
  0.0 165.6 jit_solution(13181343618554540430)
XLA Ops:
  0.0 3.1 %shard_map.73 = (bf16[4608,128]{1,0:T(8,128)(2,1)S(1)}, f32[18,128]{1,0:T(8,128)S(1)}, f32[18,128,128]{2,1,0:T(8,128)S(1)}) custom-call(s32[768]{0:T(1024)} %mask_hbm.1, s32[768]{0:T(1024)} %hot_hbm.1, s32[24,96]{1,0:T(8,128)} %inter_hbm.1, f32[2304,128]{1,0:T(8,128)} %bitcast.19, f32[2,128,512]{2,1,0:T(8,128)} %refs_0_.1), custom_call_target="tpu_custom_call" | custom-call | tf_op jit(solution)/shard_map/pallas_call | solution.py:428
  3.1 48.6 %all_to_all.20 = bf16[128,18,2,128]{3,2,1,0:T(2,128)(2,1)S(1)} all-to-all(bf16[128,18,2,128]{3,2,1,0:T(2,128)(2,1)S(1)} %bitcast.17), channel_id=1, replica_groups=mesh['z'=8,'yl'=2,'core'=2,'x'=4,'yh'=2] {'z','yl','x','yh'}, dimensions={0} | all-to-all | bytes 2359296 | tf_op jit(solution)/shard_map/all_to_all | solution.py:448
  51.7 0.0 collective-permute-start
  51.7 1.6 shard_map.74
  53.4 1.2 collective-permute-done.other_ref
  54.6 3.2 %shard_map.75 = (bf16[2304,128]{1,0:T(8,128)(2,1)}, f32[256,1024]{1,0:T(8,128)S(1)}, f32[256,1024]{1,0:T(8,128)S(1)}, f32[256,1024]{1,0:T(8,128)S(1)}, f32[256,1024]{1,0:T(8,128)S(1)}) custom-call(bf16[384,1024]{1,0:T(8,128)(2,1)S(1)} %get-tuple-element.23.left_ref, ...), custom_call_target="tpu_custom_call", output_to_operand_aliasing={{1}: (1, {}), {2}: (2, {}), {3}: (3, {}), {4}: (4, {})} | custom-call | tf_op jit(solution)/shard_map/pallas_call | solution.py:428
  57.8 0.0 copy-start
  57.8 0.0 copy-start.1
  57.8 0.0 copy-start.2
  57.8 6.6 %all-to-all-start.1 = ((bf16[128,9,2,128]{3,2,1,0:T(2,128)(2,1)}), bf16[128,9,2,128]{3,2,1,0:T(2,128)(2,1)S(1)}, u32[]{:S(2)}, u32[]{:S(2)}) async-start(bf16[128,9,2,128]{3,2,1,0:T(2,128)(2,1)} %bitcast.20), calls=%async_computation.1 | async-start | bytes 1179648 | tf_op jit(solution)/shard_map/all_to_all | solution.py:448
  64.4 0.0 copy-done
  64.5 0.0 copy-done.1
  64.5 3.0 %shard_map.76 = (f32[18,128,128]{2,1,0:T(8,128)}, bf16[128,384]{1,0:T(8,128)(2,1)}, bf16[512,384]{1,0:T(8,128)(2,1)}) custom-call(f32[18,128,128]{2,1,0:T(8,128)S(1)} %get-tuple-element.29.state_ref, f32[2,128,128]{2,1,0:T(8,128)S(1)} %copy-done.1, f32[2,128,128]{2,1,0:T(8,128)S(1)} %copy-done.2, f32[2,128,512]{2,1,0:T(8,128)S(1)} %copy-done), custom_call_target="tpu_custom_call" | custom-call | flops 226492416 | bytes 2359296 | tf_op jit(solution)/shard_map/pallas_call | solution.py:428
  67.5 18.2 %all-to-all-done.1 = bf16[128,9,2,128]{3,2,1,0:T(2,128)(2,1)S(1)} async-done(((bf16[128,9,2,128]{3,2,1,0:T(2,128)(2,1)}), bf16[128,9,2,128]{3,2,1,0:T(2,128)(2,1)S(1)}, u32[]{:S(2)}, u32[]{:S(2)}) %all-to-all-start.1) | async-done | bytes 589856 | tf_op jit(solution)/shard_map/all_to_all | solution.py:448
  85.7 3.7 %shard_map.77 = (f32[18,128,128]{2,1,0:T(8,128)S(1)}, bf16[4608,128]{1,0:T(8,128)(2,1)S(1)}) custom-call(f32[18,128]{1,0:T(8,128)S(1)} %get-tuple-element.21.edge_ref, bf16[2304,128]{1,0:T(8,128)(2,1)S(1)} %bitcast.14, f32[18,128,128]{2,1,0:T(8,128)S(1)} %get-tuple-element.29.state_ref, f32[18,128,128]{2,1,0:T(8,128)} %get-tuple-element.30.gate_hbm, ...), custom_call_target="tpu_custom_call" | custom-call | tf_op jit(solution)/shard_map/pallas_call | solution.py:428
  89.3 38.8 %all_to_all.21 = bf16[128,18,2,128]{3,2,1,0:T(2,128)(2,1)S(1)} all-to-all(bf16[128,18,2,128]{3,2,1,0:T(2,128)(2,1)S(1)} %bitcast.16), channel_id=1, replica_groups=mesh['z'=8,'yl'=2,'core'=2,'x'=4,'yh'=2] {'z','yl','x','yh'}, dimensions={0} | all-to-all | bytes 2359296 | tf_op jit(solution)/shard_map/all_to_all | solution.py:448
  128.2 0.0 collective-permute-start.1
  128.2 2.3 %shard_map.78.part_ref = f32[8,384,128]{2,1,0:T(8,128)S(1)} custom-call(bf16[4608,128]{1,0:T(8,128)(2,1)S(1)} %bitcast.13), custom_call_target="tpu_custom_call" | custom-call | tf_op jit(solution)/shard_map/pallas_call | solution.py:428
  130.5 0.5 collective-permute-done.1.other_ref
  131.0 4.2 %shard_map.79 = bf16[2304,128]{1,0:T(8,128)(2,1)} custom-call(f32[8,384,128]{2,1,0:T(8,128)S(1)} %shard_map.78.part_ref, bf16[4608,128]{1,0:T(8,128)(2,1)S(1)} %collective-permute-done.1.other_ref), custom_call_target="tpu_custom_call" | custom-call | tf_op jit(solution)/shard_map/pallas_call | solution.py:428
  135.3 6.5 %all-to-all-start.3 = ((bf16[128,9,2,128]{3,2,1,0:T(2,128)(2,1)}), bf16[128,9,2,128]{3,2,1,0:T(2,128)(2,1)S(1)}, u32[]{:S(2)}, u32[]{:S(2)}) async-start(bf16[128,9,2,128]{3,2,1,0:T(2,128)(2,1)} %bitcast.18), calls=%async_computation.3 | async-start | bytes 1179648 | tf_op jit(solution)/shard_map/all_to_all | solution.py:448
  141.8 2.3 %shard_map.80 = (f32[18,128,128]{2,1,0:T(8,128)S(1)}, bf16[128,384]{1,0:T(8,128)(2,1)}) custom-call(f32[18,128,128]{2,1,0:T(8,128)S(1)} %get-tuple-element.34.state_ref, f32[2,128,128]{2,1,0:T(8,128)S(1)} %copy-done.1, f32[2,128,128]{2,1,0:T(8,128)S(1)} %copy-done.2), custom_call_target="tpu_custom_call" | custom-call | flops 226492416 | bytes 2359296 | tf_op jit(solution)/shard_map/pallas_call | solution.py:428
  144.1 18.9 %all-to-all-done.3 = bf16[128,9,2,128]{3,2,1,0:T(2,128)(2,1)S(1)} async-done(((bf16[128,9,2,128]{3,2,1,0:T(2,128)(2,1)}), bf16[128,9,2,128]{3,2,1,0:T(2,128)(2,1)S(1)}, u32[]{:S(2)}, u32[]{:S(2)}) %all-to-all-start.3) | async-done | bytes 589856 | tf_op jit(solution)/shard_map/all_to_all | solution.py:448
  163.0 2.4 %shard_map.81 = f32[2304,128]{1,0:T(8,128)} custom-call(bf16[2304,128]{1,0:T(8,128)(2,1)S(1)} %bitcast.15, f32[18,128,128]{2,1,0:T(8,128)S(1)} %get-tuple-element.34.state_ref, f32[18,128,128]{2,1,0:T(8,128)S(1)} %get-tuple-element.35.gate_ref, bf16[128,384]{1,0:T(8,128)(2,1)} %get-tuple-element.36.outcat_hbm), custom_call_target="tpu_custom_call" | custom-call | tf_op jit(solution)/shard_map/pallas_call | solution.py:428
  (1 shorter events, 0.0 us)
Async XLA Ops:
  51.7 2.8 %collective-permute-start = (bf16[4608,128]{1,0:T(8,128)(2,1)S(1)}, bf16[4608,128]{1,0:T(8,128)(2,1)S(1)}, u32[]{:S(2)}, u32[]{:S(2)}) collective-permute-start(bf16[4608,128]{1,0:T(8,128)(2,1)S(1)} %bitcast.10), channel_id=1, source_target_pairs={{0,8},{8,0},{1,9},{9,1},{2,10},{10,2},{3,11},{11,3},{4,12},{12,4},... | collective-permute-start | bytes 3538952 | tf_op jit(solution)/shard_map/ppermute | solution.py:453
  57.8 6.7 %copy-start = (f32[2,128,512]{2,1,0:T(8,128)S(1)}, f32[2,128,512]{2,1,0:T(8,128)}, u32[]{:S(2)}) copy-start(f32[2,128,512]{2,1,0:T(8,128)} %refs_0_.1) | copy-start | bytes 1572868
  57.8 6.7 %copy-start.1 = (f32[2,128,128]{2,1,0:T(8,128)S(1)}, f32[2,128,128]{2,1,0:T(8,128)}, u32[]{:S(2)}) copy-start(f32[2,128,128]{2,1,0:T(8,128)} %gatew_ref.3) | copy-start | bytes 393220
  57.8 6.7 %copy-start.2 = (f32[2,128,128]{2,1,0:T(8,128)S(1)}, f32[2,128,128]{2,1,0:T(8,128)}, u32[]{:S(2)}) copy-start(f32[2,128,128]{2,1,0:T(8,128)} %outw_ref.3) | copy-start | bytes 393220
  57.8 27.8 %all-to-all-start.1 = ((bf16[128,9,2,128]{3,2,1,0:T(2,128)(2,1)}), bf16[128,9,2,128]{3,2,1,0:T(2,128)(2,1)S(1)}, u32[]{:S(2)}, u32[]{:S(2)}) async-start(bf16[128,9,2,128]{3,2,1,0:T(2,128)(2,1)} %bitcast.20), calls=%async_computation.1 | async-start | bytes 1179648 | tf_op jit(solution)/shard_map/all_to_all | solution.py:448
  128.2 2.8 %collective-permute-start.1 = (bf16[4608,128]{1,0:T(8,128)(2,1)S(1)}, bf16[4608,128]{1,0:T(8,128)(2,1)S(1)}, u32[]{:S(2)}, u32[]{:S(2)}) collective-permute-start(bf16[4608,128]{1,0:T(8,128)(2,1)S(1)} %bitcast.12), channel_id=1, source_target_pairs={{0,8},{8,0},{1,9},{9,1},{2,10},{10,2},{3,11},{11,3},{4,12},{12,4},... | collective-permute-start | bytes 3538952 | tf_op jit(solution)/shard_map/ppermute | solution.py:453
  135.3 27.8 %all-to-all-start.3 = ((bf16[128,9,2,128]{3,2,1,0:T(2,128)(2,1)}), bf16[128,9,2,128]{3,2,1,0:T(2,128)(2,1)S(1)}, u32[]{:S(2)}, u32[]{:S(2)}) async-start(bf16[128,9,2,128]{3,2,1,0:T(2,128)(2,1)} %bitcast.18), calls=%async_computation.3 | async-start | bytes 1179648 | tf_op jit(solution)/shard_map/all_to_all | solution.py:448

commit v9 on v8

--- a/solution.py
+++ b/solution.py
@@ -172,6 +172,11 @@
         target_ref[aligned(start + 8 * n, 8, 8), column] = part
 
 
+def turned_pair(first, second, shift):
+    both = pltpu.roll(jnp.concatenate([first, second], axis=0).astype(BF16), shift, 1).astype(F32)
+    return both[0:8], both[8:16]
+
+
 def tail_slot(half, g):
     return 8 + (half * 8 + g) * 24
 
@@ -181,12 +186,12 @@
 
     def send(i, carry):
         blocks = [(half, g, (2 * i + half) * 24) for half in range(2) for g in range(8)]
-        for half, g, base in blocks:
-            slot = tail_slot(half, g)
-            value = tri_ref[g, aligned(base + 16, 8, 8), :]
-            tail_ref[slot + 10 : slot + 18, :] = pltpu.roll(value, 32, 1)
-            tail_ref[slot + 4 : slot + 12, :] = pltpu.roll(value, 64, 1)
-            tail_ref[slot - 2 : slot + 6, :] = pltpu.roll(value, 96, 1)
+        for n in range(0, 16, 2):
+            slots = [tail_slot(half, g) for half, g, _ in blocks[n : n + 2]]
+            pair = [tri_ref[g, aligned(base + 16, 8, 8), :] for _, g, base in blocks[n : n + 2]]
+            for shift, start in ((32, 10), (64, 4), (96, -2)):
+                for slot, value in zip(slots, turned_pair(*pair, shift)):
+                    tail_ref[slot + start : slot + start + 8, :] = value
         for half, g, base in blocks:
             slot = tail_slot(half, g)
             target = ((2 * i + half) * 8 + g) * PACK
@@ -265,23 +270,27 @@
 
     def step(b, carry):
         at = aligned(8 * b, 8, 8)
-        for g in range(8):
-            column = slice(128 * g, 128 * g + 128)
-            message = PAD + (b * 8 + g) * 2 * PACK
-            for p in range(3):
-                left_ref[g, p, at, :] = wide_ref[pl.ds(message + 6 * p, 8), :]
-            right = [wide_ref[pl.ds(message + PACK + 6 * p, 8), :] for p in range(3)]
-            tail = jnp.where(lane < 64, pltpu.roll(right[1], 64, 1), pltpu.roll(right[2], 96, 1))
-            right.append(jnp.where(lane < 32, pltpu.roll(right[0], 32, 1), tail))
-            for p in range(4):
-                right_ref[p, at, column] = jnp.where(keep, right[p], 0.0)
+        for g in range(0, 8, 2):
+            right = []
+            for h in range(2):
+                message = PAD + (b * 8 + g + h) * 2 * PACK
+                for p in range(3):
+                    left_ref[g + h, p, at, :] = wide_ref[pl.ds(message + 6 * p, 8), :]
+                right.append([wide_ref[pl.ds(message + PACK + 6 * p, 8), :] for p in range(3)])
+            moved = [turned_pair(right[0][p], right[1][p], 32 + 32 * p) for p in range(3)]
+            for h in range(2):
+                column = slice(128 * (g + h), 128 * (g + h) + 128)
+                tail = jnp.where(lane < 64, moved[1][h], moved[2][h])
+                right[h].append(jnp.where(lane < 32, moved[0][h], tail))
+                for p in range(4):
+                    right_ref[p, at, column] = jnp.where(keep, right[h][p], 0.0)
         return carry
 
     lax.fori_loop(0, 16, step, 0, unroll=2)
     for z in range(8):
         slot = z % 2
         for p in range(3):
-            turned = left_ref[z, p].T
+            turned = left_ref[z, p].astype(BF16).T.astype(F32)
             turn_ref[slot, p] = turned
             turn_ref[slot, 3, 32 * p : 32 * p + 32, :] = turned[COLS:]
         for y in range(2):

time: 166 us -> 165 us (level)
  transfers between devices with their start and end apart: 4 -> 4, of which waited for: 4 -> 4; matrix products, arithmetic and copies ran while one was open for 0% -> 0% of each run, Pallas kernels for 6% -> 5%
where the time goes in v9:
time: 165 us
  blocking collectives  87.4 us (53%)
  waiting for transfers between devices  39.2 us (24%)
  Pallas kernels  24.7 us (15%)
  starting transfers between devices  13.2 us (8%)
    all_to_all x2, blocking collectives, exchange(): lax.all_to_all(message.reshape(CH, rows // 2, 2, 128), CHIPS, split_axis=...  87.4 us
    all_to_all x2, waiting for transfers between devices, exchange(): lax.all_to_all(message.reshape(CH, rows // 2, 2, 128), CHIPS, split_axis=...  37.1 us
    pallas_call x9, Pallas kernels, call(): pl.pallas_call(kernel, out_shape=out_shape, in_specs=specs or [VM] * len(...  24.7 us
    all_to_all x2, starting transfers between devices, exchange(): lax.all_to_all(message.reshape(CH, rows // 2, 2, 128), CHIPS, split_axis=...  13.2 us
  transfers between devices with their start and end apart: 4, of which 4 were waited for; matrix products, arithmetic and copies ran while one was open for 0% of the time, Pallas kernels for 5%

profile of v9, /device:TPU:6, one launch (start us, length us, event | category | flops | bytes accessed | tf_op | source)
XLA Modules:
  0.0 164.8 jit_solution(5723567135386529135)
XLA Ops:
  0.0 3.1 %shard_map.73 = (bf16[4608,128]{1,0:T(8,128)(2,1)S(1)}, f32[18,128]{1,0:T(8,128)S(1)}, f32[18,128,128]{2,1,0:T(8,128)S(1)}) custom-call(s32[768]{0:T(1024)} %mask_hbm.1, s32[768]{0:T(1024)} %hot_hbm.1, s32[24,96]{1,0:T(8,128)} %inter_hbm.1, f32[2304,128]{1,0:T(8,128)} %bitcast.19, f32[2,128,512]{2,1,0:T(8,128)} %refs_0_.1), custom_call_target="tpu_custom_call" | custom-call | tf_op jit(solution)/shard_map/pallas_call | solution.py:437
  3.1 48.6 %all_to_all.20 = bf16[128,18,2,128]{3,2,1,0:T(2,128)(2,1)S(1)} all-to-all(bf16[128,18,2,128]{3,2,1,0:T(2,128)(2,1)S(1)} %bitcast.17), channel_id=1, replica_groups=mesh['z'=8,'yl'=2,'core'=2,'x'=4,'yh'=2] {'z','yl','x','yh'}, dimensions={0} | all-to-all | bytes 2359296 | tf_op jit(solution)/shard_map/all_to_all | solution.py:457
  51.7 0.0 collective-permute-start
  51.7 1.6 shard_map.74
  53.4 1.2 collective-permute-done.other_ref
  54.6 3.0 %shard_map.75 = (bf16[2304,128]{1,0:T(8,128)(2,1)}, f32[256,1024]{1,0:T(8,128)S(1)}, f32[256,1024]{1,0:T(8,128)S(1)}, f32[256,1024]{1,0:T(8,128)S(1)}, f32[256,1024]{1,0:T(8,128)S(1)}) custom-call(bf16[384,1024]{1,0:T(8,128)(2,1)S(1)} %get-tuple-element.23.left_ref, ...), custom_call_target="tpu_custom_call", output_to_operand_aliasing={{1}: (1, {}), {2}: (2, {}), {3}: (3, {}), {4}: (4, {})} | custom-call | tf_op jit(solution)/shard_map/pallas_call | solution.py:437
  57.6 0.0 copy-start
  57.6 0.0 copy-start.1
  57.6 0.0 copy-start.2
  57.7 6.6 %all-to-all-start.1 = ((bf16[128,9,2,128]{3,2,1,0:T(2,128)(2,1)}), bf16[128,9,2,128]{3,2,1,0:T(2,128)(2,1)S(1)}, u32[]{:S(2)}, u32[]{:S(2)}) async-start(bf16[128,9,2,128]{3,2,1,0:T(2,128)(2,1)} %bitcast.20), calls=%async_computation.1 | async-start | bytes 1179648 | tf_op jit(solution)/shard_map/all_to_all | solution.py:457
  64.3 0.0 copy-done
  64.3 0.0 copy-done.1
  64.3 3.0 %shard_map.76 = (f32[18,128,128]{2,1,0:T(8,128)}, bf16[128,384]{1,0:T(8,128)(2,1)}, bf16[512,384]{1,0:T(8,128)(2,1)}) custom-call(f32[18,128,128]{2,1,0:T(8,128)S(1)} %get-tuple-element.29.state_ref, f32[2,128,128]{2,1,0:T(8,128)S(1)} %copy-done.1, f32[2,128,128]{2,1,0:T(8,128)S(1)} %copy-done.2, f32[2,128,512]{2,1,0:T(8,128)S(1)} %copy-done), custom_call_target="tpu_custom_call" | custom-call | flops 226492416 | bytes 2359296 | tf_op jit(solution)/shard_map/pallas_call | solution.py:437
  67.3 18.2 %all-to-all-done.1 = bf16[128,9,2,128]{3,2,1,0:T(2,128)(2,1)S(1)} async-done(((bf16[128,9,2,128]{3,2,1,0:T(2,128)(2,1)}), bf16[128,9,2,128]{3,2,1,0:T(2,128)(2,1)S(1)}, u32[]{:S(2)}, u32[]{:S(2)}) %all-to-all-start.1) | async-done | bytes 589856 | tf_op jit(solution)/shard_map/all_to_all | solution.py:457
  85.5 3.7 %shard_map.77 = (f32[18,128,128]{2,1,0:T(8,128)S(1)}, bf16[4608,128]{1,0:T(8,128)(2,1)S(1)}) custom-call(f32[18,128]{1,0:T(8,128)S(1)} %get-tuple-element.21.edge_ref, bf16[2304,128]{1,0:T(8,128)(2,1)S(1)} %bitcast.14, f32[18,128,128]{2,1,0:T(8,128)S(1)} %get-tuple-element.29.state_ref, f32[18,128,128]{2,1,0:T(8,128)} %get-tuple-element.30.gate_hbm, ...), custom_call_target="tpu_custom_call" | custom-call | tf_op jit(solution)/shard_map/pallas_call | solution.py:437
  89.2 38.8 %all_to_all.21 = bf16[128,18,2,128]{3,2,1,0:T(2,128)(2,1)S(1)} all-to-all(bf16[128,18,2,128]{3,2,1,0:T(2,128)(2,1)S(1)} %bitcast.16), channel_id=1, replica_groups=mesh['z'=8,'yl'=2,'core'=2,'x'=4,'yh'=2] {'z','yl','x','yh'}, dimensions={0} | all-to-all | bytes 2359296 | tf_op jit(solution)/shard_map/all_to_all | solution.py:457
  128.0 0.0 collective-permute-start.1
  128.0 1.9 %shard_map.78.part_ref = f32[8,384,128]{2,1,0:T(8,128)S(1)} custom-call(bf16[4608,128]{1,0:T(8,128)(2,1)S(1)} %bitcast.13), custom_call_target="tpu_custom_call" | custom-call | tf_op jit(solution)/shard_map/pallas_call | solution.py:437
  129.9 0.9 collective-permute-done.1.other_ref
  130.9 3.6 %shard_map.79 = bf16[2304,128]{1,0:T(8,128)(2,1)} custom-call(f32[8,384,128]{2,1,0:T(8,128)S(1)} %shard_map.78.part_ref, bf16[4608,128]{1,0:T(8,128)(2,1)S(1)} %collective-permute-done.1.other_ref), custom_call_target="tpu_custom_call" | custom-call | tf_op jit(solution)/shard_map/pallas_call | solution.py:437
  134.5 6.5 %all-to-all-start.3 = ((bf16[128,9,2,128]{3,2,1,0:T(2,128)(2,1)}), bf16[128,9,2,128]{3,2,1,0:T(2,128)(2,1)S(1)}, u32[]{:S(2)}, u32[]{:S(2)}) async-start(bf16[128,9,2,128]{3,2,1,0:T(2,128)(2,1)} %bitcast.18), calls=%async_computation.3 | async-start | bytes 1179648 | tf_op jit(solution)/shard_map/all_to_all | solution.py:457
  141.0 2.3 %shard_map.80 = (f32[18,128,128]{2,1,0:T(8,128)S(1)}, bf16[128,384]{1,0:T(8,128)(2,1)}) custom-call(f32[18,128,128]{2,1,0:T(8,128)S(1)} %get-tuple-element.34.state_ref, f32[2,128,128]{2,1,0:T(8,128)S(1)} %copy-done.1, f32[2,128,128]{2,1,0:T(8,128)S(1)} %copy-done.2), custom_call_target="tpu_custom_call" | custom-call | flops 226492416 | bytes 2359296 | tf_op jit(solution)/shard_map/pallas_call | solution.py:437
  143.3 18.9 %all-to-all-done.3 = bf16[128,9,2,128]{3,2,1,0:T(2,128)(2,1)S(1)} async-done(((bf16[128,9,2,128]{3,2,1,0:T(2,128)(2,1)}), bf16[128,9,2,128]{3,2,1,0:T(2,128)(2,1)S(1)}, u32[]{:S(2)}, u32[]{:S(2)}) %all-to-all-start.3) | async-done | bytes 589856 | tf_op jit(solution)/shard_map/all_to_all | solution.py:457
  162.3 2.4 %shard_map.81 = f32[2304,128]{1,0:T(8,128)} custom-call(bf16[2304,128]{1,0:T(8,128)(2,1)S(1)} %bitcast.15, f32[18,128,128]{2,1,0:T(8,128)S(1)} %get-tuple-element.34.state_ref, f32[18,128,128]{2,1,0:T(8,128)S(1)} %get-tuple-element.35.gate_ref, bf16[128,384]{1,0:T(8,128)(2,1)} %get-tuple-element.36.outcat_hbm), custom_call_target="tpu_custom_call" | custom-call | tf_op jit(solution)/shard_map/pallas_call | solution.py:437
  (1 shorter events, 0.0 us)
Async XLA Ops:
  51.7 2.8 %collective-permute-start = (bf16[4608,128]{1,0:T(8,128)(2,1)S(1)}, bf16[4608,128]{1,0:T(8,128)(2,1)S(1)}, u32[]{:S(2)}, u32[]{:S(2)}) collective-permute-start(bf16[4608,128]{1,0:T(8,128)(2,1)S(1)} %bitcast.10), channel_id=1, source_target_pairs={{0,8},{8,0},{1,9},{9,1},{2,10},{10,2},{3,11},{11,3},{4,12},{12,4},... | collective-permute-start | bytes 3538952 | tf_op jit(solution)/shard_map/ppermute | solution.py:462
  57.6 6.7 %copy-start = (f32[2,128,512]{2,1,0:T(8,128)S(1)}, f32[2,128,512]{2,1,0:T(8,128)}, u32[]{:S(2)}) copy-start(f32[2,128,512]{2,1,0:T(8,128)} %refs_0_.1) | copy-start | bytes 1572868
  57.6 6.7 %copy-start.1 = (f32[2,128,128]{2,1,0:T(8,128)S(1)}, f32[2,128,128]{2,1,0:T(8,128)}, u32[]{:S(2)}) copy-start(f32[2,128,128]{2,1,0:T(8,128)} %gatew_ref.3) | copy-start | bytes 393220
  57.6 6.7 %copy-start.2 = (f32[2,128,128]{2,1,0:T(8,128)S(1)}, f32[2,128,128]{2,1,0:T(8,128)}, u32[]{:S(2)}) copy-start(f32[2,128,128]{2,1,0:T(8,128)} %outw_ref.3) | copy-start | bytes 393220
  57.7 27.8 %all-to-all-start.1 = ((bf16[128,9,2,128]{3,2,1,0:T(2,128)(2,1)}), bf16[128,9,2,128]{3,2,1,0:T(2,128)(2,1)S(1)}, u32[]{:S(2)}, u32[]{:S(2)}) async-start(bf16[128,9,2,128]{3,2,1,0:T(2,128)(2,1)} %bitcast.20), calls=%async_computation.1 | async-start | bytes 1179648 | tf_op jit(solution)/shard_map/all_to_all | solution.py:457
  128.0 2.8 %collective-permute-start.1 = (bf16[4608,128]{1,0:T(8,128)(2,1)S(1)}, bf16[4608,128]{1,0:T(8,128)(2,1)S(1)}, u32[]{:S(2)}, u32[]{:S(2)}) collective-permute-start(bf16[4608,128]{1,0:T(8,128)(2,1)S(1)} %bitcast.12), channel_id=1, source_target_pairs={{0,8},{8,0},{1,9},{9,1},{2,10},{10,2},{3,11},{11,3},{4,12},{12,4},... | collective-permute-start | bytes 3538952 | tf_op jit(solution)/shard_map/ppermute | solution.py:462
  134.5 27.8 %all-to-all-start.3 = ((bf16[128,9,2,128]{3,2,1,0:T(2,128)(2,1)}), bf16[128,9,2,128]{3,2,1,0:T(2,128)(2,1)S(1)}, u32[]{:S(2)}, u32[]{:S(2)}) async-start(bf16[128,9,2,128]{3,2,1,0:T(2,128)(2,1)} %bitcast.18), calls=%async_computation.3 | async-start | bytes 1179648 | tf_op jit(solution)/shard_map/all_to_all | solution.py:457

commit v10 on v9

--- a/solution.py
+++ b/solution.py
@@ -244,12 +244,26 @@
     widen(other_ref, wide_ref)
     left = left_ref[...]
 
+    lane = lanes((8, 128))
+    sub = lax.broadcasted_iota(jnp.int32, (8, 128), 0)
+
     def fill(n):
         for c in range(4):
-            for g in range(8):
-                message = PAD + ((4 * n + c) * 8 + g) * 2 * PACK
-                start = (c // 2) * 128 + (c % 2) * 48 + 24 - core * 24
-                place(wide_ref, message + PACK, right_refs[n], start, slice(128 * g, 128 * g + 128), True)
+            start = (c // 2) * 128 + (c % 2) * 48 + 24 - core * 24
+            for g in range(0, 8, 2):
+                bases = [PAD + ((4 * n + c) * 8 + g + h) * 2 * PACK + PACK for h in range(2)]
+
+                def moved(at, shift):
+                    return turned_pair(*(wide_ref[base + at : base + at + 8, :] for base in bases), shift)
+
+                pieces = moved(-2, 32), moved(4, 64), moved(10, 96)
+                for h, base in enumerate(bases):
+                    third = jnp.where(lane < 64, pieces[1][h], pieces[2][h])
+                    third = jnp.where(lane < 32, pieces[0][h], third)
+                    third = jnp.where(sub < 2, wide_ref[base + 16 : base + 24, :], third)
+                    column = slice(128 * (g + h), 128 * (g + h) + 128)
+                    for m, part in enumerate((wide_ref[base : base + 8, :], wide_ref[base + 8 : base + 16, :], third)):
+                        right_refs[n][aligned(start + 8 * m, 8, 8), column] = jnp.where(lane < COLS, part, 0.0)
 
     fill(0)
     for n in range(4):
@@ -318,7 +332,7 @@
 
 
 def finish(tri_ref, state_ref, gate_ref, outcat_hbm, scaled_ref, stat_ref, outcat_ref, fetch_sems, gate_hbm=None, after=()):
-    fetches = [pltpu.make_async_copy(outcat_hbm, outcat_ref, fetch_sems.at[3])]
+    fetches = [] if gate_hbm is None else [pltpu.make_async_copy(outcat_hbm, outcat_ref, fetch_sems.at[3])]
     for n in range(0 if gate_hbm is None else 3):
         at = pl.ds(6 * n, 6)
         fetches.append(pltpu.make_async_copy(gate_hbm.at[at], gate_ref.at[at], fetch_sems.at[n]))
@@ -345,7 +359,8 @@
     scale = lax.rsqrt(gather(1) - average * average + EPS)
     stat_ref[0, 0:18, :] = average
     stat_ref[1, 0:18, :] = scale
-    fetches[0].wait()
+    for fetch in fetches[:1]:
+        fetch.wait()
     w_cat = outcat_ref[...]
 
     def updated(i):
@@ -381,8 +396,8 @@
     project(lambda i: (next_ref[2 * i], next_ref[2 * i + 1]), projcat_ref[...], edge_ref, mix_ref, send_ref)
 
 
-def last_kernel(tri_ref, state_ref, gate_ref, outcat_hbm, out_hbm, next_ref, sems, *scratch):
-    updated, _ = finish(tri_ref, state_ref, gate_ref, outcat_hbm, *scratch)
+def last_kernel(tri_ref, state_ref, gate_ref, outcat_ref, out_hbm, next_ref, sems, scaled_ref, stat_ref):
+    updated, _ = finish(tri_ref, state_ref, gate_ref, None, scaled_ref, stat_ref, outcat_ref, None)
     copies = []
 
     def done(n):
@@ -497,10 +512,10 @@
     part = call(incoming_own, PART, (near(own),), HALF_SCRATCH)
     tri = call(incoming_kernel, TRI, (near(part), near(other)), HALF_SCRATCH + SEND_SCRATCH, out_specs=HB)
     tri = exchange(tri, PACK)
-    gate, outcat = gating(1, (STATE, OUTCAT), near(state), gate_weight, out_weight)
+    gate, outcat = gating(1, (STATE, pltpu.VMEM((CH, 3 * CH), BF16)), near(state), gate_weight, out_weight)
     state = call(
-        last_kernel, jax.ShapeDtypeStruct((PIX, CH), F32), (near(tri), near(state), near(gate), far(outcat)),
-        [pltpu.VMEM((PIX, CH), F32), pltpu.SemaphoreType.DMA((4,))] + FINISH_SCRATCH, [VM, VM, VM, HB], out_specs=HB,
+        last_kernel, jax.ShapeDtypeStruct((PIX, CH), F32), (near(tri), near(state), near(gate), near(outcat)),
+        [pltpu.VMEM((PIX, CH), F32), pltpu.SemaphoreType.DMA((4,))] + FINISH_SCRATCH[:2], out_specs=HB,
     )
     return state.reshape(ROWS, COLS, CH)
 

time: 165 us -> 164 us (level)
  no operation moved by 1% of the time
where the time goes in v10:
time: 164 us
  blocking collectives  87.4 us (53%)
  waiting for transfers between devices  39.6 us (24%)
  Pallas kernels  23.6 us (14%)
  starting transfers between devices  13.2 us (8%)
    all_to_all x2, blocking collectives, exchange(): lax.all_to_all(message.reshape(CH, rows // 2, 2, 128), CHIPS, split_axis=...  87.4 us
    all_to_all x2, waiting for transfers between devices, exchange(): lax.all_to_all(message.reshape(CH, rows // 2, 2, 128), CHIPS, split_axis=...  37.4 us
    pallas_call x9, Pallas kernels, call(): pl.pallas_call(kernel, out_shape=out_shape, in_specs=specs or [VM] * len(...  23.6 us
    all_to_all x2, starting transfers between devices, exchange(): lax.all_to_all(message.reshape(CH, rows // 2, 2, 128), CHIPS, split_axis=...  13.2 us
  transfers between devices with their start and end apart: 4, of which 4 were waited for; matrix products, arithmetic and copies ran while one was open for 0% of the time, Pallas kernels for 5%

profile of v10, /device:TPU:6, one launch (start us, length us, event | category | flops | bytes accessed | tf_op | source)
XLA Modules:
  0.0 164.1 jit_solution(3914601283676092879)
XLA Ops:
  0.0 3.1 %shard_map.73 = (bf16[4608,128]{1,0:T(8,128)(2,1)S(1)}, f32[18,128]{1,0:T(8,128)S(1)}, f32[18,128,128]{2,1,0:T(8,128)S(1)}) custom-call(s32[768]{0:T(1024)} %mask_hbm.1, s32[768]{0:T(1024)} %hot_hbm.1, s32[24,96]{1,0:T(8,128)} %inter_hbm.1, f32[2304,128]{1,0:T(8,128)} %bitcast.19, f32[2,128,512]{2,1,0:T(8,128)} %refs_0_.1), custom_call_target="tpu_custom_call" | custom-call | tf_op jit(solution)/shard_map/pallas_call | solution.py:452
  3.1 48.6 %all_to_all.20 = bf16[128,18,2,128]{3,2,1,0:T(2,128)(2,1)S(1)} all-to-all(bf16[128,18,2,128]{3,2,1,0:T(2,128)(2,1)S(1)} %bitcast.17), channel_id=1, replica_groups=mesh['z'=8,'yl'=2,'core'=2,'x'=4,'yh'=2] {'z','yl','x','yh'}, dimensions={0} | all-to-all | bytes 2359296 | tf_op jit(solution)/shard_map/all_to_all | solution.py:472
  51.7 0.0 collective-permute-start
  51.7 1.6 shard_map.74
  53.4 1.2 collective-permute-done.other_ref
  54.6 3.0 %shard_map.75 = (bf16[2304,128]{1,0:T(8,128)(2,1)}, f32[256,1024]{1,0:T(8,128)S(1)}, f32[256,1024]{1,0:T(8,128)S(1)}, f32[256,1024]{1,0:T(8,128)S(1)}, f32[256,1024]{1,0:T(8,128)S(1)}) custom-call(bf16[384,1024]{1,0:T(8,128)(2,1)S(1)} %get-tuple-element.23.left_ref, ...), custom_call_target="tpu_custom_call", output_to_operand_aliasing={{1}: (1, {}), {2}: (2, {}), {3}: (3, {}), {4}: (4, {})} | custom-call | tf_op jit(solution)/shard_map/pallas_call | solution.py:452
  57.6 0.0 copy-start
  57.6 0.0 copy-start.1
  57.6 0.0 copy-start.2
  57.6 6.6 %all-to-all-start.1 = ((bf16[128,9,2,128]{3,2,1,0:T(2,128)(2,1)}), bf16[128,9,2,128]{3,2,1,0:T(2,128)(2,1)S(1)}, u32[]{:S(2)}, u32[]{:S(2)}) async-start(bf16[128,9,2,128]{3,2,1,0:T(2,128)(2,1)} %bitcast.20), calls=%async_computation.1 | async-start | bytes 1179648 | tf_op jit(solution)/shard_map/all_to_all | solution.py:472
  64.2 0.0 copy-done
  64.3 0.0 copy-done.1
  64.3 3.0 %shard_map.76 = (f32[18,128,128]{2,1,0:T(8,128)}, bf16[128,384]{1,0:T(8,128)(2,1)}, bf16[512,384]{1,0:T(8,128)(2,1)}) custom-call(f32[18,128,128]{2,1,0:T(8,128)S(1)} %get-tuple-element.29.state_ref, f32[2,128,128]{2,1,0:T(8,128)S(1)} %copy-done.1, f32[2,128,128]{2,1,0:T(8,128)S(1)} %copy-done.2, f32[2,128,512]{2,1,0:T(8,128)S(1)} %copy-done), custom_call_target="tpu_custom_call" | custom-call | flops 226492416 | bytes 2359296 | tf_op jit(solution)/shard_map/pallas_call | solution.py:452
  67.3 18.2 %all-to-all-done.1 = bf16[128,9,2,128]{3,2,1,0:T(2,128)(2,1)S(1)} async-done(((bf16[128,9,2,128]{3,2,1,0:T(2,128)(2,1)}), bf16[128,9,2,128]{3,2,1,0:T(2,128)(2,1)S(1)}, u32[]{:S(2)}, u32[]{:S(2)}) %all-to-all-start.1) | async-done | bytes 589856 | tf_op jit(solution)/shard_map/all_to_all | solution.py:472
  85.4 3.7 %shard_map.77 = (f32[18,128,128]{2,1,0:T(8,128)S(1)}, bf16[4608,128]{1,0:T(8,128)(2,1)S(1)}) custom-call(f32[18,128]{1,0:T(8,128)S(1)} %get-tuple-element.21.edge_ref, bf16[2304,128]{1,0:T(8,128)(2,1)S(1)} %bitcast.14, f32[18,128,128]{2,1,0:T(8,128)S(1)} %get-tuple-element.29.state_ref, f32[18,128,128]{2,1,0:T(8,128)} %get-tuple-element.30.gate_hbm, ...), custom_call_target="tpu_custom_call" | custom-call | tf_op jit(solution)/shard_map/pallas_call | solution.py:452
  89.1 38.9 %all_to_all.21 = bf16[128,18,2,128]{3,2,1,0:T(2,128)(2,1)S(1)} all-to-all(bf16[128,18,2,128]{3,2,1,0:T(2,128)(2,1)S(1)} %bitcast.16), channel_id=1, replica_groups=mesh['z'=8,'yl'=2,'core'=2,'x'=4,'yh'=2] {'z','yl','x','yh'}, dimensions={0} | all-to-all | bytes 2359296 | tf_op jit(solution)/shard_map/all_to_all | solution.py:472
  128.0 0.0 collective-permute-start.1
  128.0 1.9 %shard_map.78.part_ref = f32[8,384,128]{2,1,0:T(8,128)S(1)} custom-call(bf16[4608,128]{1,0:T(8,128)(2,1)S(1)} %bitcast.13), custom_call_target="tpu_custom_call" | custom-call | tf_op jit(solution)/shard_map/pallas_call | solution.py:452
  129.9 0.9 collective-permute-done.1.other_ref
  130.8 3.6 %shard_map.79 = bf16[2304,128]{1,0:T(8,128)(2,1)} custom-call(f32[8,384,128]{2,1,0:T(8,128)S(1)} %shard_map.78.part_ref, bf16[4608,128]{1,0:T(8,128)(2,1)S(1)} %collective-permute-done.1.other_ref), custom_call_target="tpu_custom_call" | custom-call | tf_op jit(solution)/shard_map/pallas_call | solution.py:452
  134.5 6.5 %all-to-all-start.3 = ((bf16[128,9,2,128]{3,2,1,0:T(2,128)(2,1)}), bf16[128,9,2,128]{3,2,1,0:T(2,128)(2,1)S(1)}, u32[]{:S(2)}, u32[]{:S(2)}) async-start(bf16[128,9,2,128]{3,2,1,0:T(2,128)(2,1)} %bitcast.18), calls=%async_computation.3 | async-start | bytes 1179648 | tf_op jit(solution)/shard_map/all_to_all | solution.py:472
  141.0 1.9 %shard_map.80 = (f32[18,128,128]{2,1,0:T(8,128)S(1)}, bf16[128,384]{1,0:T(8,128)(2,1)S(1)}) custom-call(f32[18,128,128]{2,1,0:T(8,128)S(1)} %get-tuple-element.34.state_ref, f32[2,128,128]{2,1,0:T(8,128)S(1)} %copy-done.1, f32[2,128,128]{2,1,0:T(8,128)S(1)} %copy-done.2), custom_call_target="tpu_custom_call" | custom-call | flops 226492416 | bytes 2359296 | tf_op jit(solution)/shard_map/pallas_call | solution.py:452
  142.9 19.3 %all-to-all-done.3 = bf16[128,9,2,128]{3,2,1,0:T(2,128)(2,1)S(1)} async-done(((bf16[128,9,2,128]{3,2,1,0:T(2,128)(2,1)}), bf16[128,9,2,128]{3,2,1,0:T(2,128)(2,1)S(1)}, u32[]{:S(2)}, u32[]{:S(2)}) %all-to-all-start.3) | async-done | bytes 589856 | tf_op jit(solution)/shard_map/all_to_all | solution.py:472
  162.2 1.7 %shard_map.81 = f32[2304,128]{1,0:T(8,128)} custom-call(bf16[2304,128]{1,0:T(8,128)(2,1)S(1)} %bitcast.15, f32[18,128,128]{2,1,0:T(8,128)S(1)} %get-tuple-element.34.state_ref, f32[18,128,128]{2,1,0:T(8,128)S(1)} %get-tuple-element.35.gate_ref, bf16[128,384]{1,0:T(8,128)(2,1)S(1)} %get-tuple-element.36.outcat_ref), custom_call_target="tpu_custom_call" | custom-call | tf_op jit(solution)/shard_map/pallas_call | solution.py:452
  (1 shorter events, 0.0 us)
Async XLA Ops:
  51.7 2.8 %collective-permute-start = (bf16[4608,128]{1,0:T(8,128)(2,1)S(1)}, bf16[4608,128]{1,0:T(8,128)(2,1)S(1)}, u32[]{:S(2)}, u32[]{:S(2)}) collective-permute-start(bf16[4608,128]{1,0:T(8,128)(2,1)S(1)} %bitcast.10), channel_id=1, source_target_pairs={{0,8},{8,0},{1,9},{9,1},{2,10},{10,2},{3,11},{11,3},{4,12},{12,4},... | collective-permute-start | bytes 3538952 | tf_op jit(solution)/shard_map/ppermute | solution.py:477
  57.6 6.7 %copy-start = (f32[2,128,512]{2,1,0:T(8,128)S(1)}, f32[2,128,512]{2,1,0:T(8,128)}, u32[]{:S(2)}) copy-start(f32[2,128,512]{2,1,0:T(8,128)} %refs_0_.1) | copy-start | bytes 1572868
  57.6 6.7 %copy-start.1 = (f32[2,128,128]{2,1,0:T(8,128)S(1)}, f32[2,128,128]{2,1,0:T(8,128)}, u32[]{:S(2)}) copy-start(f32[2,128,128]{2,1,0:T(8,128)} %gatew_ref.3) | copy-start | bytes 393220
  57.6 6.7 %copy-start.2 = (f32[2,128,128]{2,1,0:T(8,128)S(1)}, f32[2,128,128]{2,1,0:T(8,128)}, u32[]{:S(2)}) copy-start(f32[2,128,128]{2,1,0:T(8,128)} %outw_ref.3) | copy-start | bytes 393220
  57.6 27.8 %all-to-all-start.1 = ((bf16[128,9,2,128]{3,2,1,0:T(2,128)(2,1)}), bf16[128,9,2,128]{3,2,1,0:T(2,128)(2,1)S(1)}, u32[]{:S(2)}, u32[]{:S(2)}) async-start(bf16[128,9,2,128]{3,2,1,0:T(2,128)(2,1)} %bitcast.20), calls=%async_computation.1 | async-start | bytes 1179648 | tf_op jit(solution)/shard_map/all_to_all | solution.py:472
  128.0 2.8 %collective-permute-start.1 = (bf16[4608,128]{1,0:T(8,128)(2,1)S(1)}, bf16[4608,128]{1,0:T(8,128)(2,1)S(1)}, u32[]{:S(2)}, u32[]{:S(2)}) collective-permute-start(bf16[4608,128]{1,0:T(8,128)(2,1)S(1)} %bitcast.12), channel_id=1, source_target_pairs={{0,8},{8,0},{1,9},{9,1},{2,10},{10,2},{3,11},{11,3},{4,12},{12,4},... | collective-permute-start | bytes 3538952 | tf_op jit(solution)/shard_map/ppermute | solution.py:477
  134.5 27.8 %all-to-all-start.3 = ((bf16[128,9,2,128]{3,2,1,0:T(2,128)(2,1)}), bf16[128,9,2,128]{3,2,1,0:T(2,128)(2,1)S(1)}, u32[]{:S(2)}, u32[]{:S(2)}) async-start(bf16[128,9,2,128]{3,2,1,0:T(2,128)(2,1)} %bitcast.18), calls=%async_computation.3 | async-start | bytes 1179648 | tf_op jit(solution)/shard_map/all_to_all | solution.py:472
